TPU v7x, 32 devices: a whole 2x2x4 slice. The times are simulated.
32 devices in a mesh: gx: 8 (over y, x, core), gy: 4 (over z).
Axes of the slice: x: 2, y: 2, z: 4, core: 2. Of those that a mesh axis runs over, the one named last changes fastest.
Arguments:
- basis: float32 [32, 64, 32, 256], P(None, 'gx', 'gy'), may hold values from -6 to 6
- rhs: float32 [64, 32, 256], P('gx', 'gy'), may hold values from -12 to 12
- extra_diag: float32 [64, 32, 256], P('gx', 'gy'), may hold values from 0.02 to 0.5
- coeff: float32 [3, 64, 32, 256], P(None, 'gx', 'gy'), may hold values from 0.3 to 3
Outputs:
- guess: float32 [64, 32, 256], P('gx', 'gy')
- stepped: float32 [64, 32, 256], P('gx', 'gy')
All inputs are finite; a program needn't handle non-finite values.
Results may differ from a plain program's by a relative error of at most 0.0003.
Values sent between devices are 32-bit elements; how exact they have to be, the bound alone decides.
No kernel may reach another device: no remote copies, remote signals or barrier semaphores. Data moves between devices by JAX's collectives and lax.ppermute only.
A program may use at most 64 MiB of HBM per device.

v0:
```python
import jax
import jax.numpy as jnp
from jax import lax
from jax.sharding import PartitionSpec as P

precise = lax.Precision.HIGHEST


def shifted(block, axis, distance):
    devices = range(lax.axis_size(axis))
    route = [(i - distance, i) for i in devices if i - distance in devices]
    return lax.ppermute(block, axis, route)


def padded_2(cells, sides, width):
    for axis, dim in sides:
        count = lax.axis_size(axis)
        ends = count - 1
        head = lax.slice_in_dim(cells, 0, width, axis=dim)
        tail = lax.slice_in_dim(cells, cells.shape[dim] - width, cells.shape[dim], axis=dim)
        cells = jnp.concatenate(
            [
                lax.ppermute(tail, axis, [(i, (i + 1) % count) for i in range(ends)]),
                cells,
                lax.ppermute(head, axis, [((i + 1) % count, i) for i in range(ends)]),
            ],
            axis=dim,
        )
    return cells


def flux_apply(padded, coeff_pad, extra):
    center = padded[:, 1:-1, 1:-1]
    coeff_mid = coeff_pad[:, 1:-1, 1:-1]
    flux_x = coeff_mid[0] * (center - padded[:, 2:, 1:-1])
    flux_y = coeff_mid[1] * (center - padded[:, 1:-1, 2:])
    below_x = coeff_pad[0, :-2, 1:-1] * (padded[:, :-2, 1:-1] - center)
    below_y = coeff_pad[1, 1:-1, :-2] * (padded[:, 1:-1, :-2] - center)
    next_z = jnp.concatenate([center[..., 1:], jnp.zeros_like(center[..., :1])], axis=-1)
    flux_z = coeff_mid[2] * (center - next_z)
    below_z = jnp.concatenate([jnp.zeros_like(flux_z[..., :1]), flux_z[..., :-1]], axis=-1)
    return extra * center + flux_x + flux_y + flux_z - below_x - below_y - below_z


def small_solve(matrix, vector):
    lower = jnp.linalg.cholesky(matrix)
    middle = lax.linalg.triangular_solve(lower, vector[:, None], left_side=True, lower=True)
    result = lax.linalg.triangular_solve(
        lower, middle, left_side=True, lower=True, transpose_a=True
    )
    return result[:, 0]


def on_device(basis, rhs, extra_diag, coeff):
    lower_x = shifted(coeff[0][-1:], "gx", 1)
    lower_y = shifted(coeff[1][:, -1:], "gy", 1)
    coeff_pad = jnp.pad(coeff, ((0, 0), (1, 1), (1, 1), (0, 0)))
    coeff_pad = coeff_pad.at[0, 0, 1:-1].set(lower_x[0])
    coeff_pad = coeff_pad.at[1, 1:-1, 0].set(lower_y[:, 0])
    count = basis.shape[0]
    flat_basis = basis.reshape(count, -1)
    padded_basis = padded_2(basis, (("gx", 1), ("gy", 2)), 1)
    applied = flux_apply(padded_basis, coeff_pad, extra_diag)
    local_gram = jnp.dot(flat_basis, applied.reshape(count, -1).T, precision=precise)
    local_proj = jnp.dot(flat_basis, rhs.reshape(-1), precision=precise)
    gram, projected = lax.psum((local_gram, local_proj), ("gx", "gy"))
    gram = 0.5 * (gram + gram.T)
    weights = small_solve(gram, projected)
    guess = jnp.tensordot(weights, basis, axes=1, precision=precise)
    residual = rhs - jnp.tensordot(weights, applied, axes=1, precision=precise)
    coeff_mid = coeff_pad[:, 1:-1, 1:-1]
    below_kz = jnp.concatenate([jnp.zeros_like(coeff[2][..., :1]), coeff[2][..., :-1]], axis=-1)
    diagonal = (
        extra_diag
        + coeff_mid[0]
        + coeff_mid[1]
        + coeff_mid[2]
        + coeff_pad[0, :-2, 1:-1]
        + coeff_pad[1, 1:-1, :-2]
        + below_kz
    )
    direction = residual / diagonal
    direction_pad = padded_2(direction, (("gx", 0), ("gy", 1)), 1)
    applied_dir = flux_apply(direction_pad[None], coeff_pad, extra_diag)[0]
    local_corr = jnp.dot(flat_basis, applied_dir.reshape(-1), precision=precise)
    correction, numerator, curvature = lax.psum(
        (local_corr, jnp.sum(residual * direction), jnp.sum(direction * applied_dir)), ("gx", "gy")
    )
    shift_coef = small_solve(gram, correction)
    update = direction - jnp.tensordot(shift_coef, basis, axes=1, precision=precise)
    denominator = curvature - jnp.dot(correction, shift_coef, precision=precise)
    step_size = numerator / denominator
    return (guess, guess + step_size * update)


def solution(mesh):
    placed = (
        P(None, "gx", "gy", None),
        P("gx", "gy", None),
        P("gx", "gy", None),
        P(None, "gx", "gy", None),
    )
    return jax.shard_map(
        on_device,
        mesh=mesh,
        in_specs=placed,
        out_specs=(P("gx", "gy", None), P("gx", "gy", None)),
        check_vma=False,
    )
```

profile of v0, /device:TPU:0, one launch (start us, length us, event | category | flops | bytes accessed | tf_op | source)
XLA Modules:
  0.0 160.6 jit_solution(4980887315087795019)
XLA Ops:
  1.3 2.5 %collective-permute-start = (f32[1,8,256]{2,1,0:T(8,128)S(1)}, f32[1,8,256]{2,1,0:T(8,128)S(1)}, u32[]{:S(2)}, u32[]{:S(2)}) collective-permute-start(f32[1,8,256]{2,1,0:T(8,128)S(1)} %slice_bitcast_fusion.7), channel_id=1, source_target_pairs={{0,4},{4,8},{8,12},{12,16},{16,20},{20,24},{24,28},{1,5},{5,9},{9,... | collective-permute-start | bytes 24584 | tf_op jit(solution)/shard_map/ppermute | solution.py:12
  3.9 2.8 %copy.11 = f32[32,8,8,256]{3,0,2,1:T(8,128)S(1)} copy(f32[32,8,8,256]{3,2,1,0:T(8,128)} %param.13) | data formatting | bytes 4194304 | tf_op args[0]
  7.6 4.5 %collective-permute-start.3 = (f32[32,1,8,256]{3,0,2,1:T(8,128)}, f32[32,1,8,256]{3,0,2,1:T(8,128)S(1)}, u32[]{:S(2)}, u32[]{:S(2)}) collective-permute-start(f32[32,1,8,256]{3,0,2,1:T(8,128)} %get-tuple-element.44), channel_id=1, source_target_pairs={{0,4},{4,8},{8,12},{12,16},{16,20},{20,24},{24,28},{1,5},{5,9},{9,... | collective-permute-start | bytes 786440 | tf_op jit(solution)/shard_map/ppermute | solution.py:23
  12.1 3.5 %collective-permute-start.1 = (f32[8,1,256]{2,1,0:T(1,128)S(1)}, f32[8,1,256]{2,1,0:T(1,128)S(1)}, u32[]{:S(2)}, u32[]{:S(2)}) collective-permute-start(f32[8,1,256]{2,1,0:T(1,128)S(1)} %slice.229), channel_id=1, source_target_pairs={{0,1},{1,2},{2,3},{4,5},{5,6},{6,7},{8,9},{9,10},{10,11},{12,13},{... | collective-permute-start | bytes 24584 | tf_op jit(solution)/shard_map/ppermute | solution.py:12
  15.6 1.4 collective-permute-start.2
  17.1 1.9 %slice.236 = f32[32,8,8,255]{3,0,2,1:T(8,128)} slice(f32[32,8,8,256]{3,0,2,1:T(8,128)S(1)} %copy.11), slice={[0:32], [0:8], [0:8], [1:256]} | slice | bytes 4177920 | tf_op jit(solution)/shard_map/slice | solution.py:39
  19.4 3.0 %subtract_multiply_fusion = (f32[32,8,8,256]{3,0,2,1:T(8,128)S(1)}, f32[32,10,8,256]{3,0,2,1:T(8,128)S(1)}) fusion(f32[32,8,8,255]{3,0,2,1:T(8,128)} %slice.236, f32[8,8,256]{2,1,0:T(8,128)S(1)} %get-tuple-element.48, f32[32,8,8,256]{3,2,1,0:T(8,128)S(1)} %copy-done, f32[32,10,8,256]{3,0,2,1:T(8,128)S(1)} %constant_dynamic-update-slice_fusion.2), kind=kLoop, calls=%fused_computation.18 | loop fusion | flops 1048576 | bytes 8445952 | tf_op jit(solution)/shard_map/mul | solution.py:40
  24.0 4.6 %collective-permute-start.5 = (f32[32,10,1,256]{3,0,2,1:T(8,128)S(1)}, f32[32,10,1,256]{3,0,2,1:T(8,128)S(1)}, u32[]{:S(2)}, u32[]{:S(2)}) collective-permute-start(f32[32,10,1,256]{3,0,2,1:T(8,128)S(1)} %get-tuple-element.40), channel_id=1, source_target_pairs={{0,1},{1,2},{2,3},{4,5},{5,6},{6,7},{8,9},{9,10},{10,11},{12,13},{... | collective-permute-start | bytes 983048 | tf_op jit(solution)/shard_map/ppermute | solution.py:23
  28.5 2.8 %convolution_bitcast_fusion.5 = f32[32,1]{0,1:T(1,128)S(1)} fusion(f32[8,8,256,1]{2,1,0,3:T(8,128)S(1)} %bitcast.153, f32[32,8,8,256]{3,2,1,0:T(8,128)S(1)} %copy-done), kind=kOutput, calls=%fused_computation.24 | convolution fusion | flops 6291456 | bytes 2162816 | tf_op jit(solution)/shard_map/dot_general | solution.py:65
  31.3 3.7 %collective-permute-done.4 = f32[32,10,1,256]{3,0,2,1:T(8,128)S(1)} collective-permute-done((f32[32,10,1,256]{3,0,2,1:T(8,128)S(1)}, f32[32,10,1,256]{3,0,2,1:T(8,128)S(1)}, u32[]{:S(2)}, u32[]{:S(2)}) %collective-permute-start.4) | collective-permute-done | bytes 327712 | tf_op jit(solution)/shard_map/ppermute | solution.py:25
  35.0 1.5 collective-permute-done.5
  36.5 2.9 %fusion.3 = f32[32,8,8,256]{3,0,2,1:T(8,128)S(1)} fusion(f32[32,8,8,256]{3,0,2,1:T(8,128)S(1)} %copy-done.2, f32[32,10,8,256]{3,0,2,1:T(8,128)S(1)} %constant_dynamic-update-slice_fusion, f32[32,10,1,256]{3,0,2,1:T(8,128)S(1)} %collective-permute-done.5, f32[32,1,8,256]{3,0,2,1:T(8,128)S(1)} %collective-permute-done.3, ...), kind=kLoop, calls=%fused_computation.4 | loop fusion | flops 9961472 | bytes 12509184 | tf_op jit(solution)/shard_map/sub | solution.py:42
  40.7 2.9 %convolution_bitcast_fusion = f32[32,32]{1,0:T(8,128)S(1)} fusion(f32[32,8,8,256]{3,0,2,1:T(8,128)S(1)} %fusion.3, f32[32,8,8,256]{3,2,1,0:T(8,128)S(1)} %copy-done), kind=kOutput, calls=%fused_computation.19 | convolution fusion | flops 201326592 | bytes 4198400 | tf_op jit(solution)/shard_map/dot_general | solution.py:64
  43.6 40.9 %all-reduce.7 = (f32[32,1]{0,1:T(1,128)S(1)}, f32[32,32]{1,0:T(8,128)S(1)}) all-reduce(f32[32,1]{0,1:T(1,128)S(1)} %convolution_bitcast_fusion.5, f32[32,32]{1,0:T(8,128)S(1)} %convolution_bitcast_fusion), channel_id=1, replica_groups=mesh['gx'=8,'gy'=4] {'gx','gy'}, use_global_device_ids=true, to_apply=%region_3.0 | all-reduce | flops 1056 | bytes 8448 | tf_op jit(solution)/shard_map/psum | solution.py:66
  84.7 2.9 %cholesky.18 = f32[32,32]{1,0:T(8,128)S(1)} custom-call(f32[32,32]{1,0:T(8,128)S(1)} %fusion.34), custom_call_target="Cholesky" | custom-call | tf_op jit(solution)/shard_map/jit(cholesky)/cholesky | solution.py:46
  88.9 2.4 %custom-call.11 = f32[1,32,32]{1,2,0:T(8,128)S(1)} custom-call(f32[1,32,32]{2,1,0:T(8,128)S(1)} %fusion.28), custom_call_target="InvertDiagBlocksLowerTriangular" | custom-call | tf_op jit(solution)/shard_map/triangular_solve/custom-call.2 | solution.py:48
  91.7 2.7 %fusion.49 = f32[1,8,8,256]{3,0,2,1:T(1,128)S(1)} fusion(f32[32,1,1,1]{0,1,3,2:T(1,128)S(1)} %convolution_bitcast_fusion.2, f32[32,8,8,256]{3,0,2,1:T(8,128)} %copy-done.3), kind=kOutput, calls=%fused_computation.94 | convolution fusion | flops 6291456 | bytes 2162816 | tf_op jit(solution)/shard_map/dot_general | solution.py:70
  98.3 3.0 %collective-permute-done.7 = f32[1,8,256]{2,1,0:T(8,128)S(1)} collective-permute-done((f32[1,8,256]{2,1,0:T(8,128)S(1)}, f32[1,8,256]{2,1,0:T(8,128)S(1)}, u32[]{:S(2)}, u32[]{:S(2)}) %collective-permute-start.7) | collective-permute-done | bytes 8224 | tf_op jit(solution)/shard_map/ppermute | solution.py:25
  101.4 3.4 %collective-permute-start.8 = (f32[10,1,256]{2,1,0:T(1,128)S(1)}, f32[10,1,256]{2,1,0:T(1,128)S(1)}, u32[]{:S(2)}, u32[]{:S(2)}) collective-permute-start(f32[10,1,256]{2,1,0:T(1,128)S(1)} %get-tuple-element.52), channel_id=1, source_target_pairs={{0,1},{1,2},{2,3},{4,5},{5,6},{6,7},{8,9},{9,10},{10,11},{12,13},{... | collective-permute-start | bytes 30728 | tf_op jit(solution)/shard_map/ppermute | solution.py:23
  106.1 2.2 %fusion.42 = f32[1,8,8,256]{3,0,2,1:T(1,128)S(1)} fusion(f32[32,1,1,1]{0,1,3,2:T(1,128)S(1)} %convolution_bitcast_fusion.2, f32[32,8,8,256]{3,2,1,0:T(8,128)S(1)} %copy-done), kind=kOutput, calls=%fused_computation.88 | convolution fusion | flops 6291456 | bytes 2162816 | tf_op jit(solution)/shard_map/dot_general | solution.py:69
  108.4 2.0 %collective-permute-done.9 = f32[10,1,256]{2,1,0:T(1,128)S(1)} collective-permute-done((f32[10,1,256]{2,1,0:T(1,128)S(1)}, f32[10,1,256]{2,1,0:T(1,128)S(1)}, u32[]{:S(2)}, u32[]{:S(2)}) %collective-permute-start.9) | collective-permute-done | bytes 10272 | tf_op jit(solution)/shard_map/ppermute | solution.py:25
  111.3 1.7 %convolution_bitcast_fusion.4 = f32[32]{0:T(128)S(1)} fusion(f32[16384,1]{0,1:T(1,128)S(1)} %bitcast.156, f32[32,16384]{1,0:T(8,128)S(1)} %bitcast.152), kind=kOutput, calls=%fused_computation.23 | convolution fusion | flops 6291456 | bytes 2162816 | tf_op jit(solution)/shard_map/dot_general | solution.py:85
  113.0 41.7 %all-reduce.6 = (f32[32]{0:T(128)S(1)}, f32[]{:T(128)}, f32[]{:T(128)}) all-reduce(f32[32]{0:T(128)S(1)} %convolution_bitcast_fusion.4, f32[]{:T(128)} %get-tuple-element.30, f32[]{:T(128)} %get-tuple-element.29), channel_id=1, replica_groups=mesh['gx'=8,'gy'=4] {'gx','gy'}, use_global_device_ids=true, to_apply=%region_8.12 | all-reduce | flops 34 | bytes 272 | tf_op jit(solution)/shard_map/psum | solution.py:86
  155.7 2.2 %fusion.36 = f32[1,8,8,256]{3,0,2,1:T(1,128)S(1)} fusion(f32[1,32]{1,0:T(1,128)S(1)} %get-tuple-element.57, f32[32,8,8,256]{3,2,1,0:T(8,128)S(1)} %copy-done), kind=kOutput, calls=%fused_computation.81 | convolution fusion | flops 6291456 | bytes 2162816 | tf_op jit(solution)/shard_map/dot_general | solution.py:90
  (56 shorter events, 14.3 us)
Async XLA Ops:
  1.3 10.8 %copy-start.6 = (f32[3,8,8,256]{3,2,1,0:T(8,128)S(1)}, f32[3,8,8,256]{3,2,1,0:T(8,128)}, u32[]{:S(2)}) copy-start(f32[3,8,8,256]{3,2,1,0:T(8,128)} %param.16) | copy-start | bytes 589828
  1.3 17.7 %collective-permute-start = (f32[1,8,256]{2,1,0:T(8,128)S(1)}, f32[1,8,256]{2,1,0:T(8,128)S(1)}, u32[]{:S(2)}, u32[]{:S(2)}) collective-permute-start(f32[1,8,256]{2,1,0:T(8,128)S(1)} %slice_bitcast_fusion.7), channel_id=1, source_target_pairs={{0,4},{4,8},{8,12},{12,16},{16,20},{20,24},{24,28},{1,5},{5,9},{9,... | collective-permute-start | bytes 24584 | tf_op jit(solution)/shard_map/ppermute | solution.py:12
  6.7 12.3 %copy-start.1 = (f32[32,8,8,256]{3,0,2,1:T(8,128)}, f32[32,8,8,256]{3,0,2,1:T(8,128)S(1)}, u32[]{:S(2)}) copy-start(f32[32,8,8,256]{3,0,2,1:T(8,128)S(1)} %copy.11) | copy-start | bytes 6291460
  7.6 11.7 %collective-permute-start.3 = (f32[32,1,8,256]{3,0,2,1:T(8,128)}, f32[32,1,8,256]{3,0,2,1:T(8,128)S(1)}, u32[]{:S(2)}, u32[]{:S(2)}) collective-permute-start(f32[32,1,8,256]{3,0,2,1:T(8,128)} %get-tuple-element.44), channel_id=1, source_target_pairs={{0,4},{4,8},{8,12},{12,16},{16,20},{20,24},{24,28},{1,5},{5,9},{9,... | collective-permute-start | bytes 786440 | tf_op jit(solution)/shard_map/ppermute | solution.py:23
  12.1 7.1 %collective-permute-start.1 = (f32[8,1,256]{2,1,0:T(1,128)S(1)}, f32[8,1,256]{2,1,0:T(1,128)S(1)}, u32[]{:S(2)}, u32[]{:S(2)}) collective-permute-start(f32[8,1,256]{2,1,0:T(1,128)S(1)} %slice.229), channel_id=1, source_target_pairs={{0,1},{1,2},{2,3},{4,5},{5,6},{6,7},{8,9},{9,10},{10,11},{12,13},{... | collective-permute-start | bytes 24584 | tf_op jit(solution)/shard_map/ppermute | solution.py:12
  15.6 3.7 %copy-start = (f32[32,8,8,256]{3,2,1,0:T(8,128)S(1)}, f32[32,8,8,256]{3,2,1,0:T(8,128)}, u32[]{:S(2)}) copy-start(f32[32,8,8,256]{3,2,1,0:T(8,128)} %param.13) | copy-start | bytes 6291460
  15.6 6.8 %collective-permute-start.2 = (f32[32,1,8,256]{3,0,2,1:T(8,128)}, f32[32,1,8,256]{3,0,2,1:T(8,128)S(1)}, u32[]{:S(2)}, u32[]{:S(2)}) collective-permute-start(f32[32,1,8,256]{3,0,2,1:T(8,128)} %get-tuple-element.43), channel_id=1, source_target_pairs={{4,0},{8,4},{12,8},{16,12},{20,16},{24,20},{28,24},{5,1},{9,5},{13... | collective-permute-start | bytes 786440 | tf_op jit(solution)/shard_map/ppermute | solution.py:25
  19.4 9.2 %copy-start.5 = (f32[8,8,256]{2,1,0:T(8,128)S(1)}, f32[8,8,256]{2,1,0:T(8,128)}, u32[]{:S(2)}) copy-start(f32[8,8,256]{2,1,0:T(8,128)} %param.14) | copy-start | bytes 196612
  22.4 14.1 %copy-start.2 = (f32[32,8,8,256]{3,0,2,1:T(8,128)S(1)}, f32[32,8,8,256]{3,0,2,1:T(8,128)}, u32[]{:S(2)}) copy-start(f32[32,8,8,256]{3,0,2,1:T(8,128)} %copy-done.1) | copy-start | bytes 6291460
  22.4 14.1 %copy-start.4 = (f32[8,8,256]{2,1,0:T(8,128)S(1)}, f32[8,8,256]{2,1,0:T(8,128)}, u32[]{:S(2)}) copy-start(f32[8,8,256]{2,1,0:T(8,128)} %param.15) | copy-start | bytes 196612
  22.5 12.5 %collective-permute-start.4 = (f32[32,10,1,256]{3,0,2,1:T(8,128)S(1)}, f32[32,10,1,256]{3,0,2,1:T(8,128)S(1)}, u32[]{:S(2)}, u32[]{:S(2)}) collective-permute-start(f32[32,10,1,256]{3,0,2,1:T(8,128)S(1)} %get-tuple-element.39), channel_id=1, source_target_pairs={{1,0},{2,1},{3,2},{5,4},{6,5},{7,6},{9,8},{10,9},{11,10},{13,12},{... | collective-permute-start | bytes 983048 | tf_op jit(solution)/shard_map/ppermute | solution.py:25
  24.0 12.5 %collective-permute-start.5 = (f32[32,10,1,256]{3,0,2,1:T(8,128)S(1)}, f32[32,10,1,256]{3,0,2,1:T(8,128)S(1)}, u32[]{:S(2)}, u32[]{:S(2)}) collective-permute-start(f32[32,10,1,256]{3,0,2,1:T(8,128)S(1)} %get-tuple-element.40), channel_id=1, source_target_pairs={{0,1},{1,2},{2,3},{4,5},{5,6},{6,7},{8,9},{9,10},{10,11},{12,13},{... | collective-permute-start | bytes 983048 | tf_op jit(solution)/shard_map/ppermute | solution.py:23
  39.4 1.3 copy-start.3
  94.5 3.8 %collective-permute-start.6 = (f32[1,8,256]{2,1,0:T(8,128)S(1)}, f32[1,8,256]{2,1,0:T(8,128)S(1)}, u32[]{:S(2)}, u32[]{:S(2)}) collective-permute-start(f32[1,8,256]{2,1,0:T(8,128)S(1)} %get-tuple-element.54), channel_id=1, source_target_pairs={{0,4},{4,8},{8,12},{12,16},{16,20},{20,24},{24,28},{1,5},{5,9},{9,... | collective-permute-start | bytes 24584 | tf_op jit(solution)/shard_map/ppermute | solution.py:23
  95.8 5.6 %collective-permute-start.7 = (f32[1,8,256]{2,1,0:T(8,128)S(1)}, f32[1,8,256]{2,1,0:T(8,128)S(1)}, u32[]{:S(2)}, u32[]{:S(2)}) collective-permute-start(f32[1,8,256]{2,1,0:T(8,128)S(1)} %get-tuple-element.55), channel_id=1, source_target_pairs={{4,0},{8,4},{12,8},{16,12},{20,16},{24,20},{28,24},{5,1},{9,5},{13... | collective-permute-start | bytes 24584 | tf_op jit(solution)/shard_map/ppermute | solution.py:25
  101.4 7.0 %collective-permute-start.8 = (f32[10,1,256]{2,1,0:T(1,128)S(1)}, f32[10,1,256]{2,1,0:T(1,128)S(1)}, u32[]{:S(2)}, u32[]{:S(2)}) collective-permute-start(f32[10,1,256]{2,1,0:T(1,128)S(1)} %get-tuple-element.52), channel_id=1, source_target_pairs={{0,1},{1,2},{2,3},{4,5},{5,6},{6,7},{8,9},{9,10},{10,11},{12,13},{... | collective-permute-start | bytes 30728 | tf_op jit(solution)/shard_map/ppermute | solution.py:23
  104.8 5.6 %collective-permute-start.9 = (f32[10,1,256]{2,1,0:T(1,128)S(1)}, f32[10,1,256]{2,1,0:T(1,128)S(1)}, u32[]{:S(2)}, u32[]{:S(2)}) collective-permute-start(f32[10,1,256]{2,1,0:T(1,128)S(1)} %get-tuple-element.53), channel_id=1, source_target_pairs={{1,0},{2,1},{3,2},{5,4},{6,5},{7,6},{9,8},{10,9},{11,10},{13,12},{... | collective-permute-start | bytes 30728 | tf_op jit(solution)/shard_map/ppermute | solution.py:25
where the time goes:
time: 161 us
  blocking collectives  82.6 us (51%)
  starting transfers between devices  25.2 us (16%)
  matrix products  15.8 us (10%)
  other arithmetic  14.2 us (9%)
  waiting for transfers between devices  10.2 us (6%)
  local copies, waits for them, and re-layouts  9.6 us (6%)
  between operations  2.99 us (2%)
    psum x1, blocking collectives, on_device(): lax.psum((local_corr, jnp.sum(residual * direction), jnp.sum(direction *...  41.7 us
    psum x1, blocking collectives, on_device(): gram, projected = lax.psum((local_gram, local_proj), ('gx', 'gy'))  40.9 us
    ppermute x4, starting transfers between devices, padded_2(): lax.ppermute(tail, axis, [(i, (i + 1) % count) for i in range(ends)])  13.8 us
    ppermute x4, waiting for transfers between devices, padded_2(): lax.ppermute(head, axis, [((i + 1) % count, i) for i in range(ends)])  8.74 us
    ppermute x2, starting transfers between devices, shifted(): return lax.ppermute(block, axis, route)  6 us
    unnamed x18, local copies, waits for them, and re-layouts  5.48 us
    ppermute x4, starting transfers between devices, padded_2(): lax.ppermute(head, axis, [((i + 1) % count, i) for i in range(ends)])  5.43 us
    another operation x3, other arithmetic, small_solve(): lower = jnp.linalg.cholesky(matrix)  3.6 us
  transfers between devices with their start and end apart: 10, of which 4 were waited for; matrix products, arithmetic and copies ran while one was open for 9% of the time, Pallas kernels for 0%

commit v1 on v0

--- a/solution.py
+++ b/solution.py
@@ -27,6 +27,38 @@
             axis=dim,
         )
     return cells
+
+
+def sum_stages():
+    wide, deep = lax.axis_size("gx"), lax.axis_size("gy")
+    along_x = [(1 << k, 0) for k in range(wide.bit_length() - 1)]
+    along_y = [(0, 1 << k) for k in range(deep.bit_length() - 1)]
+    steps = along_y[:0:-1] + along_x + along_y[:1]
+    single = len(steps) % 2
+    stages = [[step] for step in steps[:single]]
+    for at in range(single, len(steps), 2):
+        (a, b), (c, d) = steps[at], steps[at + 1]
+        stages.append([(a, b), (c, d), (a ^ c, b ^ d)])
+    return stages
+
+
+def sum_all(part):
+    wide, deep = lax.axis_size("gx"), lax.axis_size("gy")
+    if wide & (wide - 1) or deep & (deep - 1):
+        return lax.psum(part, ("gx", "gy"))
+    devices = [(i, j) for i in range(wide) for j in range(deep)]
+    for stage in sum_stages():
+        others = [
+            lax.ppermute(
+                part,
+                ("gx", "gy"),
+                [(i * deep + j, (i ^ a) * deep + (j ^ b)) for i, j in devices],
+            )
+            for a, b in stage
+        ]
+        for other in others:
+            part = part + other
+    return part
 
 
 def flux_apply(padded, coeff_pad, extra):
@@ -63,7 +95,8 @@
     applied = flux_apply(padded_basis, coeff_pad, extra_diag)
     local_gram = jnp.dot(flat_basis, applied.reshape(count, -1).T, precision=precise)
     local_proj = jnp.dot(flat_basis, rhs.reshape(-1), precision=precise)
-    gram, projected = lax.psum((local_gram, local_proj), ("gx", "gy"))
+    total = sum_all(jnp.concatenate([local_gram, local_proj[:, None]], axis=1))
+    gram, projected = total[:, :count], total[:, count]
     gram = 0.5 * (gram + gram.T)
     weights = small_solve(gram, projected)
     guess = jnp.tensordot(weights, basis, axes=1, precision=precise)
@@ -83,9 +116,9 @@
     direction_pad = padded_2(direction, (("gx", 0), ("gy", 1)), 1)
     applied_dir = flux_apply(direction_pad[None], coeff_pad, extra_diag)[0]
     local_corr = jnp.dot(flat_basis, applied_dir.reshape(-1), precision=precise)
-    correction, numerator, curvature = lax.psum(
-        (local_corr, jnp.sum(residual * direction), jnp.sum(direction * applied_dir)), ("gx", "gy")
-    )
+    local_sums = jnp.stack([jnp.sum(residual * direction), jnp.sum(direction * applied_dir)])
+    total = sum_all(jnp.concatenate([local_corr, local_sums])[None])[0]
+    correction, numerator, curvature = total[:count], total[count], total[count + 1]
     shift_coef = small_solve(gram, correction)
     update = direction - jnp.tensordot(shift_coef, basis, axes=1, precision=precise)
     denominator = curvature - jnp.dot(correction, shift_coef, precision=precise)

time: 161 us -> 115 us (0.71)
  blocking collectives: 82.6 us -> 0 us
  waiting for transfers between devices: 10.2 us -> 27.6 us
  starting transfers between devices: 25.2 us -> 42.3 us
  other arithmetic: 14.2 us -> 17.1 us
    psum x2 -> x0, blocking collectives: 82.6 us -> none  [the longest x1 41.7 us: on_device(): lax.psum((local_corr, jnp.sum(residual * direction), jnp.sum(direction *...]
    ppermute x0 -> x14, starting transfers between devices: none -> 18.1 us  [sum_all(): lax.ppermute(part, ('gx', 'gy'), [(i * deep + j, (i ^ a) * deep + (j ^ b)...]
    ppermute x0 -> x14, waiting for transfers between devices: none -> 15.3 us  [sum_all(): lax.ppermute(part, ('gx', 'gy'), [(i * deep + j, (i ^ a) * deep + (j ^ b)...]
    ppermute x4, waiting for transfers between devices: 8.74 us -> 10.8 us  [padded_2(): lax.ppermute(head, axis, [((i + 1) % count, i) for i in range(ends)])]
  transfers between devices with their start and end apart: 10 -> 24, of which waited for: 4 -> 16; matrix products, arithmetic and copies ran while one was open for 9% -> 13% of each run, Pallas kernels for 0% -> 0%
where the time goes in v1:
time: 115 us
  starting transfers between devices  42.3 us (37%)
  waiting for transfers between devices  27.6 us (24%)
  other arithmetic  17.1 us (15%)
  matrix products  15.7 us (14%)
  local copies, waits for them, and re-layouts  9.05 us (8%)
  between operations  2.98 us (3%)
    ppermute x14, starting transfers between devices, sum_all(): lax.ppermute(part, ('gx', 'gy'), [(i * deep + j, (i ^ a) * deep + (j ^ b)...  18.1 us
    ppermute x14, waiting for transfers between devices, sum_all(): lax.ppermute(part, ('gx', 'gy'), [(i * deep + j, (i ^ a) * deep + (j ^ b)...  15.3 us
    ppermute x4, starting transfers between devices, padded_2(): lax.ppermute(tail, axis, [(i, (i + 1) % count) for i in range(ends)])  12.6 us
    ppermute x4, waiting for transfers between devices, padded_2(): lax.ppermute(head, axis, [((i + 1) % count, i) for i in range(ends)])  10.8 us
    ppermute x2, starting transfers between devices, shifted(): return lax.ppermute(block, axis, route)  6 us
    ppermute x4, starting transfers between devices, padded_2(): lax.ppermute(head, axis, [((i + 1) % count, i) for i in range(ends)])  5.65 us
    unnamed x18, local copies, waits for them, and re-layouts  4.15 us
    another operation x3, other arithmetic, small_solve(): lower = jnp.linalg.cholesky(matrix)  3.6 us
  transfers between devices with their start and end apart: 24, of which 16 were waited for; matrix products, arithmetic and copies ran while one was open for 13% of the time, Pallas kernels for 0%

profile of v1, /device:TPU:0, one launch (start us, length us, event | category | flops | bytes accessed | tf_op | source)
XLA Modules:
  0.0 114.7 jit_solution(8460109473232104176)
XLA Ops:
  1.3 2.5 %collective-permute-start = (f32[1,8,256]{2,1,0:T(8,128)S(1)}, f32[1,8,256]{2,1,0:T(8,128)S(1)}, u32[]{:S(2)}, u32[]{:S(2)}) collective-permute-start(f32[1,8,256]{2,1,0:T(8,128)S(1)} %slice_bitcast_fusion.7), channel_id=1, source_target_pairs={{0,4},{4,8},{8,12},{12,16},{16,20},{20,24},{24,28},{1,5},{5,9},{9,... | collective-permute-start | bytes 24584 | tf_op jit(solution)/shard_map/ppermute | solution.py:12
  3.9 2.8 %copy.16 = f32[32,8,8,256]{3,0,2,1:T(8,128)S(1)} copy(f32[32,8,8,256]{3,2,1,0:T(8,128)} %param.13) | data formatting | bytes 4194304 | tf_op args[0]
  7.6 4.5 %collective-permute-start.3 = (f32[32,1,8,256]{3,0,2,1:T(8,128)}, f32[32,1,8,256]{3,0,2,1:T(8,128)S(1)}, u32[]{:S(2)}, u32[]{:S(2)}) collective-permute-start(f32[32,1,8,256]{3,0,2,1:T(8,128)} %get-tuple-element.39), channel_id=1, source_target_pairs={{0,4},{4,8},{8,12},{12,16},{16,20},{20,24},{24,28},{1,5},{5,9},{9,... | collective-permute-start | bytes 786440 | tf_op jit(solution)/shard_map/ppermute | solution.py:23
  12.1 3.5 %collective-permute-start.1 = (f32[8,1,256]{2,1,0:T(1,128)S(1)}, f32[8,1,256]{2,1,0:T(1,128)S(1)}, u32[]{:S(2)}, u32[]{:S(2)}) collective-permute-start(f32[8,1,256]{2,1,0:T(1,128)S(1)} %slice.255), channel_id=1, source_target_pairs={{0,1},{1,2},{2,3},{4,5},{5,6},{6,7},{8,9},{9,10},{10,11},{12,13},{... | collective-permute-start | bytes 24584 | tf_op jit(solution)/shard_map/ppermute | solution.py:12
  19.4 3.0 %subtract_multiply_fusion = (f32[32,8,8,256]{3,0,2,1:T(8,128)S(1)}, f32[32,10,8,256]{3,0,2,1:T(8,128)S(1)}) fusion(f32[32,8,8,255]{3,0,2,1:T(8,128)} %slice.262, f32[8,8,256]{2,1,0:T(8,128)S(1)} %get-tuple-element.43, f32[32,8,8,256]{3,2,1,0:T(8,128)S(1)} %copy-done, f32[32,10,8,256]{3,0,2,1:T(8,128)S(1)} %constant_dynamic-update-slice_fusion.2), kind=kLoop, calls=%fused_computation.18 | loop fusion | flops 1048576 | bytes 8445952 | tf_op jit(solution)/shard_map/mul | solution.py:72
  24.0 4.7 %collective-permute-start.5 = (f32[32,10,1,256]{3,0,2,1:T(8,128)S(1)}, f32[32,10,1,256]{3,0,2,1:T(8,128)S(1)}, u32[]{:S(2)}, u32[]{:S(2)}) collective-permute-start(f32[32,10,1,256]{3,0,2,1:T(8,128)S(1)} %get-tuple-element.35), channel_id=1, source_target_pairs={{0,1},{1,2},{2,3},{4,5},{5,6},{6,7},{8,9},{9,10},{10,11},{12,13},{... | collective-permute-start | bytes 983048 | tf_op jit(solution)/shard_map/ppermute | solution.py:23
  28.7 2.7 %convolution_bitcast_fusion = f32[32,1]{1,0:T(8,128)S(1)} fusion(f32[8,8,256,1]{2,1,0,3:T(8,128)S(1)} %bitcast.169, f32[32,8,8,256]{3,2,1,0:T(8,128)S(1)} %copy-done), kind=kOutput, calls=%fused_computation.19 | convolution fusion | flops 6291456 | bytes 2162816 | tf_op jit(solution)/shard_map/dot_general | solution.py:97
  31.5 3.5 %collective-permute-done.4 = f32[32,10,1,256]{3,0,2,1:T(8,128)S(1)} collective-permute-done((f32[32,10,1,256]{3,0,2,1:T(8,128)S(1)}, f32[32,10,1,256]{3,0,2,1:T(8,128)S(1)}, u32[]{:S(2)}, u32[]{:S(2)}) %collective-permute-start.4) | collective-permute-done | bytes 327712 | tf_op jit(solution)/shard_map/ppermute | solution.py:25
  36.5 2.9 %fusion.3 = f32[32,8,8,256]{3,0,2,1:T(8,128)S(1)} fusion(f32[32,8,8,256]{3,0,2,1:T(8,128)S(1)} %copy-done.2, f32[32,10,8,256]{3,0,2,1:T(8,128)S(1)} %constant_dynamic-update-slice_fusion, f32[32,10,1,256]{3,0,2,1:T(8,128)S(1)} %collective-permute-done.5, f32[32,1,8,256]{3,0,2,1:T(8,128)S(1)} %collective-permute-done.3, ...), kind=kLoop, calls=%fused_computation.4 | loop fusion | flops 9961472 | bytes 12509184 | tf_op jit(solution)/shard_map/sub | solution.py:74
  39.4 2.9 %convolution_bitcast_fusion.1 = f32[32,32]{1,0:T(8,128)S(1)} fusion(f32[32,8,8,256]{3,0,2,1:T(8,128)S(1)} %fusion.3, f32[32,8,8,256]{3,2,1,0:T(8,128)S(1)} %copy-done), kind=kOutput, calls=%fused_computation.20 | convolution fusion | flops 201326592 | bytes 4198400 | tf_op jit(solution)/shard_map/dot_general | solution.py:96
  42.4 3.5 %collective-permute-start.6 = (f32[32,33]{1,0:T(8,128)S(1)}, f32[32,33]{1,0:T(8,128)S(1)}, u32[]{:S(2)}, u32[]{:S(2)}) collective-permute-start(f32[32,33]{1,0:T(8,128)S(1)} %pad_maximum_fusion.4), channel_id=1, source_target_pairs={{0,2},{1,3},{2,0},{3,1},{4,6},{5,7},{6,4},{7,5},{8,10},{9,11},{10,... | collective-permute-start | bytes 12680 | tf_op jit(solution)/shard_map/ppermute | solution.py:52
  47.7 2.1 %collective-permute-start.8 = (f32[32,33]{1,0:T(8,128)S(1)}, f32[32,33]{1,0:T(8,128)S(1)}, u32[]{:S(2)}, u32[]{:S(2)}) collective-permute-start(f32[32,33]{1,0:T(8,128)S(1)} %fusion.62), channel_id=1, source_target_pairs={{0,8},{1,9},{2,10},{3,11},{4,12},{5,13},{6,14},{7,15},{8,0},{9,1},... | collective-permute-start | bytes 12680 | tf_op jit(solution)/shard_map/ppermute | solution.py:52
  56.8 2.8 %collective-permute-done.12 = f32[32,33]{1,0:T(8,128)S(1)} collective-permute-done((f32[32,33]{1,0:T(8,128)S(1)}, f32[32,33]{1,0:T(8,128)S(1)}, u32[]{:S(2)}, u32[]{:S(2)}) %collective-permute-start.12) | collective-permute-done | bytes 4256 | tf_op jit(solution)/shard_map/ppermute | solution.py:52
  60.0 2.9 %cholesky.18 = f32[32,32]{1,0:T(8,128)S(1)} custom-call(f32[32,32]{1,0:T(8,128)S(1)} %fusion.34), custom_call_target="Cholesky" | custom-call | tf_op jit(solution)/shard_map/jit(cholesky)/cholesky | solution.py:78
  64.2 2.4 %custom-call.11 = f32[1,32,32]{1,2,0:T(8,128)S(1)} custom-call(f32[1,32,32]{2,1,0:T(8,128)S(1)} %fusion.28), custom_call_target="InvertDiagBlocksLowerTriangular" | custom-call | tf_op jit(solution)/shard_map/triangular_solve/custom-call.2 | solution.py:80
  67.0 2.7 %fusion.52 = f32[1,8,8,256]{3,0,2,1:T(1,128)S(1)} fusion(f32[32,1,1,1]{0,1,3,2:T(1,128)S(1)} %convolution_bitcast_fusion.3, f32[32,8,8,256]{3,0,2,1:T(8,128)} %copy-done.3), kind=kOutput, calls=%fused_computation.104 | convolution fusion | flops 6291456 | bytes 2162816 | tf_op jit(solution)/shard_map/dot_general | solution.py:103
  72.4 3.4 %collective-permute-done.14 = f32[1,8,256]{2,1,0:T(8,128)S(1)} collective-permute-done((f32[1,8,256]{2,1,0:T(8,128)S(1)}, f32[1,8,256]{2,1,0:T(8,128)S(1)}, u32[]{:S(2)}, u32[]{:S(2)}) %collective-permute-start.14) | collective-permute-done | bytes 8224 | tf_op jit(solution)/shard_map/ppermute | solution.py:25
  75.8 2.0 %collective-permute-start.15 = (f32[10,1,256]{2,1,0:T(1,128)S(1)}, f32[10,1,256]{2,1,0:T(1,128)S(1)}, u32[]{:S(2)}, u32[]{:S(2)}) collective-permute-start(f32[10,1,256]{2,1,0:T(1,128)S(1)} %get-tuple-element.47), channel_id=1, source_target_pairs={{0,1},{1,2},{2,3},{4,5},{5,6},{6,7},{8,9},{9,10},{10,11},{12,13},{... | collective-permute-start | bytes 30728 | tf_op jit(solution)/shard_map/ppermute | solution.py:23
  80.6 3.9 %collective-permute-done.16 = f32[10,1,256]{2,1,0:T(1,128)S(1)} collective-permute-done((f32[10,1,256]{2,1,0:T(1,128)S(1)}, f32[10,1,256]{2,1,0:T(1,128)S(1)}, u32[]{:S(2)}, u32[]{:S(2)}) %collective-permute-start.16) | collective-permute-done | bytes 10272 | tf_op jit(solution)/shard_map/ppermute | solution.py:25
  90.4 2.2 %fusion.44 = f32[1,8,8,256]{3,0,2,1:T(1,128)S(1)} fusion(f32[32,1,1,1]{0,1,3,2:T(1,128)S(1)} %convolution_bitcast_fusion.3, f32[32,8,8,256]{3,2,1,0:T(8,128)S(1)} %copy-done), kind=kOutput, calls=%fused_computation.97 | convolution fusion | flops 6291456 | bytes 2162816 | tf_op jit(solution)/shard_map/dot_general | solution.py:102
  95.0 2.9 %collective-permute-start.19 = (f32[1,34]{1,0:T(1,128)S(1)}, f32[1,34]{1,0:T(1,128)S(1)}, u32[]{:S(2)}, u32[]{:S(2)}) collective-permute-start(f32[1,34]{1,0:T(1,128)S(1)} %fusion.61), channel_id=1, source_target_pairs={{0,8},{1,9},{2,10},{3,11},{4,12},{5,13},{6,14},{7,15},{8,0},{9,1},... | collective-permute-start | bytes 416 | tf_op jit(solution)/shard_map/ppermute | solution.py:52
  101.9 2.0 %collective-permute-start.22 = (f32[1,34]{1,0:T(1,128)S(1)}, f32[1,34]{1,0:T(1,128)S(1)}, u32[]{:S(2)}, u32[]{:S(2)}) collective-permute-start(f32[1,34]{1,0:T(1,128)S(1)} %add_add_fusion.3), channel_id=1, source_target_pairs={{0,1},{1,0},{2,3},{3,2},{4,5},{5,4},{6,7},{7,6},{8,9},{9,8},{10,11... | collective-permute-start | bytes 416 | tf_op jit(solution)/shard_map/ppermute | solution.py:52
  105.4 2.9 %collective-permute-done.23 = f32[1,34]{1,0:T(1,128)S(1)} collective-permute-done((f32[1,34]{1,0:T(1,128)S(1)}, f32[1,34]{1,0:T(1,128)S(1)}, u32[]{:S(2)}, u32[]{:S(2)}) %collective-permute-start.23) | collective-permute-done | bytes 168 | tf_op jit(solution)/shard_map/ppermute | solution.py:52
  109.8 2.2 %fusion.37 = f32[1,8,8,256]{3,0,2,1:T(1,128)S(1)} fusion(f32[1,32]{1,0:T(1,128)S(1)} %get-tuple-element.54, f32[32,8,8,256]{3,2,1,0:T(8,128)S(1)} %copy-done), kind=kOutput, calls=%fused_computation.87 | convolution fusion | flops 6291456 | bytes 2162816 | tf_op jit(solution)/shard_map/dot_general | solution.py:123
  (92 shorter events, 40.5 us)
Async XLA Ops:
  1.3 17.7 %collective-permute-start = (f32[1,8,256]{2,1,0:T(8,128)S(1)}, f32[1,8,256]{2,1,0:T(8,128)S(1)}, u32[]{:S(2)}, u32[]{:S(2)}) collective-permute-start(f32[1,8,256]{2,1,0:T(8,128)S(1)} %slice_bitcast_fusion.7), channel_id=1, source_target_pairs={{0,4},{4,8},{8,12},{12,16},{16,20},{20,24},{24,28},{1,5},{5,9},{9,... | collective-permute-start | bytes 24584 | tf_op jit(solution)/shard_map/ppermute | solution.py:12
  7.6 11.7 %collective-permute-start.3 = (f32[32,1,8,256]{3,0,2,1:T(8,128)}, f32[32,1,8,256]{3,0,2,1:T(8,128)S(1)}, u32[]{:S(2)}, u32[]{:S(2)}) collective-permute-start(f32[32,1,8,256]{3,0,2,1:T(8,128)} %get-tuple-element.39), channel_id=1, source_target_pairs={{0,4},{4,8},{8,12},{12,16},{16,20},{20,24},{24,28},{1,5},{5,9},{9,... | collective-permute-start | bytes 786440 | tf_op jit(solution)/shard_map/ppermute | solution.py:23
  12.1 7.1 %collective-permute-start.1 = (f32[8,1,256]{2,1,0:T(1,128)S(1)}, f32[8,1,256]{2,1,0:T(1,128)S(1)}, u32[]{:S(2)}, u32[]{:S(2)}) collective-permute-start(f32[8,1,256]{2,1,0:T(1,128)S(1)} %slice.255), channel_id=1, source_target_pairs={{0,1},{1,2},{2,3},{4,5},{5,6},{6,7},{8,9},{9,10},{10,11},{12,13},{... | collective-permute-start | bytes 24584 | tf_op jit(solution)/shard_map/ppermute | solution.py:12
  15.6 6.8 %collective-permute-start.2 = (f32[32,1,8,256]{3,0,2,1:T(8,128)}, f32[32,1,8,256]{3,0,2,1:T(8,128)S(1)}, u32[]{:S(2)}, u32[]{:S(2)}) collective-permute-start(f32[32,1,8,256]{3,0,2,1:T(8,128)} %get-tuple-element.38), channel_id=1, source_target_pairs={{4,0},{8,4},{12,8},{16,12},{20,16},{24,20},{28,24},{5,1},{9,5},{13... | collective-permute-start | bytes 786440 | tf_op jit(solution)/shard_map/ppermute | solution.py:25
  22.5 12.5 %collective-permute-start.4 = (f32[32,10,1,256]{3,0,2,1:T(8,128)S(1)}, f32[32,10,1,256]{3,0,2,1:T(8,128)S(1)}, u32[]{:S(2)}, u32[]{:S(2)}) collective-permute-start(f32[32,10,1,256]{3,0,2,1:T(8,128)S(1)} %get-tuple-element.34), channel_id=1, source_target_pairs={{1,0},{2,1},{3,2},{5,4},{6,5},{7,6},{9,8},{10,9},{11,10},{13,12},{... | collective-permute-start | bytes 983048 | tf_op jit(solution)/shard_map/ppermute | solution.py:25
  24.0 12.5 %collective-permute-start.5 = (f32[32,10,1,256]{3,0,2,1:T(8,128)S(1)}, f32[32,10,1,256]{3,0,2,1:T(8,128)S(1)}, u32[]{:S(2)}, u32[]{:S(2)}) collective-permute-start(f32[32,10,1,256]{3,0,2,1:T(8,128)S(1)} %get-tuple-element.35), channel_id=1, source_target_pairs={{0,1},{1,2},{2,3},{4,5},{5,6},{6,7},{8,9},{9,10},{10,11},{12,13},{... | collective-permute-start | bytes 983048 | tf_op jit(solution)/shard_map/ppermute | solution.py:23
  42.4 5.2 %collective-permute-start.6 = (f32[32,33]{1,0:T(8,128)S(1)}, f32[32,33]{1,0:T(8,128)S(1)}, u32[]{:S(2)}, u32[]{:S(2)}) collective-permute-start(f32[32,33]{1,0:T(8,128)S(1)} %pad_maximum_fusion.4), channel_id=1, source_target_pairs={{0,2},{1,3},{2,0},{3,1},{4,6},{5,7},{6,4},{7,5},{8,10},{9,11},{10,... | collective-permute-start | bytes 12680 | tf_op jit(solution)/shard_map/ppermute | solution.py:52
  47.7 2.2 %collective-permute-start.7 = (f32[32,33]{1,0:T(8,128)S(1)}, f32[32,33]{1,0:T(8,128)S(1)}, u32[]{:S(2)}, u32[]{:S(2)}) collective-permute-start(f32[32,33]{1,0:T(8,128)S(1)} %fusion.62), channel_id=1, source_target_pairs={{0,4},{1,5},{2,6},{3,7},{4,0},{5,1},{6,2},{7,3},{8,12},{9,13},{10,... | collective-permute-start | bytes 12680 | tf_op jit(solution)/shard_map/ppermute | solution.py:52
  47.7 3.9 %collective-permute-start.8 = (f32[32,33]{1,0:T(8,128)S(1)}, f32[32,33]{1,0:T(8,128)S(1)}, u32[]{:S(2)}, u32[]{:S(2)}) collective-permute-start(f32[32,33]{1,0:T(8,128)S(1)} %fusion.62), channel_id=1, source_target_pairs={{0,8},{1,9},{2,10},{3,11},{4,12},{5,13},{6,14},{7,15},{8,0},{9,1},... | collective-permute-start | bytes 12680 | tf_op jit(solution)/shard_map/ppermute | solution.py:52
  49.8 3.2 %collective-permute-start.9 = (f32[32,33]{1,0:T(8,128)S(1)}, f32[32,33]{1,0:T(8,128)S(1)}, u32[]{:S(2)}, u32[]{:S(2)}) collective-permute-start(f32[32,33]{1,0:T(8,128)S(1)} %fusion.62), channel_id=1, source_target_pairs={{0,12},{1,13},{2,14},{3,15},{4,8},{5,9},{6,10},{7,11},{8,4},{9,5},... | collective-permute-start | bytes 12680 | tf_op jit(solution)/shard_map/ppermute | solution.py:52
  53.0 3.7 %collective-permute-start.10 = (f32[32,33]{1,0:T(8,128)S(1)}, f32[32,33]{1,0:T(8,128)S(1)}, u32[]{:S(2)}, u32[]{:S(2)}) collective-permute-start(f32[32,33]{1,0:T(8,128)S(1)} %add_add_fusion.1), channel_id=1, source_target_pairs={{0,16},{1,17},{2,18},{3,19},{4,20},{5,21},{6,22},{7,23},{8,24},{9,... | collective-permute-start | bytes 12680 | tf_op jit(solution)/shard_map/ppermute | solution.py:52
  53.1 3.7 %collective-permute-start.11 = (f32[32,33]{1,0:T(8,128)S(1)}, f32[32,33]{1,0:T(8,128)S(1)}, u32[]{:S(2)}, u32[]{:S(2)}) collective-permute-start(f32[32,33]{1,0:T(8,128)S(1)} %add_add_fusion.1), channel_id=1, source_target_pairs={{0,1},{1,0},{2,3},{3,2},{4,5},{5,4},{6,7},{7,6},{8,9},{9,8},{10,11... | collective-permute-start | bytes 12680 | tf_op jit(solution)/shard_map/ppermute | solution.py:52
  55.0 4.6 %collective-permute-start.12 = (f32[32,33]{1,0:T(8,128)S(1)}, f32[32,33]{1,0:T(8,128)S(1)}, u32[]{:S(2)}, u32[]{:S(2)}) collective-permute-start(f32[32,33]{1,0:T(8,128)S(1)} %add_add_fusion.1), channel_id=1, source_target_pairs={{0,17},{1,16},{2,19},{3,18},{4,21},{5,20},{6,23},{7,22},{8,25},{9,... | collective-permute-start | bytes 12680 | tf_op jit(solution)/shard_map/ppermute | solution.py:52
  69.8 2.6 %collective-permute-start.13 = (f32[1,8,256]{2,1,0:T(8,128)S(1)}, f32[1,8,256]{2,1,0:T(8,128)S(1)}, u32[]{:S(2)}, u32[]{:S(2)}) collective-permute-start(f32[1,8,256]{2,1,0:T(8,128)S(1)} %get-tuple-element.49), channel_id=1, source_target_pairs={{0,4},{4,8},{8,12},{12,16},{16,20},{20,24},{24,28},{1,5},{5,9},{9,... | collective-permute-start | bytes 24584 | tf_op jit(solution)/shard_map/ppermute | solution.py:23
  71.1 4.7 %collective-permute-start.14 = (f32[1,8,256]{2,1,0:T(8,128)S(1)}, f32[1,8,256]{2,1,0:T(8,128)S(1)}, u32[]{:S(2)}, u32[]{:S(2)}) collective-permute-start(f32[1,8,256]{2,1,0:T(8,128)S(1)} %get-tuple-element.50), channel_id=1, source_target_pairs={{4,0},{8,4},{12,8},{16,12},{20,16},{24,20},{28,24},{5,1},{9,5},{13... | collective-permute-start | bytes 24584 | tf_op jit(solution)/shard_map/ppermute | solution.py:25
  75.8 4.8 %collective-permute-start.15 = (f32[10,1,256]{2,1,0:T(1,128)S(1)}, f32[10,1,256]{2,1,0:T(1,128)S(1)}, u32[]{:S(2)}, u32[]{:S(2)}) collective-permute-start(f32[10,1,256]{2,1,0:T(1,128)S(1)} %get-tuple-element.47), channel_id=1, source_target_pairs={{0,1},{1,2},{2,3},{4,5},{5,6},{6,7},{8,9},{9,10},{10,11},{12,13},{... | collective-permute-start | bytes 30728 | tf_op jit(solution)/shard_map/ppermute | solution.py:23
  77.8 6.7 %collective-permute-start.16 = (f32[10,1,256]{2,1,0:T(1,128)S(1)}, f32[10,1,256]{2,1,0:T(1,128)S(1)}, u32[]{:S(2)}, u32[]{:S(2)}) collective-permute-start(f32[10,1,256]{2,1,0:T(1,128)S(1)} %get-tuple-element.48), channel_id=1, source_target_pairs={{1,0},{2,1},{3,2},{5,4},{6,5},{7,6},{9,8},{10,9},{11,10},{13,12},{... | collective-permute-start | bytes 30728 | tf_op jit(solution)/shard_map/ppermute | solution.py:25
  88.5 4.5 %collective-permute-start.17 = (f32[1,34]{1,0:T(1,128)S(1)}, f32[1,34]{1,0:T(1,128)S(1)}, u32[]{:S(2)}, u32[]{:S(2)}) collective-permute-start(f32[1,34]{1,0:T(1,128)S(1)} %maximum_bitcast_fusion.1), channel_id=1, source_target_pairs={{0,2},{1,3},{2,0},{3,1},{4,6},{5,7},{6,4},{7,5},{8,10},{9,11},{10,... | collective-permute-start | bytes 416 | tf_op jit(solution)/shard_map/ppermute | solution.py:52
  94.4 3.6 %collective-permute-start.18 = (f32[1,34]{1,0:T(1,128)S(1)}, f32[1,34]{1,0:T(1,128)S(1)}, u32[]{:S(2)}, u32[]{:S(2)}) collective-permute-start(f32[1,34]{1,0:T(1,128)S(1)} %fusion.61), channel_id=1, source_target_pairs={{0,4},{1,5},{2,6},{3,7},{4,0},{5,1},{6,2},{7,3},{8,12},{9,13},{10,... | collective-permute-start | bytes 416 | tf_op jit(solution)/shard_map/ppermute | solution.py:52
  95.0 4.5 %collective-permute-start.19 = (f32[1,34]{1,0:T(1,128)S(1)}, f32[1,34]{1,0:T(1,128)S(1)}, u32[]{:S(2)}, u32[]{:S(2)}) collective-permute-start(f32[1,34]{1,0:T(1,128)S(1)} %fusion.61), channel_id=1, source_target_pairs={{0,8},{1,9},{2,10},{3,11},{4,12},{5,13},{6,14},{7,15},{8,0},{9,1},... | collective-permute-start | bytes 416 | tf_op jit(solution)/shard_map/ppermute | solution.py:52
  97.9 3.0 %collective-permute-start.20 = (f32[1,34]{1,0:T(1,128)S(1)}, f32[1,34]{1,0:T(1,128)S(1)}, u32[]{:S(2)}, u32[]{:S(2)}) collective-permute-start(f32[1,34]{1,0:T(1,128)S(1)} %fusion.61), channel_id=1, source_target_pairs={{0,12},{1,13},{2,14},{3,15},{4,8},{5,9},{6,10},{7,11},{8,4},{9,5},... | collective-permute-start | bytes 416 | tf_op jit(solution)/shard_map/ppermute | solution.py:52
  100.9 3.6 %collective-permute-start.21 = (f32[1,34]{1,0:T(1,128)S(1)}, f32[1,34]{1,0:T(1,128)S(1)}, u32[]{:S(2)}, u32[]{:S(2)}) collective-permute-start(f32[1,34]{1,0:T(1,128)S(1)} %add_add_fusion.3), channel_id=1, source_target_pairs={{0,16},{1,17},{2,18},{3,19},{4,20},{5,21},{6,22},{7,23},{8,24},{9,... | collective-permute-start | bytes 416 | tf_op jit(solution)/shard_map/ppermute | solution.py:52
  101.9 3.6 %collective-permute-start.22 = (f32[1,34]{1,0:T(1,128)S(1)}, f32[1,34]{1,0:T(1,128)S(1)}, u32[]{:S(2)}, u32[]{:S(2)}) collective-permute-start(f32[1,34]{1,0:T(1,128)S(1)} %add_add_fusion.3), channel_id=1, source_target_pairs={{0,1},{1,0},{2,3},{3,2},{4,5},{5,4},{6,7},{7,6},{8,9},{9,8},{10,11... | collective-permute-start | bytes 416 | tf_op jit(solution)/shard_map/ppermute | solution.py:52
  103.9 4.5 %collective-permute-start.23 = (f32[1,34]{1,0:T(1,128)S(1)}, f32[1,34]{1,0:T(1,128)S(1)}, u32[]{:S(2)}, u32[]{:S(2)}) collective-permute-start(f32[1,34]{1,0:T(1,128)S(1)} %add_add_fusion.3), channel_id=1, source_target_pairs={{0,17},{1,16},{2,19},{3,18},{4,21},{5,20},{6,23},{7,22},{8,25},{9,... | collective-permute-start | bytes 416 | tf_op jit(solution)/shard_map/ppermute | solution.py:52
  (7 other events, 67.2 us)

commit v2 on v1

v2 whole, which is shorter than its diff:
```python
import functools
import jax
import jax.numpy as jnp
from jax import lax
from jax.experimental import pallas as pl
from jax.experimental.pallas import tpu as pltpu
from jax.sharding import PartitionSpec as P

F32 = jnp.float32
BF16 = jnp.bfloat16
EXTRA = 16
LANES = 128
VM = pl.BlockSpec(memory_space=pltpu.VMEM)
RAW = pl.BlockSpec(memory_space=pl.ANY)
SM = pl.BlockSpec(memory_space=pltpu.SMEM)


def shape(*dims, dtype=F32):
    return jax.ShapeDtypeStruct(dims, dtype)


def call(body, outs, ins, scratch=(), limit=24, work=0, moved=0):
    return pl.pallas_call(
        body,
        out_shape=outs,
        in_specs=ins,
        out_specs=jax.tree.map(lambda _: VM, outs),
        scratch_shapes=list(scratch),
        compiler_params=pltpu.CompilerParams(vmem_limit_bytes=limit << 20),
        cost_estimate=pl.CostEstimate(flops=work, bytes_accessed=moved, transcendentals=0),
    )


def sum_stages():
    wide, deep = lax.axis_size("gx"), lax.axis_size("gy")
    along_x = [(1 << k, 0) for k in range(wide.bit_length() - 1)]
    along_y = [(0, 1 << k) for k in range(deep.bit_length() - 1)]
    steps = along_y[:0:-1] + along_x + along_y[:1]
    single = len(steps) % 2
    stages = [[step] for step in steps[:single]]
    for at in range(single, len(steps), 2):
        (a, b), (c, d) = steps[at], steps[at + 1]
        stages.append([(a, b), (c, d), (a ^ c, b ^ d)])
    return stages


def sum_all(part):
    wide, deep = lax.axis_size("gx"), lax.axis_size("gy")
    if wide & (wide - 1) or deep & (deep - 1):
        return lax.psum(part, ("gx", "gy"))
    devices = [(i, j) for i in range(wide) for j in range(deep)]
    for stage in sum_stages():
        others = [
            lax.ppermute(
                part,
                ("gx", "gy"),
                [(i * deep + j, (i ^ a) * deep + (j ^ b)) for i, j in devices],
            )
            for a, b in stage
        ]
        for other in others:
            part = part + other
    return part


def send(block, axis, step):
    size = lax.axis_size(axis)
    return lax.ppermute(block, axis, [(i, i + step) for i in range(size) if 0 <= i + step < size])


def halves(value):
    high = value.astype(BF16)
    return high, (value - high.astype(F32)).astype(BF16)


def put(stack, at, value, extra=None):
    count, deep = value.shape
    lanes = pl.ds(at * deep, deep)
    high, low = halves(value)
    stack[pl.ds(0, count), lanes] = high
    stack[pl.ds(count, count), lanes] = low
    if extra is not None:
        high, low = halves(extra)
        row = lax.broadcasted_iota(jnp.int32, (EXTRA, deep), 0)
        both = jnp.where(row == 0, high.astype(F32), jnp.where(row == 1, low.astype(F32), 0.0))
        stack[pl.ds(2 * count, EXTRA), lanes] = both.astype(BF16)


def by_rows(left, right):
    return lax.dot_general(left, right, (((1,), (1,)), ((), ())), preferred_element_type=F32)


def fold_rows(full, count):
    top = full[:count] + full[count : 2 * count]
    if full.shape[0] == 2 * count:
        return top
    last = full[2 * count : 2 * count + 1] + full[2 * count + 1 : 2 * count + 2]
    return jnp.concatenate([top, jnp.broadcast_to(last, (8, full.shape[1]))], axis=0)


def fold(full, count):
    rows = fold_rows(full, count)
    body = rows[:, :count] + rows[:, count : 2 * count]
    last = rows[:, 2 * count : 2 * count + 1] + rows[:, 2 * count + 1 : 2 * count + 2]
    return body, last


def faces_kernel(basis, coeff, up_x, down_x, up_y, down_y, sems):
    count, nx, ny, deep = basis.shape
    moves = []
    for y in range(ny):
        rows = pl.ds(y * count, count)
        moves.append((basis.at[:, nx - 1, y, :], up_x.at[rows]))
        moves.append((basis.at[:, 0, y, :], down_x.at[rows]))
    for x in range(nx):
        rows = pl.ds(x * count, count)
        moves.append((basis.at[:, x, ny - 1, :], up_y.at[rows]))
        moves.append((basis.at[:, x, 0, :], down_y.at[rows]))
    moves.append((coeff.at[0, nx - 1], up_x.at[pl.ds(ny * count, ny)]))
    moves.append((coeff.at[1, :, ny - 1, :], up_y.at[pl.ds(nx * count, nx)]))
    copies = [pltpu.make_async_copy(a, b, sems.at[k]) for k, (a, b) in enumerate(moves)]
    for copy in copies:
        copy.start()
    for copy in copies:
        copy.wait()


def faces(basis, coeff):
    count, nx, ny, deep = basis.shape
    outs = (
        shape(ny * count + ny, deep),
        shape(ny * count, deep),
        shape(nx * count + nx, deep),
        shape(nx * count, deep),
    )
    sems = pltpu.SemaphoreType.DMA((2 * nx + 2 * ny + 2,))
    return call(faces_kernel, outs, [RAW, RAW], [sems], limit=4)(basis, coeff)


def row(ref, *at):
    return ref[at[:-1] + (pl.ds(at[-1], 1), slice(None))]


def near_z(field, upper, lower):
    deep = field.shape[1]
    above, below = pltpu.roll(field, deep - 1, 1), pltpu.roll(field, 1, 1)
    return upper * above + lower * below


def inner_kernel(basis, coeff, extra, cols, inner, stack, upper, lower, diag, sems):
    nx, ny, count, deep = cols.shape
    copies = []
    for x in range(nx):
        for y in range(ny):
            copies.append(
                pltpu.make_async_copy(basis.at[:, x, y, :], cols.at[x, y], sems.at[x * ny + y])
            )
            copies[-1].start()
    level = lax.broadcasted_iota(jnp.int32, (ny, deep), 0)
    lane = lax.broadcasted_iota(jnp.int32, (ny, deep), 1)
    for x in range(nx):
        cz = coeff[2, x]
        upper[x] = jnp.where(lane == deep - 1, 0.0, cz)
        under = jnp.where(lane == 0, 0.0, pltpu.roll(cz, 1, 1))
        lower[x] = under
        cy = coeff[1, x]
        total = extra[x] + coeff[0, x] + cy + cz + under
        total = total + jnp.where(level == 0, 0.0, pltpu.roll(cy, 1, 0))
        if x:
            total = total + coeff[0, x - 1]
        diag[x] = total
    for copy in copies:
        copy.wait()
    for x in range(nx):
        for y in range(ny):
            here = cols[x, y]
            sums = near_z(here, row(upper, x, y), row(lower, x, y))
            if x + 1 < nx:
                sums += row(coeff, 0, x, y) * cols[x + 1, y]
            if x:
                sums += row(coeff, 0, x - 1, y) * cols[x - 1, y]
            if y + 1 < ny:
                sums += row(coeff, 1, x, y) * cols[x, y + 1]
            if y:
                sums += row(coeff, 1, x, y - 1) * cols[x, y - 1]
            inner[x, y] = row(diag, x, y) * here - sums
            put(stack, x * ny + y, here)


def inside(basis, coeff, extra):
    count, nx, ny, deep = basis.shape
    cells = nx * ny * deep
    outs = (shape(nx, ny, count, deep), shape(nx, ny, count, deep), shape(2 * count, cells, dtype=BF16))
    small = pltpu.VMEM((nx, ny, deep), F32)
    sems = pltpu.SemaphoreType.DMA((nx * ny,))
    return call(
        inner_kernel, outs, [RAW, VM, VM], [small, small, small, sems],
        work=20 * count * cells, moved=16 * count * cells,
    )(basis, coeff, extra)


def inverse_diagonal(coeff, extra, from_left, from_front, count, x):
    nx, ny, deep = extra.shape
    level = lax.broadcasted_iota(jnp.int32, (ny, deep), 0)
    lane = lax.broadcasted_iota(jnp.int32, (ny, deep), 1)
    cy, cz = coeff[1, x], coeff[2, x]
    total = extra[x] + coeff[0, x] + cy + cz
    total += jnp.where(lane == 0, 0.0, pltpu.roll(cz, 1, 1))
    front = from_front[pl.ds(nx * count + x, 1), :]
    total += jnp.where(level == 0, front, pltpu.roll(cy, 1, 0))
    total += coeff[0, x - 1] if x else from_left[pl.ds(ny * count, ny), :]
    return 1.0 / total


def full_value(cols, inner, coeff, left, right, front, back, x, y):
    nx, ny, count, deep = cols.shape
    value = inner[x, y]
    of_x, of_y = pl.ds(y * count, count), pl.ds(x * count, count)
    if x == 0:
        value += left[pl.ds(ny * count + y, 1), :] * (cols[x, y] - left[of_x])
    if x == nx - 1:
        value -= row(coeff, 0, x, y) * right[of_x]
    if y == 0:
        value += front[pl.ds(nx * count + x, 1), :] * (cols[x, y] - front[of_y])
    if y == ny - 1:
        value -= row(coeff, 1, x, y) * back[of_y]
    return value


def border_kernel(odd, cols, inner, coeff, extra, rhs, left, right, front, back, face_x, face_y, scale):
    nx, ny, count, deep = cols.shape
    for x in range(nx):
        scale[x] = inverse_diagonal(coeff, extra, left, front, count, x)
    value = functools.partial(full_value, cols, inner, coeff, left, right, front, back)
    for y in range(ny):
        face_x[pl.ds(y * count, count), :] = value(0, y) * row(scale, 0, y)
    face_x[pl.ds(ny * count, ny), :] = scale[0] * rhs[0]

    def side(y):
        for x in range(nx):
            face_y[pl.ds(x * count, count), :] = value(x, y) * row(scale, x, y)
            face_y[pl.ds(nx * count + x, 1), :] = row(scale, x, y) * row(rhs, x, y)

    @pl.when(odd[0] == 0)
    def _():
        side(0)

    @pl.when(odd[0] == 1)
    def _():
        side(ny - 1)


def border(odd, cols, inner, coeff, extra, rhs, halo):
    nx, ny, count, deep = cols.shape
    outs = (shape(ny * count + ny, deep), shape(nx * count + nx, deep))
    return call(
        border_kernel, outs, [SM] + [VM] * 9, [pltpu.VMEM((nx, ny, deep), F32)], limit=10
    )(odd, cols, inner, coeff, extra, rhs, *halo)


def local_kernel(
    cols, inner, basis_stack, coeff, extra, rhs, left, right, front, back,
    part, scaled_stack, value_stack, pair_stack, scaled, scale, upper, scaled_rhs,
):
    nx, ny, count, deep = cols.shape
    lane = lax.broadcasted_iota(jnp.int32, (ny, deep), 1)
    for x in range(nx):
        inverse = inverse_diagonal(coeff, extra, left, front, count, x)
        scale[x] = inverse
        scaled_rhs[x] = inverse * rhs[x]
        upper[x] = jnp.where(lane == deep - 1, 0.0, coeff[2, x])
    for x in range(nx):
        for y in range(ny):
            value = full_value(cols, inner, coeff, left, right, front, back, x, y)
            result = value * row(scale, x, y)
            scaled[x, y] = result
            put(value_stack, x * ny + y, value, row(rhs, x, y))
            put(scaled_stack, x * ny + y, result, row(scaled_rhs, x, y))
    for x in range(nx):
        for y in range(ny):
            over, ahead = row(upper, x, y), pltpu.roll(scaled[x, y], deep - 1, 1)
            pair = over * ahead
            pair_rhs = over * pltpu.roll(jnp.broadcast_to(row(scaled_rhs, x, y), (8, deep)), deep - 1, 1)[:1]
            if x + 1 < nx:
                pair += row(coeff, 0, x, y) * scaled[x + 1, y]
                pair_rhs += row(coeff, 0, x, y) * row(scaled_rhs, x + 1, y)
            if y + 1 < ny:
                pair += row(coeff, 1, x, y) * scaled[x, y + 1]
                pair_rhs += row(coeff, 1, x, y) * row(scaled_rhs, x, y + 1)
            put(pair_stack, x * ny + y, pair, pair_rhs)
    gram, projected = fold(by_rows(basis_stack[...], value_stack[...]), count)
    square, square_rhs = fold(by_rows(value_stack[...], scaled_stack[...]), count)
    pairs, pairs_rhs = fold(by_rows(scaled_stack[...], pair_stack[...]), count)
    part[...] = jnp.zeros_like(part)
    part[pl.ds(0, count), pl.ds(0, count)] = gram
    part[:, pl.ds(count, count)] = square
    part[:, pl.ds(2 * count, count)] = pairs
    part[pl.ds(0, count), pl.ds(3 * count, 1)] = projected
    part[:, pl.ds(3 * count + 1, 1)] = square_rhs
    part[:, pl.ds(3 * count + 2, 1)] = pairs_rhs


def local_sums(cols, inner, basis_stack, coeff, extra, rhs, halo):
    nx, ny, count, deep = cols.shape
    cells = nx * ny * deep
    tall = 2 * count + EXTRA
    small = pltpu.VMEM((nx, ny, deep), F32)
    outs = (shape(count + 8, -(-(3 * count + 3) // LANES) * LANES), shape(tall, cells, dtype=BF16))
    return call(
        local_kernel,
        outs,
        [VM] * 10,
        [
            pltpu.VMEM((tall, cells), BF16),
            pltpu.VMEM((tall, cells), BF16),
            pltpu.VMEM((nx, ny, count, deep), F32),
            small, small, small,
        ],
        limit=28,
        work=60 * count * cells,
        moved=24 * count * cells,
    )(cols, inner, basis_stack, coeff, extra, rhs, *halo)


def shared_kernel(odd, part, scaled_stack, coeff, front, far_x, far_y, total, mine, pair_stack):
    count = part.shape[0] - 8
    nx, ny, deep = coeff.shape[1:]
    for y in range(ny):
        face = row(coeff, 0, nx - 1, y)
        put(
            pair_stack, y, face * far_x[pl.ds(y * count, count), :],
            face * far_x[pl.ds(ny * count + y, 1), :],
        )
        mine[:, pl.ds(y * deep, deep)] = scaled_stack[:, pl.ds(((nx - 1) * ny + y) * deep, deep)]
    for x in range(nx):
        own = front[pl.ds(nx * count + x, 1), :]
        face = jnp.where(odd[0] == 0, row(coeff, 1, x, ny - 1), own)
        put(
            pair_stack, ny + x, face * far_y[pl.ds(x * count, count), :],
            face * far_y[pl.ds(nx * count + x, 1), :],
        )

    def side(y):
        for x in range(nx):
            mine[:, pl.ds((ny + x) * deep, deep)] = scaled_stack[:, pl.ds((x * ny + y) * deep, deep)]

    @pl.when(odd[0] == 0)
    def _():
        side(ny - 1)

    @pl.when(odd[0] == 1)
    def _():
        side(0)

    pairs, pairs_rhs = fold(by_rows(mine[...], pair_stack[...]), count)
    total[...] = part[...]
    total[:, pl.ds(2 * count, count)] += pairs
    total[:, pl.ds(3 * count + 2, 1)] += pairs_rhs


def shared_sums(odd, part, scaled_stack, coeff, front, far_x, far_y):
    nx, ny, deep = coeff.shape[1:]
    wide = pltpu.VMEM((scaled_stack.shape[0], (nx + ny) * deep), BF16)
    return call(
        shared_kernel, shape(*part.shape), [SM] + [VM] * 6, [wide, wide], limit=12
    )(odd, part, scaled_stack, coeff, front, far_x, far_y)


def finish_kernel(total, basis_stack, scaled_stack, guess, stepped):
    count = total.shape[0] - 8
    nx, ny, deep = guess.shape
    sums = total[pl.ds(0, count), :]
    work = sums
    level = lax.broadcasted_iota(jnp.int32, (count, 1), 0)
    for k in range(count):
        line = work[k : k + 1, :] / work[k : k + 1, k : k + 1]
        column = work[:, k : k + 1]
        work = jnp.where(level == k, line, work - column * line)
    at = 3 * count
    turned = work.T
    weights = work[:, at : at + 1]
    weights_row = turned[at : at + 1, :]
    shift_row = turned[at + 1 : at + 2, :] - jnp.sum(weights * turned[count : 2 * count, :], axis=0, keepdims=True)
    sums_row = sums.T
    rhs_row = sums_row[at + 1 : at + 2, :]
    both = jnp.sum(weights * sums, axis=0, keepdims=True)
    correction = rhs_row - both[:, count : 2 * count]
    along = jnp.sum(weights_row * (rhs_row + correction), axis=1, keepdims=True)
    tail = total[pl.ds(count, 1), :]
    size = tail[:, at + 1 : at + 2] - along
    crossing = jnp.sum(
        weights_row * (both[:, 2 * count : at] - sums_row[at + 2 : at + 3, :] - tail[:, 2 * count : at]),
        axis=1, keepdims=True,
    ) + tail[:, at + 2 : at + 3]
    lost = jnp.sum(correction * shift_row, axis=1, keepdims=True)
    step = size / (size - 2.0 * crossing - lost)
    first = lax.broadcasted_iota(jnp.int32, (EXTRA, count), 0)
    of_basis = jnp.where(first == 0, weights_row, jnp.where(first == 1, weights_row - step * shift_row, 0.0))
    of_scaled = jnp.where(first == 1, -step * weights_row, 0.0)
    last = lax.broadcasted_iota(jnp.int32, (EXTRA, EXTRA), 0)
    place = lax.broadcasted_iota(jnp.int32, (EXTRA, EXTRA), 1)
    of_rhs = jnp.where((last == 1) & (place < 2), step, 0.0)
    basis_high, basis_low = halves(jnp.concatenate([of_basis, of_basis], axis=1))
    scaled_high, scaled_low = halves(jnp.concatenate([of_scaled, of_scaled, of_rhs], axis=1))
    for x in range(nx):
        lanes = pl.ds(x * ny * deep, ny * deep)
        fields = basis_stack[:, lanes]
        result = jnp.dot(basis_high, fields, preferred_element_type=F32)
        result += jnp.dot(basis_low, fields, preferred_element_type=F32)
        fields = scaled_stack[:, lanes]
        result += jnp.dot(scaled_high, fields, preferred_element_type=F32)
        result += jnp.dot(scaled_low, fields, preferred_element_type=F32)
        for y in range(ny):
            guess[x, pl.ds(y, 1), :] = result[0:1, y * deep : (y + 1) * deep]
            stepped[x, pl.ds(y, 1), :] = result[1:2, y * deep : (y + 1) * deep]


def finish(total, basis_stack, scaled_stack, block):
    return call(finish_kernel, (shape(*block),) * 2, [VM] * 3, limit=24)(
        total, basis_stack, scaled_stack
    )


def on_device(basis, rhs, extra_diag, coeff):
    odd = lax.axis_index("gx") % 2
    odd = odd.astype(jnp.int32).reshape(1)
    up_x, down_x, up_y, down_y = faces(basis, coeff)
    front, back = send(up_y, "gy", 1), send(down_y, "gy", -1)
    left, right = send(up_x, "gx", 1), send(down_x, "gx", -1)
    cols, inner, basis_stack = inside(basis, coeff, extra_diag)
    halo = (left, right, front, back)
    face_x, face_y = border(odd, cols, inner, coeff, extra_diag, rhs, halo)
    wide, deep = lax.axis_size("gx"), lax.axis_size("gy")
    route = []
    for i in range(wide):
        step = 1 if i % 2 else -1
        route += [(i * deep + j, i * deep + j + step) for j in range(deep) if 0 <= j + step < deep]
    far_y = lax.ppermute(face_y, ("gx", "gy"), route)
    far_x = send(face_x, "gx", -1)
    part, scaled_stack = local_sums(cols, inner, basis_stack, coeff, extra_diag, rhs, halo)
    part = shared_sums(odd, part, scaled_stack, coeff, front, far_x, far_y)
    total = sum_all(part)
    return finish(total, basis_stack, scaled_stack, rhs.shape)


def solution(mesh):
    placed = (
        P(None, "gx", "gy", None),
        P("gx", "gy", None),
        P("gx", "gy", None),
        P(None, "gx", "gy", None),
    )
    return jax.shard_map(
        on_device,
        mesh=mesh,
        in_specs=placed,
        out_specs=(P("gx", "gy", None), P("gx", "gy", None)),
        check_vma=False,
    )
```

time: 115 us -> 59.3 us (0.52)
  starting transfers between devices: 42.3 us -> 23.4 us
  other arithmetic: 17.1 us -> 0.02 us
  matrix products: 15.7 us -> 0 us
  Pallas kernels: 0 us -> 15.2 us
  waiting for transfers between devices: 27.6 us -> 16.1 us
  local copies, waits for them, and re-layouts: 9.05 us -> 3.36 us
  between operations: 2.98 us -> 0.81 us
    pallas_call x0 -> x6, Pallas kernels: none -> 15.2 us  [the longest x1 5.19 us: finish(): call(finish_kernel, (shape(*block),) * 2, [VM] * 3, limit=24)]
    dot_general x6 -> x0, matrix products: 14.5 us -> none  [the longest x1 2.89 us: on_device(): jnp.dot(flat_basis, applied.reshape(count, -1).T, precision=precise)]
    ppermute x10 -> x6, starting transfers between devices: 24.2 us -> 11.6 us  [the longest x5 10.3 us: send(): lax.ppermute(block, axis, [(i, i + step) for i in range(size) if 0 <= i +...]
    another operation x5 -> x0, other arithmetic: 6.69 us -> none  [the longest x3 3.6 us: small_solve(): lower = jnp.linalg.cholesky(matrix)]
    ppermute x14 -> x7, waiting for transfers between devices: 15.3 us -> 8.68 us  [sum_all(): lax.ppermute(part, ('gx', 'gy'), [(i * deep + j, (i ^ a) * deep + (j ^ b)...]
    ppermute x14 -> x7, starting transfers between devices: 18.1 us -> 11.8 us  [sum_all(): lax.ppermute(part, ('gx', 'gy'), [(i * deep + j, (i ^ a) * deep + (j ^ b)...]
    ppermute x10 -> x6, waiting for transfers between devices: 12.3 us -> 7.46 us  [the longest x1 3.89 us: on_device(): far_y = lax.ppermute(face_y, ('gx', 'gy'), route)]
    slice x10 -> x0, local copies, waits for them, and re-layouts: 4.51 us -> none  [the longest x2 2 us: flux_apply(): center[..., 1:]]
  transfers between devices with their start and end apart: 24 -> 13, of which waited for: 16 -> 8; matrix products, arithmetic and copies ran while one was open for 13% -> 0% of each run, Pallas kernels for 0% -> 12%
where the time goes in v2:
time: 59.3 us; the launch traced here: 58.9 us
  starting transfers between devices  23.4 us (39%)
  waiting for transfers between devices  16.1 us (27%)
  Pallas kernels  15.2 us (26%)
  local copies, waits for them, and re-layouts  3.36 us (6%)
  between operations  0.81 us (1%)
    ppermute x7, starting transfers between devices, sum_all(): lax.ppermute(part, ('gx', 'gy'), [(i * deep + j, (i ^ a) * deep + (j ^ b)...  11.8 us
    ppermute x5, starting transfers between devices, send(): lax.ppermute(block, axis, [(i, i + step) for i in range(size) if 0 <= i +...  10.3 us
    ppermute x7, waiting for transfers between devices, sum_all(): lax.ppermute(part, ('gx', 'gy'), [(i * deep + j, (i ^ a) * deep + (j ^ b)...  8.68 us
    pallas_call x1, Pallas kernels, finish(): call(finish_kernel, (shape(*block),) * 2, [VM] * 3, limit=24)  5.19 us
    ppermute x1, waiting for transfers between devices, on_device(): far_y = lax.ppermute(face_y, ('gx', 'gy'), route)  3.89 us
    pallas_call x1, Pallas kernels, inside(): call(inner_kernel, outs, [RAW, VM, VM], [small, small, small, sems], work...  3.83 us
    ppermute x5, waiting for transfers between devices, send(): lax.ppermute(block, axis, [(i, i + step) for i in range(size) if 0 <= i +...  3.57 us
    unnamed x14, local copies, waits for them, and re-layouts  3.36 us
  transfers between devices with their start and end apart: 13, of which 8 were waited for; matrix products, arithmetic and copies ran while one was open for 0% of the time, Pallas kernels for 12%

profile of v2, /device:TPU:0, one launch (start us, length us, event | category | flops | bytes accessed | tf_op | source)
XLA Modules:
  0.0 58.9 jit_solution(10419816851226599484)
XLA Ops:
  0.6 1.6 %copy-done = f32[32,8,8,256]{3,2,1,0:T(8,128)S(1)} copy-done((f32[32,8,8,256]{3,2,1,0:T(8,128)S(1)}, f32[32,8,8,256]{3,2,1,0:T(8,128)}, u32[]{:S(2)}) %copy-start) | copy-done | bytes 2097176
  2.2 0.9 %copy-done.2 = f32[3,8,8,256]{3,2,1,0:T(8,128)S(1)} copy-done((f32[3,8,8,256]{3,2,1,0:T(8,128)S(1)}, f32[3,8,8,256]{3,2,1,0:T(8,128)}, u32[]{:S(2)}) %copy-start.2) | copy-done | bytes 196632
  3.2 2.1 %shard_map.60 = (f32[264,256]{1,0:T(8,128)}, f32[256,256]{1,0:T(8,128)}, f32[264,256]{1,0:T(8,128)}, f32[256,256]{1,0:T(8,128)}) custom-call(f32[32,8,8,256]{3,2,1,0:T(8,128)S(1)} %copy-done, f32[3,8,8,256]{3,2,1,0:T(8,128)S(1)} %copy-done.2), custom_call_target="tpu_custom_call" | custom-call | tf_op jit(solution)/shard_map/pallas_call | solution.py:137
  5.3 5.0 %collective-permute-start.2 = (f32[264,256]{1,0:T(8,128)}, f32[264,256]{1,0:T(8,128)S(1)}, u32[]{:S(2)}, u32[]{:S(2)}) collective-permute-start(f32[264,256]{1,0:T(8,128)} %get-tuple-element.18), channel_id=1, source_target_pairs={{0,1},{1,2},{2,3},{4,5},{5,6},{6,7},{8,9},{9,10},{10,11},{12,13},{... | collective-permute-start | bytes 811016 | tf_op jit(solution)/shard_map/ppermute | solution.py:68
  10.3 1.5 %collective-permute-start = (f32[264,256]{1,0:T(8,128)}, f32[264,256]{1,0:T(8,128)S(1)}, u32[]{:S(2)}, u32[]{:S(2)}) collective-permute-start(f32[264,256]{1,0:T(8,128)} %get-tuple-element.16), channel_id=1, source_target_pairs={{0,4},{4,8},{8,12},{12,16},{16,20},{20,24},{24,28},{1,5},{5,9},{9,... | collective-permute-start | bytes 811016 | tf_op jit(solution)/shard_map/ppermute | solution.py:68
  11.8 1.3 %collective-permute-start.1 = (f32[256,256]{1,0:T(8,128)}, f32[256,256]{1,0:T(8,128)S(1)}, u32[]{:S(2)}, u32[]{:S(2)}) collective-permute-start(f32[256,256]{1,0:T(8,128)} %get-tuple-element.17), channel_id=1, source_target_pairs={{4,0},{8,4},{12,8},{16,12},{20,16},{24,20},{28,24},{5,1},{9,5},{13... | collective-permute-start | bytes 786440 | tf_op jit(solution)/shard_map/ppermute | solution.py:68
  13.1 1.3 %collective-permute-start.3 = (f32[256,256]{1,0:T(8,128)}, f32[256,256]{1,0:T(8,128)S(1)}, u32[]{:S(2)}, u32[]{:S(2)}) collective-permute-start(f32[256,256]{1,0:T(8,128)} %get-tuple-element.19), channel_id=1, source_target_pairs={{1,0},{2,1},{3,2},{5,4},{6,5},{7,6},{9,8},{10,9},{11,10},{13,12},{... | collective-permute-start | bytes 786440 | tf_op jit(solution)/shard_map/ppermute | solution.py:68
  14.4 0.8 %copy-done.4 = f32[8,8,256]{2,1,0:T(8,128)S(1)} copy-done((f32[8,8,256]{2,1,0:T(8,128)S(1)}, f32[8,8,256]{2,1,0:T(8,128)}, u32[]{:S(2)}) %copy-start.4) | copy-done | bytes 65560
  15.2 3.8 %shard_map.59 = (f32[8,8,32,256]{3,2,1,0:T(8,128)S(1)}, f32[8,8,32,256]{3,2,1,0:T(8,128)S(1)}, bf16[64,16384]{1,0:T(8,128)(2,1)S(1)}) custom-call(f32[32,8,8,256]{3,2,1,0:T(8,128)S(1)} %copy-done.1, f32[3,8,8,256]{3,2,1,0:T(8,128)S(1)} %copy-done.3, f32[8,8,256]{2,1,0:T(8,128)S(1)} %copy-done.4), custom_call_target="tpu_custom_call" | custom-call | flops 10485760 | bytes 8388608 | tf_op jit(solution)/shard_map/pallas_call | solution.py:196
  19.1 3.6 %collective-permute-done.3.back = f32[256,256]{1,0:T(8,128)S(1)} collective-permute-done((f32[256,256]{1,0:T(8,128)}, f32[256,256]{1,0:T(8,128)S(1)}, u32[]{:S(2)}, u32[]{:S(2)}) %collective-permute-start.3) | collective-permute-done | bytes 262176 | tf_op jit(solution)/shard_map/ppermute | solution.py:68
  22.9 1.3 %collective-permute-start.4 = (f32[264,256]{1,0:T(8,128)S(1)}, f32[264,256]{1,0:T(8,128)S(1)}, u32[]{:S(2)}, u32[]{:S(2)}) collective-permute-start(f32[264,256]{1,0:T(8,128)S(1)} %get-tuple-element.22), channel_id=1, source_target_pairs={{4,0},{8,4},{12,8},{16,12},{20,16},{24,20},{28,24},{5,1},{9,5},{13... | collective-permute-start | bytes 811016 | tf_op jit(solution)/shard_map/ppermute | solution.py:68
  24.2 1.3 %collective-permute-start.5 = (f32[264,256]{1,0:T(8,128)S(1)}, f32[264,256]{1,0:T(8,128)S(1)}, u32[]{:S(2)}, u32[]{:S(2)}) collective-permute-start(f32[264,256]{1,0:T(8,128)S(1)} %get-tuple-element.23), channel_id=1, source_target_pairs={{1,0},{2,1},{3,2},{4,5},{5,6},{6,7},{9,8},{10,9},{11,10},{12,13},{... | collective-permute-start | bytes 811016 | tf_op jit(solution)/shard_map/ppermute | solution.py:438
  25.5 3.1 %shard_map.61 = (f32[40,128]{1,0:T(8,128)S(1)}, bf16[80,16384]{1,0:T(8,128)(2,1)S(1)}) custom-call(f32[8,8,32,256]{3,2,1,0:T(8,128)S(1)} %get-tuple-element.13.cols, f32[8,8,32,256]{3,2,1,0:T(8,128)S(1)} %get-tuple-element.14.inner, bf16[64,16384]{1,0:T(8,128)(2,1)S(1)} %get-tuple-element.15.basis_stack, f32[3,8,8,256]{3,2,1,0:T(8,128)S(1)} %copy-done.3, ...), custom_call_target="tpu_custom_call" | custom-call | flops 31457280 | bytes 12582912 | tf_op jit(solution)/shard_map/pallas_call | solution.py:309
  28.6 3.9 %collective-permute-done.5.far_y = f32[264,256]{1,0:T(8,128)S(1)} collective-permute-done((f32[264,256]{1,0:T(8,128)S(1)}, f32[264,256]{1,0:T(8,128)S(1)}, u32[]{:S(2)}, u32[]{:S(2)}) %collective-permute-start.5) | collective-permute-done | bytes 270368 | tf_op jit(solution)/shard_map/ppermute | solution.py:438
  33.2 2.6 %collective-permute-start.6 = (f32[40,128]{1,0:T(8,128)S(1)}, f32[40,128]{1,0:T(8,128)S(1)}, u32[]{:S(2)}, u32[]{:S(2)}) collective-permute-start(f32[40,128]{1,0:T(8,128)S(1)} %shard_map.63), channel_id=1, source_target_pairs={{0,2},{1,3},{2,0},{3,1},{4,6},{5,7},{6,4},{7,5},{8,10},{9,11},{10,... | collective-permute-start | bytes 61448 | tf_op jit(solution)/shard_map/ppermute | solution.py:54
  35.8 2.1 %collective-permute-done.6 = f32[40,128]{1,0:T(8,128)S(1)} collective-permute-done((f32[40,128]{1,0:T(8,128)S(1)}, f32[40,128]{1,0:T(8,128)S(1)}, u32[]{:S(2)}, u32[]{:S(2)}) %collective-permute-start.6) | collective-permute-done | bytes 20512 | tf_op jit(solution)/shard_map/ppermute | solution.py:54
  38.2 5.3 %collective-permute-start.8 = (f32[40,128]{1,0:T(8,128)S(1)}, f32[40,128]{1,0:T(8,128)S(1)}, u32[]{:S(2)}, u32[]{:S(2)}) collective-permute-start(f32[40,128]{1,0:T(8,128)S(1)} %add.26), channel_id=1, source_target_pairs={{0,8},{1,9},{2,10},{3,11},{4,12},{5,13},{6,14},{7,15},{8,0},{9,1},... | collective-permute-start | bytes 61448 | tf_op jit(solution)/shard_map/ppermute | solution.py:54
  43.6 1.7 %collective-permute-done.8 = f32[40,128]{1,0:T(8,128)S(1)} collective-permute-done((f32[40,128]{1,0:T(8,128)S(1)}, f32[40,128]{1,0:T(8,128)S(1)}, u32[]{:S(2)}, u32[]{:S(2)}) %collective-permute-start.8) | collective-permute-done | bytes 20512 | tf_op jit(solution)/shard_map/ppermute | solution.py:54
  45.3 1.4 %collective-permute-done.9 = f32[40,128]{1,0:T(8,128)S(1)} collective-permute-done((f32[40,128]{1,0:T(8,128)S(1)}, f32[40,128]{1,0:T(8,128)S(1)}, u32[]{:S(2)}, u32[]{:S(2)}) %collective-permute-start.9) | collective-permute-done | bytes 20512 | tf_op jit(solution)/shard_map/ppermute | solution.py:54
  46.8 0.7 %collective-permute-start.10 = (f32[40,128]{1,0:T(8,128)S(1)}, f32[40,128]{1,0:T(8,128)S(1)}, u32[]{:S(2)}, u32[]{:S(2)}) collective-permute-start(f32[40,128]{1,0:T(8,128)S(1)} %add_add_fusion.1), channel_id=1, source_target_pairs={{0,16},{1,17},{2,18},{3,19},{4,20},{5,21},{6,22},{7,23},{8,24},{9,... | collective-permute-start | bytes 61448 | tf_op jit(solution)/shard_map/ppermute | solution.py:54
  47.5 1.6 %collective-permute-start.11 = (f32[40,128]{1,0:T(8,128)S(1)}, f32[40,128]{1,0:T(8,128)S(1)}, u32[]{:S(2)}, u32[]{:S(2)}) collective-permute-start(f32[40,128]{1,0:T(8,128)S(1)} %add_add_fusion.1), channel_id=1, source_target_pairs={{0,1},{1,0},{2,3},{3,2},{4,5},{5,4},{6,7},{7,6},{8,9},{9,8},{10,11... | collective-permute-start | bytes 61448 | tf_op jit(solution)/shard_map/ppermute | solution.py:54
  49.0 1.3 %collective-permute-start.12 = (f32[40,128]{1,0:T(8,128)S(1)}, f32[40,128]{1,0:T(8,128)S(1)}, u32[]{:S(2)}, u32[]{:S(2)}) collective-permute-start(f32[40,128]{1,0:T(8,128)S(1)} %add_add_fusion.1), channel_id=1, source_target_pairs={{0,17},{1,16},{2,19},{3,18},{4,21},{5,20},{6,23},{7,22},{8,25},{9,... | collective-permute-start | bytes 61448 | tf_op jit(solution)/shard_map/ppermute | solution.py:54
  51.3 2.5 %collective-permute-done.12 = f32[40,128]{1,0:T(8,128)S(1)} collective-permute-done((f32[40,128]{1,0:T(8,128)S(1)}, f32[40,128]{1,0:T(8,128)S(1)}, u32[]{:S(2)}, u32[]{:S(2)}) %collective-permute-start.12) | collective-permute-done | bytes 20512 | tf_op jit(solution)/shard_map/ppermute | solution.py:54
  53.7 5.2 %shard_map.64 = (f32[8,8,256]{2,1,0:T(8,128)}, f32[8,8,256]{2,1,0:T(8,128)}) custom-call(f32[40,128]{1,0:T(8,128)S(1)} %add_add_fusion.total, bf16[64,16384]{1,0:T(8,128)(2,1)S(1)} %get-tuple-element.15.basis_stack, bf16[80,16384]{1,0:T(8,128)(2,1)S(1)} %get-tuple-element.21.scaled_stack), custom_call_target="tpu_custom_call" | custom-call | tf_op jit(solution)/shard_map/pallas_call | solution.py:419
  (25 shorter events, 2.2 us)
Async XLA Ops:
  0.6 1.6 %copy-start = (f32[32,8,8,256]{3,2,1,0:T(8,128)S(1)}, f32[32,8,8,256]{3,2,1,0:T(8,128)}, u32[]{:S(2)}) copy-start(f32[32,8,8,256]{3,2,1,0:T(8,128)} %basis.3) | copy-start | bytes 6291460
  2.2 0.9 %copy-start.2 = (f32[3,8,8,256]{3,2,1,0:T(8,128)S(1)}, f32[3,8,8,256]{3,2,1,0:T(8,128)}, u32[]{:S(2)}) copy-start(f32[3,8,8,256]{3,2,1,0:T(8,128)} %coeff.9) | copy-start | bytes 589828
  3.1 11.2 %copy-start.1 = (f32[32,8,8,256]{3,2,1,0:T(8,128)S(1)}, f32[32,8,8,256]{3,2,1,0:T(8,128)}, u32[]{:S(2)}) copy-start(f32[32,8,8,256]{3,2,1,0:T(8,128)} %basis.3) | copy-start | bytes 6291460
  3.2 11.2 %copy-start.3 = (f32[3,8,8,256]{3,2,1,0:T(8,128)S(1)}, f32[3,8,8,256]{3,2,1,0:T(8,128)}, u32[]{:S(2)}) copy-start(f32[3,8,8,256]{3,2,1,0:T(8,128)} %coeff.9) | copy-start | bytes 589828
  5.3 17.4 %collective-permute-start.2 = (f32[264,256]{1,0:T(8,128)}, f32[264,256]{1,0:T(8,128)S(1)}, u32[]{:S(2)}, u32[]{:S(2)}) collective-permute-start(f32[264,256]{1,0:T(8,128)} %get-tuple-element.18), channel_id=1, source_target_pairs={{0,1},{1,2},{2,3},{4,5},{5,6},{6,7},{8,9},{9,10},{10,11},{12,13},{... | collective-permute-start | bytes 811016 | tf_op jit(solution)/shard_map/ppermute | solution.py:68
  10.3 12.4 %collective-permute-start = (f32[264,256]{1,0:T(8,128)}, f32[264,256]{1,0:T(8,128)S(1)}, u32[]{:S(2)}, u32[]{:S(2)}) collective-permute-start(f32[264,256]{1,0:T(8,128)} %get-tuple-element.16), channel_id=1, source_target_pairs={{0,4},{4,8},{8,12},{12,16},{16,20},{20,24},{24,28},{1,5},{5,9},{9,... | collective-permute-start | bytes 811016 | tf_op jit(solution)/shard_map/ppermute | solution.py:68
  11.8 7.3 %collective-permute-start.1 = (f32[256,256]{1,0:T(8,128)}, f32[256,256]{1,0:T(8,128)S(1)}, u32[]{:S(2)}, u32[]{:S(2)}) collective-permute-start(f32[256,256]{1,0:T(8,128)} %get-tuple-element.17), channel_id=1, source_target_pairs={{4,0},{8,4},{12,8},{16,12},{20,16},{24,20},{28,24},{5,1},{9,5},{13... | collective-permute-start | bytes 786440 | tf_op jit(solution)/shard_map/ppermute | solution.py:68
  13.1 9.6 %collective-permute-start.3 = (f32[256,256]{1,0:T(8,128)}, f32[256,256]{1,0:T(8,128)S(1)}, u32[]{:S(2)}, u32[]{:S(2)}) collective-permute-start(f32[256,256]{1,0:T(8,128)} %get-tuple-element.19), channel_id=1, source_target_pairs={{1,0},{2,1},{3,2},{5,4},{6,5},{7,6},{9,8},{10,9},{11,10},{13,12},{... | collective-permute-start | bytes 786440 | tf_op jit(solution)/shard_map/ppermute | solution.py:68
  14.4 0.8 %copy-start.4 = (f32[8,8,256]{2,1,0:T(8,128)S(1)}, f32[8,8,256]{2,1,0:T(8,128)}, u32[]{:S(2)}) copy-start(f32[8,8,256]{2,1,0:T(8,128)} %extra.5) | copy-start | bytes 196612
  15.2 7.4 %copy-start.6 = (f32[8,8,256]{2,1,0:T(8,128)S(1)}, f32[8,8,256]{2,1,0:T(8,128)}, u32[]{:S(2)}) copy-start(f32[8,8,256]{2,1,0:T(8,128)} %rhs.3) | copy-start | bytes 196612
  22.7 2.8 %copy-start.5 = (f32[8,8,256]{2,1,0:T(8,128)S(1)}, f32[8,8,256]{2,1,0:T(8,128)}, u32[]{:S(2)}) copy-start(f32[8,8,256]{2,1,0:T(8,128)} %extra.5) | copy-start | bytes 196612
  22.9 5.8 %collective-permute-start.4 = (f32[264,256]{1,0:T(8,128)S(1)}, f32[264,256]{1,0:T(8,128)S(1)}, u32[]{:S(2)}, u32[]{:S(2)}) collective-permute-start(f32[264,256]{1,0:T(8,128)S(1)} %get-tuple-element.22), channel_id=1, source_target_pairs={{4,0},{8,4},{12,8},{16,12},{20,16},{24,20},{28,24},{5,1},{9,5},{13... | collective-permute-start | bytes 811016 | tf_op jit(solution)/shard_map/ppermute | solution.py:68
  24.2 8.4 %collective-permute-start.5 = (f32[264,256]{1,0:T(8,128)S(1)}, f32[264,256]{1,0:T(8,128)S(1)}, u32[]{:S(2)}, u32[]{:S(2)}) collective-permute-start(f32[264,256]{1,0:T(8,128)S(1)} %get-tuple-element.23), channel_id=1, source_target_pairs={{1,0},{2,1},{3,2},{4,5},{5,6},{6,7},{9,8},{10,9},{11,10},{12,13},{... | collective-permute-start | bytes 811016 | tf_op jit(solution)/shard_map/ppermute | solution.py:438
  33.2 4.7 %collective-permute-start.6 = (f32[40,128]{1,0:T(8,128)S(1)}, f32[40,128]{1,0:T(8,128)S(1)}, u32[]{:S(2)}, u32[]{:S(2)}) collective-permute-start(f32[40,128]{1,0:T(8,128)S(1)} %shard_map.63), channel_id=1, source_target_pairs={{0,2},{1,3},{2,0},{3,1},{4,6},{5,7},{6,4},{7,5},{8,10},{9,11},{10,... | collective-permute-start | bytes 61448 | tf_op jit(solution)/shard_map/ppermute | solution.py:54
  37.9 5.6 %collective-permute-start.7 = (f32[40,128]{1,0:T(8,128)S(1)}, f32[40,128]{1,0:T(8,128)S(1)}, u32[]{:S(2)}, u32[]{:S(2)}) collective-permute-start(f32[40,128]{1,0:T(8,128)S(1)} %add.26), channel_id=1, source_target_pairs={{0,4},{1,5},{2,6},{3,7},{4,0},{5,1},{6,2},{7,3},{8,12},{9,13},{10,... | collective-permute-start | bytes 61448 | tf_op jit(solution)/shard_map/ppermute | solution.py:54
  38.2 7.1 %collective-permute-start.8 = (f32[40,128]{1,0:T(8,128)S(1)}, f32[40,128]{1,0:T(8,128)S(1)}, u32[]{:S(2)}, u32[]{:S(2)}) collective-permute-start(f32[40,128]{1,0:T(8,128)S(1)} %add.26), channel_id=1, source_target_pairs={{0,8},{1,9},{2,10},{3,11},{4,12},{5,13},{6,14},{7,15},{8,0},{9,1},... | collective-permute-start | bytes 61448 | tf_op jit(solution)/shard_map/ppermute | solution.py:54
  43.5 3.2 %collective-permute-start.9 = (f32[40,128]{1,0:T(8,128)S(1)}, f32[40,128]{1,0:T(8,128)S(1)}, u32[]{:S(2)}, u32[]{:S(2)}) collective-permute-start(f32[40,128]{1,0:T(8,128)S(1)} %add.26), channel_id=1, source_target_pairs={{0,12},{1,13},{2,14},{3,15},{4,8},{5,9},{6,10},{7,11},{8,4},{9,5},... | collective-permute-start | bytes 61448 | tf_op jit(solution)/shard_map/ppermute | solution.py:54
  46.8 3.8 %collective-permute-start.10 = (f32[40,128]{1,0:T(8,128)S(1)}, f32[40,128]{1,0:T(8,128)S(1)}, u32[]{:S(2)}, u32[]{:S(2)}) collective-permute-start(f32[40,128]{1,0:T(8,128)S(1)} %add_add_fusion.1), channel_id=1, source_target_pairs={{0,16},{1,17},{2,18},{3,19},{4,20},{5,21},{6,22},{7,23},{8,24},{9,... | collective-permute-start | bytes 61448 | tf_op jit(solution)/shard_map/ppermute | solution.py:54
  47.5 3.8 %collective-permute-start.11 = (f32[40,128]{1,0:T(8,128)S(1)}, f32[40,128]{1,0:T(8,128)S(1)}, u32[]{:S(2)}, u32[]{:S(2)}) collective-permute-start(f32[40,128]{1,0:T(8,128)S(1)} %add_add_fusion.1), channel_id=1, source_target_pairs={{0,1},{1,0},{2,3},{3,2},{4,5},{5,4},{6,7},{7,6},{8,9},{9,8},{10,11... | collective-permute-start | bytes 61448 | tf_op jit(solution)/shard_map/ppermute | solution.py:54
  49.0 4.7 %collective-permute-start.12 = (f32[40,128]{1,0:T(8,128)S(1)}, f32[40,128]{1,0:T(8,128)S(1)}, u32[]{:S(2)}, u32[]{:S(2)}) collective-permute-start(f32[40,128]{1,0:T(8,128)S(1)} %add_add_fusion.1), channel_id=1, source_target_pairs={{0,17},{1,16},{2,19},{3,18},{4,21},{5,20},{6,23},{7,22},{8,25},{9,... | collective-permute-start | bytes 61448 | tf_op jit(solution)/shard_map/ppermute | solution.py:54

commit v3 on v2

--- a/solution.py
+++ b/solution.py
@@ -68,6 +68,12 @@
     return lax.ppermute(block, axis, [(i, i + step) for i in range(size) if 0 <= i + step < size])
 
 
+def swap(block, axis, start):
+    size = lax.axis_size(axis)
+    pairs = [(i, i + 1) for i in range(start, size - 1, 2)]
+    return lax.ppermute(block, axis, pairs + [(j, i) for i, j in pairs])
+
+
 def halves(value):
     high = value.astype(BF16)
     return high, (value - high.astype(F32)).astype(BF16)
@@ -105,36 +111,46 @@
     return body, last
 
 
-def faces_kernel(basis, coeff, up_x, down_x, up_y, down_y, sems):
+def faces_kernel(odd, basis, coeff, first_x, second_x, first_y, second_y, sems):
     count, nx, ny, deep = basis.shape
+    first, second = (nx - 1) * (1 - odd[0]), (nx - 1) * odd[0]
     moves = []
+    for x in range(nx):
+        rows = pl.ds(x * count, count)
+        moves.append((basis.at[:, x, ny - 1, :], first_y.at[rows], basis.at[:, x, 0, :]))
+        moves.append((basis.at[:, x, 0, :], second_y.at[rows], basis.at[:, x, ny - 1, :]))
+    sided = len(moves)
     for y in range(ny):
         rows = pl.ds(y * count, count)
-        moves.append((basis.at[:, nx - 1, y, :], up_x.at[rows]))
-        moves.append((basis.at[:, 0, y, :], down_x.at[rows]))
-    for x in range(nx):
-        rows = pl.ds(x * count, count)
-        moves.append((basis.at[:, x, ny - 1, :], up_y.at[rows]))
-        moves.append((basis.at[:, x, 0, :], down_y.at[rows]))
-    moves.append((coeff.at[0, nx - 1], up_x.at[pl.ds(ny * count, ny)]))
-    moves.append((coeff.at[1, :, ny - 1, :], up_y.at[pl.ds(nx * count, nx)]))
-    copies = [pltpu.make_async_copy(a, b, sems.at[k]) for k, (a, b) in enumerate(moves)]
-    for copy in copies:
+        moves.append((basis.at[:, first, y, :], first_x.at[rows], None))
+        moves.append((basis.at[:, second, y, :], second_x.at[rows], None))
+    for target in (first_x, second_x):
+        moves.append((coeff.at[0, nx - 1], target.at[pl.ds(ny * count, ny)], None))
+    for target in (first_y, second_y):
+        moves.append((coeff.at[1, :, ny - 1, :], target.at[pl.ds(nx * count, nx)], None))
+
+    @pl.when(odd[1] == 0)
+    def _():
+        for k, (source, target, _) in enumerate(moves[:sided]):
+            pltpu.make_async_copy(source, target, sems.at[k]).start()
+
+    @pl.when(odd[1] == 1)
+    def _():
+        for k, (_, target, source) in enumerate(moves[:sided]):
+            pltpu.make_async_copy(source, target, sems.at[k]).start()
+
+    copies = [pltpu.make_async_copy(a, b, sems.at[k]) for k, (a, b, _) in enumerate(moves)]
+    for copy in copies[sided:]:
         copy.start()
     for copy in copies:
         copy.wait()
 
 
-def faces(basis, coeff):
+def faces(odd, basis, coeff):
     count, nx, ny, deep = basis.shape
-    outs = (
-        shape(ny * count + ny, deep),
-        shape(ny * count, deep),
-        shape(nx * count + nx, deep),
-        shape(nx * count, deep),
-    )
-    sems = pltpu.SemaphoreType.DMA((2 * nx + 2 * ny + 2,))
-    return call(faces_kernel, outs, [RAW, RAW], [sems], limit=4)(basis, coeff)
+    of_x, of_y = shape(ny * count + ny, deep), shape(nx * count + nx, deep)
+    sems = pltpu.SemaphoreType.DMA((2 * nx + 2 * ny + 4,))
+    return call(faces_kernel, (of_x, of_x, of_y, of_y), [SM, RAW, RAW], [sems], limit=60)(odd, basis, coeff)
 
 
 def row(ref, *at):
@@ -147,8 +163,10 @@
     return upper * above + lower * below
 
 
-def inner_kernel(basis, coeff, extra, cols, inner, stack, upper, lower, diag, sems):
-    nx, ny, count, deep = cols.shape
+def inner_kernel(basis, coeff, extra_raw, cols, inner, stack, diag, upper, lower, extra, sems):
+    nx, ny, count, deep = cols.shape
+    extra_copy = pltpu.make_async_copy(extra_raw, extra, sems.at[nx * ny])
+    extra_copy.start()
     copies = []
     for x in range(nx):
         for y in range(ny):
@@ -158,6 +176,7 @@
             copies[-1].start()
     level = lax.broadcasted_iota(jnp.int32, (ny, deep), 0)
     lane = lax.broadcasted_iota(jnp.int32, (ny, deep), 1)
+    extra_copy.wait()
     for x in range(nx):
         cz = coeff[2, x]
         upper[x] = jnp.where(lane == deep - 1, 0.0, cz)
@@ -169,9 +188,11 @@
         if x:
             total = total + coeff[0, x - 1]
         diag[x] = total
-    for copy in copies:
+    for copy in copies[:ny]:
         copy.wait()
     for x in range(nx):
+        for copy in copies[(x + 1) * ny : (x + 2) * ny]:
+            copy.wait()
         for y in range(ny):
             here = cols[x, y]
             sums = near_z(here, row(upper, x, y), row(lower, x, y))
@@ -190,48 +211,56 @@
 def inside(basis, coeff, extra):
     count, nx, ny, deep = basis.shape
     cells = nx * ny * deep
-    outs = (shape(nx, ny, count, deep), shape(nx, ny, count, deep), shape(2 * count, cells, dtype=BF16))
+    full = shape(nx, ny, count, deep)
+    outs = (full, full, shape(2 * count, cells, dtype=BF16), shape(nx, ny, deep))
     small = pltpu.VMEM((nx, ny, deep), F32)
-    sems = pltpu.SemaphoreType.DMA((nx * ny,))
+    sems = pltpu.SemaphoreType.DMA((nx * ny + 1,))
     return call(
-        inner_kernel, outs, [RAW, VM, VM], [small, small, small, sems],
+        inner_kernel, outs, [RAW, VM, RAW], [small, small, small, sems],
         work=20 * count * cells, moved=16 * count * cells,
     )(basis, coeff, extra)
 
 
-def inverse_diagonal(coeff, extra, from_left, from_front, count, x):
-    nx, ny, deep = extra.shape
+class Halo:
+    def __init__(self, odd, refs):
+        self.odd = odd
+        self.refs = refs
+
+    def rows(self, axis, upper, start, size):
+        first, second = self.refs[2 * axis : 2 * axis + 2]
+        here = pl.ds(start, size)
+        return jnp.where(self.odd[axis] == (0 if upper else 1), first[here, :], second[here, :])
+
+
+def inverse_diagonal(diag, halo, count, x):
+    nx, ny, deep = diag.shape
     level = lax.broadcasted_iota(jnp.int32, (ny, deep), 0)
-    lane = lax.broadcasted_iota(jnp.int32, (ny, deep), 1)
-    cy, cz = coeff[1, x], coeff[2, x]
-    total = extra[x] + coeff[0, x] + cy + cz
-    total += jnp.where(lane == 0, 0.0, pltpu.roll(cz, 1, 1))
-    front = from_front[pl.ds(nx * count + x, 1), :]
-    total += jnp.where(level == 0, front, pltpu.roll(cy, 1, 0))
-    total += coeff[0, x - 1] if x else from_left[pl.ds(ny * count, ny), :]
+    total = diag[x] + jnp.where(level == 0, halo.rows(1, False, nx * count + x, 1), 0.0)
+    if x == 0:
+        total += halo.rows(0, False, ny * count, ny)
     return 1.0 / total
 
 
-def full_value(cols, inner, coeff, left, right, front, back, x, y):
+def full_value(cols, inner, coeff, halo, x, y):
     nx, ny, count, deep = cols.shape
     value = inner[x, y]
-    of_x, of_y = pl.ds(y * count, count), pl.ds(x * count, count)
     if x == 0:
-        value += left[pl.ds(ny * count + y, 1), :] * (cols[x, y] - left[of_x])
+        value += halo.rows(0, False, ny * count + y, 1) * (cols[x, y] - halo.rows(0, False, y * count, count))
     if x == nx - 1:
-        value -= row(coeff, 0, x, y) * right[of_x]
+        value -= row(coeff, 0, x, y) * halo.rows(0, True, y * count, count)
     if y == 0:
-        value += front[pl.ds(nx * count + x, 1), :] * (cols[x, y] - front[of_y])
+        value += halo.rows(1, False, nx * count + x, 1) * (cols[x, y] - halo.rows(1, False, x * count, count))
     if y == ny - 1:
-        value -= row(coeff, 1, x, y) * back[of_y]
+        value -= row(coeff, 1, x, y) * halo.rows(1, True, x * count, count)
     return value
 
 
-def border_kernel(odd, cols, inner, coeff, extra, rhs, left, right, front, back, face_x, face_y, scale):
-    nx, ny, count, deep = cols.shape
-    for x in range(nx):
-        scale[x] = inverse_diagonal(coeff, extra, left, front, count, x)
-    value = functools.partial(full_value, cols, inner, coeff, left, right, front, back)
+def border_kernel(odd, cols, inner, coeff, diag, rhs, xa, xb, ya, yb, face_x, face_y, scale):
+    nx, ny, count, deep = cols.shape
+    halo = Halo(odd, (xa, xb, ya, yb))
+    for x in range(nx):
+        scale[x] = inverse_diagonal(diag, halo, count, x)
+    value = functools.partial(full_value, cols, inner, coeff, halo)
     for y in range(ny):
         face_x[pl.ds(y * count, count), :] = value(0, y) * row(scale, 0, y)
     face_x[pl.ds(ny * count, ny), :] = scale[0] * rhs[0]
@@ -250,28 +279,29 @@
         side(ny - 1)
 
 
-def border(odd, cols, inner, coeff, extra, rhs, halo):
+def border(odd, cols, inner, coeff, diag, rhs, halo):
     nx, ny, count, deep = cols.shape
     outs = (shape(ny * count + ny, deep), shape(nx * count + nx, deep))
     return call(
         border_kernel, outs, [SM] + [VM] * 9, [pltpu.VMEM((nx, ny, deep), F32)], limit=10
-    )(odd, cols, inner, coeff, extra, rhs, *halo)
+    )(odd, cols, inner, coeff, diag, rhs, *halo)
 
 
 def local_kernel(
-    cols, inner, basis_stack, coeff, extra, rhs, left, right, front, back,
+    odd, cols, inner, basis_stack, coeff, diag, rhs, xa, xb, ya, yb,
     part, scaled_stack, value_stack, pair_stack, scaled, scale, upper, scaled_rhs,
 ):
     nx, ny, count, deep = cols.shape
+    halo = Halo(odd, (xa, xb, ya, yb))
     lane = lax.broadcasted_iota(jnp.int32, (ny, deep), 1)
     for x in range(nx):
-        inverse = inverse_diagonal(coeff, extra, left, front, count, x)
+        inverse = inverse_diagonal(diag, halo, count, x)
         scale[x] = inverse
         scaled_rhs[x] = inverse * rhs[x]
         upper[x] = jnp.where(lane == deep - 1, 0.0, coeff[2, x])
     for x in range(nx):
         for y in range(ny):
-            value = full_value(cols, inner, coeff, left, right, front, back, x, y)
+            value = full_value(cols, inner, coeff, halo, x, y)
             result = value * row(scale, x, y)
             scaled[x, y] = result
             put(value_stack, x * ny + y, value, row(rhs, x, y))
@@ -300,7 +330,7 @@
     part[:, pl.ds(3 * count + 2, 1)] = pairs_rhs
 
 
-def local_sums(cols, inner, basis_stack, coeff, extra, rhs, halo):
+def local_sums(odd, cols, inner, basis_stack, coeff, diag, rhs, halo):
     nx, ny, count, deep = cols.shape
     cells = nx * ny * deep
     tall = 2 * count + EXTRA
@@ -309,7 +339,7 @@
     return call(
         local_kernel,
         outs,
-        [VM] * 10,
+        [SM] + [VM] * 10,
         [
             pltpu.VMEM((tall, cells), BF16),
             pltpu.VMEM((tall, cells), BF16),
@@ -319,10 +349,11 @@
         limit=28,
         work=60 * count * cells,
         moved=24 * count * cells,
-    )(cols, inner, basis_stack, coeff, extra, rhs, *halo)
-
-
-def shared_kernel(odd, part, scaled_stack, coeff, front, far_x, far_y, total, mine, pair_stack):
+    )(odd, cols, inner, basis_stack, coeff, diag, rhs, *halo)
+
+
+def shared_kernel(odd, part, scaled_stack, coeff, ya, yb, far_x, far_y, total, mine, pair_stack):
+    halo = Halo(odd, (None, None, ya, yb))
     count = part.shape[0] - 8
     nx, ny, deep = coeff.shape[1:]
     for y in range(ny):
@@ -333,7 +364,7 @@
         )
         mine[:, pl.ds(y * deep, deep)] = scaled_stack[:, pl.ds(((nx - 1) * ny + y) * deep, deep)]
     for x in range(nx):
-        own = front[pl.ds(nx * count + x, 1), :]
+        own = halo.rows(1, False, nx * count + x, 1)
         face = jnp.where(odd[0] == 0, row(coeff, 1, x, ny - 1), own)
         put(
             pair_stack, ny + x, face * far_y[pl.ds(x * count, count), :],
@@ -358,12 +389,12 @@
     total[:, pl.ds(3 * count + 2, 1)] += pairs_rhs
 
 
-def shared_sums(odd, part, scaled_stack, coeff, front, far_x, far_y):
+def shared_sums(odd, part, scaled_stack, coeff, ya, yb, far_x, far_y):
     nx, ny, deep = coeff.shape[1:]
     wide = pltpu.VMEM((scaled_stack.shape[0], (nx + ny) * deep), BF16)
     return call(
-        shared_kernel, shape(*part.shape), [SM] + [VM] * 6, [wide, wide], limit=12
-    )(odd, part, scaled_stack, coeff, front, far_x, far_y)
+        shared_kernel, shape(*part.shape), [SM] + [VM] * 7, [wide, wide], limit=12
+    )(odd, part, scaled_stack, coeff, ya, yb, far_x, far_y)
 
 
 def finish_kernel(total, basis_stack, scaled_stack, guess, stepped):
@@ -422,14 +453,13 @@
 
 
 def on_device(basis, rhs, extra_diag, coeff):
-    odd = lax.axis_index("gx") % 2
-    odd = odd.astype(jnp.int32).reshape(1)
-    up_x, down_x, up_y, down_y = faces(basis, coeff)
-    front, back = send(up_y, "gy", 1), send(down_y, "gy", -1)
-    left, right = send(up_x, "gx", 1), send(down_x, "gx", -1)
-    cols, inner, basis_stack = inside(basis, coeff, extra_diag)
-    halo = (left, right, front, back)
-    face_x, face_y = border(odd, cols, inner, coeff, extra_diag, rhs, halo)
+    odd = jnp.stack([lax.axis_index("gx") % 2, lax.axis_index("gy") % 2]).astype(jnp.int32)
+    first_x, second_x, first_y, second_y = faces(odd, basis, coeff)
+    first_y, second_y = swap(first_y, "gy", 0), swap(second_y, "gy", 1)
+    first_x, second_x = swap(first_x, "gx", 0), swap(second_x, "gx", 1)
+    cols, inner, basis_stack, diag = inside(basis, coeff, extra_diag)
+    halo = (first_x, second_x, first_y, second_y)
+    face_x, face_y = border(odd, cols, inner, coeff, diag, rhs, halo)
     wide, deep = lax.axis_size("gx"), lax.axis_size("gy")
     route = []
     for i in range(wide):
@@ -437,8 +467,8 @@
         route += [(i * deep + j, i * deep + j + step) for j in range(deep) if 0 <= j + step < deep]
     far_y = lax.ppermute(face_y, ("gx", "gy"), route)
     far_x = send(face_x, "gx", -1)
-    part, scaled_stack = local_sums(cols, inner, basis_stack, coeff, extra_diag, rhs, halo)
-    part = shared_sums(odd, part, scaled_stack, coeff, front, far_x, far_y)
+    part, scaled_stack = local_sums(odd, cols, inner, basis_stack, coeff, diag, rhs, halo)
+    part = shared_sums(odd, part, scaled_stack, coeff, first_y, second_y, far_x, far_y)
     total = sum_all(part)
     return finish(total, basis_stack, scaled_stack, rhs.shape)
 

time: 59.3 us -> 56.8 us (0.958)
  Pallas kernels: 15.2 us -> 18.7 us
  starting transfers between devices: 23.4 us -> 20 us
  local copies, waits for them, and re-layouts: 3.36 us -> 0.02 us
  other arithmetic: 0.02 us -> 0.63 us
    ppermute x5 -> x1, starting transfers between devices: 10.3 us -> 1.29 us  [send(): lax.ppermute(block, axis, [(i, i + step) for i in range(size) if 0 <= i +...]
    ppermute x0 -> x4, starting transfers between devices: none -> 4.54 us  [swap(): return lax.ppermute(block, axis, pairs + [(j, i) for i, j in pairs])]
    ppermute x5 -> x1, waiting for transfers between devices: 3.57 us -> 0.01 us  [send(): lax.ppermute(block, axis, [(i, i + step) for i in range(size) if 0 <= i +...]
    unnamed x14 -> x10, local copies, waits for them, and re-layouts: 3.36 us -> 0.02 us
    pallas_call x4, Pallas kernels: 9.78 us -> 12.8 us  [the longest x1 4.34 us: inside(): call(inner_kernel, outs, [RAW, VM, RAW], [small, small, small, sems], wor...]
    ppermute x1, waiting for transfers between devices: 3.89 us -> 6.65 us  [on_device(): far_y = lax.ppermute(face_y, ('gx', 'gy'), route)]
    ppermute x7, starting transfers between devices: 11.8 us -> 12.8 us  [sum_all(): lax.ppermute(part, ('gx', 'gy'), [(i * deep + j, (i ^ a) * deep + (j ^ b)...]
    ppermute x7, waiting for transfers between devices: 8.68 us -> 9.49 us  [sum_all(): lax.ppermute(part, ('gx', 'gy'), [(i * deep + j, (i ^ a) * deep + (j ^ b)...]
  transfers between devices with their start and end apart: 13 -> 13, of which waited for: 8 -> 8; matrix products, arithmetic and copies ran while one was open for 0% -> 0% of each run, Pallas kernels for 12% -> 14%
where the time goes in v3:
time: 56.8 us; the launch traced here: 56.5 us
  starting transfers between devices  20 us (35%)
  Pallas kernels  18.7 us (33%)
  waiting for transfers between devices  16.4 us (29%)
  between operations  0.8 us (1%)
  other arithmetic  0.63 us (1%)
    ppermute x7, starting transfers between devices, sum_all(): lax.ppermute(part, ('gx', 'gy'), [(i * deep + j, (i ^ a) * deep + (j ^ b)...  12.8 us
    ppermute x7, waiting for transfers between devices, sum_all(): lax.ppermute(part, ('gx', 'gy'), [(i * deep + j, (i ^ a) * deep + (j ^ b)...  9.49 us
    ppermute x1, waiting for transfers between devices, on_device(): far_y = lax.ppermute(face_y, ('gx', 'gy'), route)  6.65 us
    pallas_call x1, Pallas kernels, finish(): call(finish_kernel, (shape(*block),) * 2, [VM] * 3, limit=24)  5.19 us
    ppermute x4, starting transfers between devices, swap(): return lax.ppermute(block, axis, pairs + [(j, i) for i, j in pairs])  4.54 us
    pallas_call x1, Pallas kernels, inside(): call(inner_kernel, outs, [RAW, VM, RAW], [small, small, small, sems], wor...  4.34 us
    pallas_call x1, Pallas kernels, local_sums(): call(local_kernel, outs, [SM] + [VM] * 10, [pltpu.VMEM((tall, cells), BF1...  3.76 us
    pallas_call x1, Pallas kernels, faces(): call(faces_kernel, (of_x, of_x, of_y, of_y), [SM, RAW, RAW], [sems], limi...  3.47 us
  transfers between devices with their start and end apart: 13, of which 8 were waited for; matrix products, arithmetic and copies ran while one was open for 0% of the time, Pallas kernels for 14%

profile of v3, /device:TPU:0, one launch (start us, length us, event | category | flops | bytes accessed | tf_op | source)
XLA Modules:
  0.0 56.5 jit_solution(16293344989140674194)
XLA Ops:
  0.7 0.6 %pad_add_fusion.odd = s32[2]{0:T(128)} fusion(s32[1]{0:T(128)} %bitcast.1, s32[1]{0:T(128)} %bitcast), kind=kLoop, calls=%fused_computation.2 | loop fusion | flops 2 | bytes 16 | tf_op jit(solution)/shard_map/stack | solution.py:456
  1.3 3.5 %shard_map.60 = (f32[264,256]{1,0:T(8,128)}, f32[264,256]{1,0:T(8,128)}, f32[264,256]{1,0:T(8,128)}, f32[264,256]{1,0:T(8,128)}) custom-call(s32[2]{0:T(128)} %pad_add_fusion.odd, f32[32,8,8,256]{3,2,1,0:T(8,128)} %basis.3, f32[3,8,8,256]{3,2,1,0:T(8,128)} %coeff.9), custom_call_target="tpu_custom_call" | custom-call | tf_op jit(solution)/shard_map/pallas_call | solution.py:153
  4.8 0.6 collective-permute-start
  5.3 0.7 %collective-permute-start.1 = (f32[264,256]{1,0:T(8,128)}, f32[264,256]{1,0:T(8,128)S(1)}, u32[]{:S(2)}, u32[]{:S(2)}) collective-permute-start(f32[264,256]{1,0:T(8,128)} %get-tuple-element.19), channel_id=1, source_target_pairs={{4,8},{12,16},{20,24},{8,4},{16,12},{24,20},{5,9},{13,17},{21,25},... | collective-permute-start | bytes 811016 | tf_op jit(solution)/shard_map/ppermute | solution.py:74
  6.0 2.7 %collective-permute-start.2 = (f32[264,256]{1,0:T(8,128)}, f32[264,256]{1,0:T(8,128)S(1)}, u32[]{:S(2)}, u32[]{:S(2)}) collective-permute-start(f32[264,256]{1,0:T(8,128)} %get-tuple-element.20), channel_id=1, source_target_pairs={{0,1},{2,3},{1,0},{3,2},{4,5},{6,7},{5,4},{7,6},{8,9},{10,11},{9,8... | collective-permute-start | bytes 811016 | tf_op jit(solution)/shard_map/ppermute | solution.py:74
  8.7 0.7 %collective-permute-start.3 = (f32[264,256]{1,0:T(8,128)}, f32[264,256]{1,0:T(8,128)S(1)}, u32[]{:S(2)}, u32[]{:S(2)}) collective-permute-start(f32[264,256]{1,0:T(8,128)} %get-tuple-element.21), channel_id=1, source_target_pairs={{1,2},{2,1},{5,6},{6,5},{9,10},{10,9},{13,14},{14,13},{17,18},{18,... | collective-permute-start | bytes 811016 | tf_op jit(solution)/shard_map/ppermute | solution.py:74
  9.4 4.3 %shard_map.59 = (f32[8,8,32,256]{3,2,1,0:T(8,128)S(1)}, f32[8,8,32,256]{3,2,1,0:T(8,128)S(1)}, bf16[64,16384]{1,0:T(8,128)(2,1)S(1)}, f32[8,8,256]{2,1,0:T(8,128)S(1)}) custom-call(f32[32,8,8,256]{3,2,1,0:T(8,128)S(1)} %copy-done, f32[3,8,8,256]{3,2,1,0:T(8,128)S(1)} %copy-done.1, f32[8,8,256]{2,1,0:T(8,128)S(1)} %copy-done.3), custom_call_target="tpu_custom_call" | custom-call | flops 10485760 | bytes 8388608 | tf_op jit(solution)/shard_map/pallas_call | solution.py:218
  14.0 0.7 %shard_map.62 = (f32[264,256]{1,0:T(8,128)S(1)}, f32[264,256]{1,0:T(8,128)S(1)}) custom-call(s32[2]{0:T(128)S(1)} %copy-done.4, f32[8,8,32,256]{3,2,1,0:T(8,128)S(1)} %get-tuple-element.14.cols, f32[8,8,32,256]{3,2,1,0:T(8,128)S(1)} %get-tuple-element.15.inner, f32[3,8,8,256]{3,2,1,0:T(8,128)S(1)} %copy-done.1, f32[8,8,256]{2,1,0:T(8,128)S(1)} %get-tuple-element.17.diag, ...), custom_call_target="tpu_custom_call" | custom-call | tf_op jit(solution)/shard_map/pallas_call | solution.py:285
  14.7 1.3 %collective-permute-start.4 = (f32[264,256]{1,0:T(8,128)S(1)}, f32[264,256]{1,0:T(8,128)S(1)}, u32[]{:S(2)}, u32[]{:S(2)}) collective-permute-start(f32[264,256]{1,0:T(8,128)S(1)} %get-tuple-element.24), channel_id=1, source_target_pairs={{4,0},{8,4},{12,8},{16,12},{20,16},{24,20},{28,24},{5,1},{9,5},{13... | collective-permute-start | bytes 811016 | tf_op jit(solution)/shard_map/ppermute | solution.py:68
  16.0 1.3 %collective-permute-start.5 = (f32[264,256]{1,0:T(8,128)S(1)}, f32[264,256]{1,0:T(8,128)S(1)}, u32[]{:S(2)}, u32[]{:S(2)}) collective-permute-start(f32[264,256]{1,0:T(8,128)S(1)} %get-tuple-element.25), channel_id=1, source_target_pairs={{1,0},{2,1},{3,2},{4,5},{5,6},{6,7},{9,8},{10,9},{11,10},{12,13},{... | collective-permute-start | bytes 811016 | tf_op jit(solution)/shard_map/ppermute | solution.py:468
  17.3 3.8 %shard_map.61 = (f32[40,128]{1,0:T(8,128)S(1)}, bf16[80,16384]{1,0:T(8,128)(2,1)S(1)}) custom-call(s32[2]{0:T(128)S(1)} %copy-done.4, f32[8,8,32,256]{3,2,1,0:T(8,128)S(1)} %get-tuple-element.14.cols, f32[8,8,32,256]{3,2,1,0:T(8,128)S(1)} %get-tuple-element.15.inner, bf16[64,16384]{1,0:T(8,128)(2,1)S(1)} %get-tuple-element.16.basis_stack, ...), custom_call_target="tpu_custom_call" | custom-call | flops 31457280 | bytes 12582912 | tf_op jit(solution)/shard_map/pallas_call | solution.py:339
  21.1 6.7 %collective-permute-done.5.far_y = f32[264,256]{1,0:T(8,128)S(1)} collective-permute-done((f32[264,256]{1,0:T(8,128)S(1)}, f32[264,256]{1,0:T(8,128)S(1)}, u32[]{:S(2)}, u32[]{:S(2)}) %collective-permute-start.5) | collective-permute-done | bytes 270368 | tf_op jit(solution)/shard_map/ppermute | solution.py:468
  27.8 1.2 %shard_map.63 = f32[40,128]{1,0:T(8,128)S(1)} custom-call(s32[2]{0:T(128)S(1)} %copy-done.4, f32[40,128]{1,0:T(8,128)S(1)} %get-tuple-element.22.part, bf16[80,16384]{1,0:T(8,128)(2,1)S(1)} %get-tuple-element.23.scaled_stack, f32[3,8,8,256]{3,2,1,0:T(8,128)S(1)} %copy-done.1, f32[264,256]{1,0:T(8,128)S(1)} %collective-permute-done.2.ya, ...), custom_call_target="tpu_custom_call" | custom-call | tf_op jit(solution)/shard_map/pallas_call | solution.py:395
  29.0 3.8 %collective-permute-start.6 = (f32[40,128]{1,0:T(8,128)S(1)}, f32[40,128]{1,0:T(8,128)S(1)}, u32[]{:S(2)}, u32[]{:S(2)}) collective-permute-start(f32[40,128]{1,0:T(8,128)S(1)} %shard_map.63), channel_id=1, source_target_pairs={{0,2},{1,3},{2,0},{3,1},{4,6},{5,7},{6,4},{7,5},{8,10},{9,11},{10,... | collective-permute-start | bytes 61448 | tf_op jit(solution)/shard_map/ppermute | solution.py:54
  32.8 1.8 %collective-permute-done.6 = f32[40,128]{1,0:T(8,128)S(1)} collective-permute-done((f32[40,128]{1,0:T(8,128)S(1)}, f32[40,128]{1,0:T(8,128)S(1)}, u32[]{:S(2)}, u32[]{:S(2)}) %collective-permute-start.6) | collective-permute-done | bytes 20512 | tf_op jit(solution)/shard_map/ppermute | solution.py:54
  34.6 0.3 collective-permute-start.7
  34.9 5.1 %collective-permute-start.8 = (f32[40,128]{1,0:T(8,128)S(1)}, f32[40,128]{1,0:T(8,128)S(1)}, u32[]{:S(2)}, u32[]{:S(2)}) collective-permute-start(f32[40,128]{1,0:T(8,128)S(1)} %add.30), channel_id=1, source_target_pairs={{0,8},{1,9},{2,10},{3,11},{4,12},{5,13},{6,14},{7,15},{8,0},{9,1},... | collective-permute-start | bytes 61448 | tf_op jit(solution)/shard_map/ppermute | solution.py:54
  40.0 1.7 %collective-permute-done.8 = f32[40,128]{1,0:T(8,128)S(1)} collective-permute-done((f32[40,128]{1,0:T(8,128)S(1)}, f32[40,128]{1,0:T(8,128)S(1)}, u32[]{:S(2)}, u32[]{:S(2)}) %collective-permute-start.8) | collective-permute-done | bytes 20512 | tf_op jit(solution)/shard_map/ppermute | solution.py:54
  41.7 1.4 %collective-permute-done.9 = f32[40,128]{1,0:T(8,128)S(1)} collective-permute-done((f32[40,128]{1,0:T(8,128)S(1)}, f32[40,128]{1,0:T(8,128)S(1)}, u32[]{:S(2)}, u32[]{:S(2)}) %collective-permute-start.9) | collective-permute-done | bytes 20512 | tf_op jit(solution)/shard_map/ppermute | solution.py:54
  43.2 1.5 %collective-permute-start.10 = (f32[40,128]{1,0:T(8,128)S(1)}, f32[40,128]{1,0:T(8,128)S(1)}, u32[]{:S(2)}, u32[]{:S(2)}) collective-permute-start(f32[40,128]{1,0:T(8,128)S(1)} %add_add_fusion.1), channel_id=1, source_target_pairs={{0,16},{1,17},{2,18},{3,19},{4,20},{5,21},{6,22},{7,23},{8,24},{9,... | collective-permute-start | bytes 61448 | tf_op jit(solution)/shard_map/ppermute | solution.py:54
  44.7 2.0 %collective-permute-start.11 = (f32[40,128]{1,0:T(8,128)S(1)}, f32[40,128]{1,0:T(8,128)S(1)}, u32[]{:S(2)}, u32[]{:S(2)}) collective-permute-start(f32[40,128]{1,0:T(8,128)S(1)} %add_add_fusion.1), channel_id=1, source_target_pairs={{0,1},{1,0},{2,3},{3,2},{4,5},{5,4},{6,7},{7,6},{8,9},{9,8},{10,11... | collective-permute-start | bytes 61448 | tf_op jit(solution)/shard_map/ppermute | solution.py:54
  47.1 1.4 %collective-permute-done.11 = f32[40,128]{1,0:T(8,128)S(1)} collective-permute-done((f32[40,128]{1,0:T(8,128)S(1)}, f32[40,128]{1,0:T(8,128)S(1)}, u32[]{:S(2)}, u32[]{:S(2)}) %collective-permute-start.11) | collective-permute-done | bytes 20512 | tf_op jit(solution)/shard_map/ppermute | solution.py:54
  48.4 2.9 %collective-permute-done.12 = f32[40,128]{1,0:T(8,128)S(1)} collective-permute-done((f32[40,128]{1,0:T(8,128)S(1)}, f32[40,128]{1,0:T(8,128)S(1)}, u32[]{:S(2)}, u32[]{:S(2)}) %collective-permute-start.12) | collective-permute-done | bytes 20512 | tf_op jit(solution)/shard_map/ppermute | solution.py:54
  51.3 5.2 %shard_map.64 = (f32[8,8,256]{2,1,0:T(8,128)}, f32[8,8,256]{2,1,0:T(8,128)}) custom-call(f32[40,128]{1,0:T(8,128)S(1)} %add_add_fusion.total, bf16[64,16384]{1,0:T(8,128)(2,1)S(1)} %get-tuple-element.16.basis_stack, bf16[80,16384]{1,0:T(8,128)(2,1)S(1)} %get-tuple-element.23.scaled_stack), custom_call_target="tpu_custom_call" | custom-call | tf_op jit(solution)/shard_map/pallas_call | solution.py:450
  (22 shorter events, 0.8 us)
Async XLA Ops:
  0.6 8.7 %copy-start = (f32[32,8,8,256]{3,2,1,0:T(8,128)S(1)}, f32[32,8,8,256]{3,2,1,0:T(8,128)}, u32[]{:S(2)}) copy-start(f32[32,8,8,256]{3,2,1,0:T(8,128)} %basis.3) | copy-start | bytes 6291460
  0.6 8.7 %copy-start.1 = (f32[3,8,8,256]{3,2,1,0:T(8,128)S(1)}, f32[3,8,8,256]{3,2,1,0:T(8,128)}, u32[]{:S(2)}) copy-start(f32[3,8,8,256]{3,2,1,0:T(8,128)} %coeff.9) | copy-start | bytes 589828
  0.7 8.7 %copy-start.3 = (f32[8,8,256]{2,1,0:T(8,128)S(1)}, f32[8,8,256]{2,1,0:T(8,128)}, u32[]{:S(2)}) copy-start(f32[8,8,256]{2,1,0:T(8,128)} %extra_raw.1) | copy-start | bytes 196612
  1.3 12.7 %copy-start.2 = (f32[8,8,256]{2,1,0:T(8,128)S(1)}, f32[8,8,256]{2,1,0:T(8,128)}, u32[]{:S(2)}) copy-start(f32[8,8,256]{2,1,0:T(8,128)} %rhs.3) | copy-start | bytes 196612
  1.3 12.7 %copy-start.4 = (s32[2]{0:T(128)S(1)}, s32[2]{0:T(128)}, u32[]{:S(2)}) copy-start(s32[2]{0:T(128)} %pad_add_fusion.odd) | copy-start | bytes 28
  4.8 8.9 %collective-permute-start = (f32[264,256]{1,0:T(8,128)}, f32[264,256]{1,0:T(8,128)S(1)}, u32[]{:S(2)}, u32[]{:S(2)}) collective-permute-start(f32[264,256]{1,0:T(8,128)} %get-tuple-element.18), channel_id=1, source_target_pairs={{0,4},{8,12},{16,20},{24,28},{4,0},{12,8},{20,16},{28,24},{1,5},{9... | collective-permute-start | bytes 811016 | tf_op jit(solution)/shard_map/ppermute | solution.py:74
  5.3 8.4 %collective-permute-start.1 = (f32[264,256]{1,0:T(8,128)}, f32[264,256]{1,0:T(8,128)S(1)}, u32[]{:S(2)}, u32[]{:S(2)}) collective-permute-start(f32[264,256]{1,0:T(8,128)} %get-tuple-element.19), channel_id=1, source_target_pairs={{4,8},{12,16},{20,24},{8,4},{16,12},{24,20},{5,9},{13,17},{21,25},... | collective-permute-start | bytes 811016 | tf_op jit(solution)/shard_map/ppermute | solution.py:74
  6.0 8.0 %collective-permute-start.2 = (f32[264,256]{1,0:T(8,128)}, f32[264,256]{1,0:T(8,128)S(1)}, u32[]{:S(2)}, u32[]{:S(2)}) collective-permute-start(f32[264,256]{1,0:T(8,128)} %get-tuple-element.20), channel_id=1, source_target_pairs={{0,1},{2,3},{1,0},{3,2},{4,5},{6,7},{5,4},{7,6},{8,9},{10,11},{9,8... | collective-permute-start | bytes 811016 | tf_op jit(solution)/shard_map/ppermute | solution.py:74
  8.7 5.3 %collective-permute-start.3 = (f32[264,256]{1,0:T(8,128)}, f32[264,256]{1,0:T(8,128)S(1)}, u32[]{:S(2)}, u32[]{:S(2)}) collective-permute-start(f32[264,256]{1,0:T(8,128)} %get-tuple-element.21), channel_id=1, source_target_pairs={{1,2},{2,1},{5,6},{6,5},{9,10},{10,9},{13,14},{14,13},{17,18},{18,... | collective-permute-start | bytes 811016 | tf_op jit(solution)/shard_map/ppermute | solution.py:74
  14.7 6.4 %collective-permute-start.4 = (f32[264,256]{1,0:T(8,128)S(1)}, f32[264,256]{1,0:T(8,128)S(1)}, u32[]{:S(2)}, u32[]{:S(2)}) collective-permute-start(f32[264,256]{1,0:T(8,128)S(1)} %get-tuple-element.24), channel_id=1, source_target_pairs={{4,0},{8,4},{12,8},{16,12},{20,16},{24,20},{28,24},{5,1},{9,5},{13... | collective-permute-start | bytes 811016 | tf_op jit(solution)/shard_map/ppermute | solution.py:68
  16.0 11.7 %collective-permute-start.5 = (f32[264,256]{1,0:T(8,128)S(1)}, f32[264,256]{1,0:T(8,128)S(1)}, u32[]{:S(2)}, u32[]{:S(2)}) collective-permute-start(f32[264,256]{1,0:T(8,128)S(1)} %get-tuple-element.25), channel_id=1, source_target_pairs={{1,0},{2,1},{3,2},{4,5},{5,6},{6,7},{9,8},{10,9},{11,10},{12,13},{... | collective-permute-start | bytes 811016 | tf_op jit(solution)/shard_map/ppermute | solution.py:468
  29.0 5.6 %collective-permute-start.6 = (f32[40,128]{1,0:T(8,128)S(1)}, f32[40,128]{1,0:T(8,128)S(1)}, u32[]{:S(2)}, u32[]{:S(2)}) collective-permute-start(f32[40,128]{1,0:T(8,128)S(1)} %shard_map.63), channel_id=1, source_target_pairs={{0,2},{1,3},{2,0},{3,1},{4,6},{5,7},{6,4},{7,5},{8,10},{9,11},{10,... | collective-permute-start | bytes 61448 | tf_op jit(solution)/shard_map/ppermute | solution.py:54
  34.6 5.5 %collective-permute-start.7 = (f32[40,128]{1,0:T(8,128)S(1)}, f32[40,128]{1,0:T(8,128)S(1)}, u32[]{:S(2)}, u32[]{:S(2)}) collective-permute-start(f32[40,128]{1,0:T(8,128)S(1)} %add.30), channel_id=1, source_target_pairs={{0,4},{1,5},{2,6},{3,7},{4,0},{5,1},{6,2},{7,3},{8,12},{9,13},{10,... | collective-permute-start | bytes 61448 | tf_op jit(solution)/shard_map/ppermute | solution.py:54
  34.9 6.9 %collective-permute-start.8 = (f32[40,128]{1,0:T(8,128)S(1)}, f32[40,128]{1,0:T(8,128)S(1)}, u32[]{:S(2)}, u32[]{:S(2)}) collective-permute-start(f32[40,128]{1,0:T(8,128)S(1)} %add.30), channel_id=1, source_target_pairs={{0,8},{1,9},{2,10},{3,11},{4,12},{5,13},{6,14},{7,15},{8,0},{9,1},... | collective-permute-start | bytes 61448 | tf_op jit(solution)/shard_map/ppermute | solution.py:54
  40.0 3.2 %collective-permute-start.9 = (f32[40,128]{1,0:T(8,128)S(1)}, f32[40,128]{1,0:T(8,128)S(1)}, u32[]{:S(2)}, u32[]{:S(2)}) collective-permute-start(f32[40,128]{1,0:T(8,128)S(1)} %add.30), channel_id=1, source_target_pairs={{0,12},{1,13},{2,14},{3,15},{4,8},{5,9},{6,10},{7,11},{8,4},{9,5},... | collective-permute-start | bytes 61448 | tf_op jit(solution)/shard_map/ppermute | solution.py:54
  43.2 3.8 %collective-permute-start.10 = (f32[40,128]{1,0:T(8,128)S(1)}, f32[40,128]{1,0:T(8,128)S(1)}, u32[]{:S(2)}, u32[]{:S(2)}) collective-permute-start(f32[40,128]{1,0:T(8,128)S(1)} %add_add_fusion.1), channel_id=1, source_target_pairs={{0,16},{1,17},{2,18},{3,19},{4,20},{5,21},{6,22},{7,23},{8,24},{9,... | collective-permute-start | bytes 61448 | tf_op jit(solution)/shard_map/ppermute | solution.py:54
  44.7 3.8 %collective-permute-start.11 = (f32[40,128]{1,0:T(8,128)S(1)}, f32[40,128]{1,0:T(8,128)S(1)}, u32[]{:S(2)}, u32[]{:S(2)}) collective-permute-start(f32[40,128]{1,0:T(8,128)S(1)} %add_add_fusion.1), channel_id=1, source_target_pairs={{0,1},{1,0},{2,3},{3,2},{4,5},{5,4},{6,7},{7,6},{8,9},{9,8},{10,11... | collective-permute-start | bytes 61448 | tf_op jit(solution)/shard_map/ppermute | solution.py:54
  46.6 4.7 %collective-permute-start.12 = (f32[40,128]{1,0:T(8,128)S(1)}, f32[40,128]{1,0:T(8,128)S(1)}, u32[]{:S(2)}, u32[]{:S(2)}) collective-permute-start(f32[40,128]{1,0:T(8,128)S(1)} %add_add_fusion.1), channel_id=1, source_target_pairs={{0,17},{1,16},{2,19},{3,18},{4,21},{5,20},{6,23},{7,22},{8,25},{9,... | collective-permute-start | bytes 61448 | tf_op jit(solution)/shard_map/ppermute | solution.py:54

commit v4 on v3

--- a/solution.py
+++ b/solution.py
@@ -12,7 +12,6 @@
 LANES = 128
 VM = pl.BlockSpec(memory_space=pltpu.VMEM)
 RAW = pl.BlockSpec(memory_space=pl.ANY)
-SM = pl.BlockSpec(memory_space=pltpu.SMEM)
 
 
 def shape(*dims, dtype=F32):
@@ -81,7 +80,7 @@
 
 def put(stack, at, value, extra=None):
     count, deep = value.shape
-    lanes = pl.ds(at * deep, deep)
+    lanes = pl.ds(at * deep if isinstance(at, int) else pl.multiple_of(at * deep, deep), deep)
     high, low = halves(value)
     stack[pl.ds(0, count), lanes] = high
     stack[pl.ds(count, count), lanes] = low
@@ -111,46 +110,44 @@
     return body, last
 
 
-def faces_kernel(odd, basis, coeff, first_x, second_x, first_y, second_y, sems):
+def parity():
+    return lax.axis_index("gx") % 2, lax.axis_index("gy") % 2
+
+
+def faces_kernel(basis, coeff, first_x, second_x, first_y, second_y, cols, slabs, sems):
     count, nx, ny, deep = basis.shape
-    first, second = (nx - 1) * (1 - odd[0]), (nx - 1) * odd[0]
-    moves = []
-    for x in range(nx):
+    odd = parity()
+    copies = [pltpu.make_async_copy(basis.at[:, x], slabs.at[x], sems.at[x]) for x in range(nx)]
+    ends = []
+    for k, target in enumerate((first_x, second_x)):
+        ends.append((coeff.at[0, nx - 1], target.at[pl.ds(ny * count, ny)]))
+    for k, target in enumerate((first_y, second_y)):
+        ends.append((coeff.at[1, :, ny - 1, :], target.at[pl.ds(nx * count, nx)]))
+    ends = [pltpu.make_async_copy(a, b, sems.at[nx + k]) for k, (a, b) in enumerate(ends)]
+    for copy in copies + ends:
+        copy.start()
+    for x in range(nx):
+        copies[x].wait()
+        slab = jnp.swapaxes(slabs[x], 0, 1)
+        cols[x] = slab
         rows = pl.ds(x * count, count)
-        moves.append((basis.at[:, x, ny - 1, :], first_y.at[rows], basis.at[:, x, 0, :]))
-        moves.append((basis.at[:, x, 0, :], second_y.at[rows], basis.at[:, x, ny - 1, :]))
-    sided = len(moves)
+        first_y[rows, :] = jnp.where(odd[1] == 0, slab[ny - 1], slab[0])
+        second_y[rows, :] = jnp.where(odd[1] == 0, slab[0], slab[ny - 1])
     for y in range(ny):
         rows = pl.ds(y * count, count)
-        moves.append((basis.at[:, first, y, :], first_x.at[rows], None))
-        moves.append((basis.at[:, second, y, :], second_x.at[rows], None))
-    for target in (first_x, second_x):
-        moves.append((coeff.at[0, nx - 1], target.at[pl.ds(ny * count, ny)], None))
-    for target in (first_y, second_y):
-        moves.append((coeff.at[1, :, ny - 1, :], target.at[pl.ds(nx * count, nx)], None))
-
-    @pl.when(odd[1] == 0)
-    def _():
-        for k, (source, target, _) in enumerate(moves[:sided]):
-            pltpu.make_async_copy(source, target, sems.at[k]).start()
-
-    @pl.when(odd[1] == 1)
-    def _():
-        for k, (_, target, source) in enumerate(moves[:sided]):
-            pltpu.make_async_copy(source, target, sems.at[k]).start()
-
-    copies = [pltpu.make_async_copy(a, b, sems.at[k]) for k, (a, b, _) in enumerate(moves)]
-    for copy in copies[sided:]:
-        copy.start()
-    for copy in copies:
+        first_x[rows, :] = jnp.where(odd[0] == 0, cols[nx - 1, y], cols[0, y])
+        second_x[rows, :] = jnp.where(odd[0] == 0, cols[0, y], cols[nx - 1, y])
+    for copy in ends:
         copy.wait()
 
 
-def faces(odd, basis, coeff):
+def faces(basis, coeff):
     count, nx, ny, deep = basis.shape
     of_x, of_y = shape(ny * count + ny, deep), shape(nx * count + nx, deep)
-    sems = pltpu.SemaphoreType.DMA((2 * nx + 2 * ny + 4,))
-    return call(faces_kernel, (of_x, of_x, of_y, of_y), [SM, RAW, RAW], [sems], limit=60)(odd, basis, coeff)
+    outs = (of_x, of_x, of_y, of_y, shape(nx, ny, count, deep))
+    slabs = pltpu.VMEM((nx, count, ny, deep), F32)
+    sems = pltpu.SemaphoreType.DMA((nx + 4,))
+    return call(faces_kernel, outs, [RAW, RAW], [slabs, sems], limit=40)(basis, coeff)
 
 
 def row(ref, *at):
@@ -163,62 +160,51 @@
     return upper * above + lower * below
 
 
-def inner_kernel(basis, coeff, extra_raw, cols, inner, stack, diag, upper, lower, extra, sems):
-    nx, ny, count, deep = cols.shape
-    extra_copy = pltpu.make_async_copy(extra_raw, extra, sems.at[nx * ny])
+def inner_kernel(cols, coeff, extra_raw, inner, stack, diag, upper, lower, ahead, behind, extra, sem):
+    nx, ny, count, deep = cols.shape
+    extra_copy = pltpu.make_async_copy(extra_raw, extra, sem)
     extra_copy.start()
-    copies = []
-    for x in range(nx):
-        for y in range(ny):
-            copies.append(
-                pltpu.make_async_copy(basis.at[:, x, y, :], cols.at[x, y], sems.at[x * ny + y])
-            )
-            copies[-1].start()
     level = lax.broadcasted_iota(jnp.int32, (ny, deep), 0)
     lane = lax.broadcasted_iota(jnp.int32, (ny, deep), 1)
     extra_copy.wait()
     for x in range(nx):
-        cz = coeff[2, x]
+        cx, cy, cz = coeff[0, x], coeff[1, x], coeff[2, x]
         upper[x] = jnp.where(lane == deep - 1, 0.0, cz)
         under = jnp.where(lane == 0, 0.0, pltpu.roll(cz, 1, 1))
         lower[x] = under
-        cy = coeff[1, x]
-        total = extra[x] + coeff[0, x] + cy + cz + under
-        total = total + jnp.where(level == 0, 0.0, pltpu.roll(cy, 1, 0))
-        if x:
-            total = total + coeff[0, x - 1]
-        diag[x] = total
-    for copy in copies[:ny]:
-        copy.wait()
-    for x in range(nx):
-        for copy in copies[(x + 1) * ny : (x + 2) * ny]:
-            copy.wait()
+        before = coeff[0, x - 1] if x else jnp.zeros_like(cx)
+        behind[x] = before
+        ahead[x] = cx if x + 1 < nx else jnp.zeros_like(cx)
+        total = extra[x] + cx + cy + cz + under + before
+        diag[x] = total + jnp.where(level == 0, 0.0, pltpu.roll(cy, 1, 0))
+
+    def slab(x, carry):
+        after, before = jnp.minimum(x + 1, nx - 1), jnp.maximum(x - 1, 0)
         for y in range(ny):
             here = cols[x, y]
             sums = near_z(here, row(upper, x, y), row(lower, x, y))
-            if x + 1 < nx:
-                sums += row(coeff, 0, x, y) * cols[x + 1, y]
-            if x:
-                sums += row(coeff, 0, x - 1, y) * cols[x - 1, y]
+            sums += row(ahead, x, y) * cols[after, y]
+            sums += row(behind, x, y) * cols[before, y]
             if y + 1 < ny:
                 sums += row(coeff, 1, x, y) * cols[x, y + 1]
             if y:
                 sums += row(coeff, 1, x, y - 1) * cols[x, y - 1]
             inner[x, y] = row(diag, x, y) * here - sums
             put(stack, x * ny + y, here)
-
-
-def inside(basis, coeff, extra):
-    count, nx, ny, deep = basis.shape
+        return carry
+
+    lax.fori_loop(0, nx, slab, 0)
+
+
+def inside(cols, coeff, extra):
+    nx, ny, count, deep = cols.shape
     cells = nx * ny * deep
-    full = shape(nx, ny, count, deep)
-    outs = (full, full, shape(2 * count, cells, dtype=BF16), shape(nx, ny, deep))
+    outs = (shape(nx, ny, count, deep), shape(2 * count, cells, dtype=BF16), shape(nx, ny, deep))
     small = pltpu.VMEM((nx, ny, deep), F32)
-    sems = pltpu.SemaphoreType.DMA((nx * ny + 1,))
     return call(
-        inner_kernel, outs, [RAW, VM, RAW], [small, small, small, sems],
+        inner_kernel, outs, [VM, VM, RAW], [small] * 5 + [pltpu.SemaphoreType.DMA],
         work=20 * count * cells, moved=16 * count * cells,
-    )(basis, coeff, extra)
+    )(cols, coeff, extra)
 
 
 class Halo:
@@ -255,8 +241,9 @@
     return value
 
 
-def border_kernel(odd, cols, inner, coeff, diag, rhs, xa, xb, ya, yb, face_x, face_y, scale):
-    nx, ny, count, deep = cols.shape
+def border_kernel(cols, inner, coeff, diag, rhs, xa, xb, ya, yb, face_x, face_y, scale):
+    nx, ny, count, deep = cols.shape
+    odd = parity()
     halo = Halo(odd, (xa, xb, ya, yb))
     for x in range(nx):
         scale[x] = inverse_diagonal(diag, halo, count, x)
@@ -279,19 +266,20 @@
         side(ny - 1)
 
 
-def border(odd, cols, inner, coeff, diag, rhs, halo):
+def border(cols, inner, coeff, diag, rhs, halo):
     nx, ny, count, deep = cols.shape
     outs = (shape(ny * count + ny, deep), shape(nx * count + nx, deep))
     return call(
-        border_kernel, outs, [SM] + [VM] * 9, [pltpu.VMEM((nx, ny, deep), F32)], limit=10
-    )(odd, cols, inner, coeff, diag, rhs, *halo)
+        border_kernel, outs, [VM] * 9, [pltpu.VMEM((nx, ny, deep), F32)], limit=10
+    )(cols, inner, coeff, diag, rhs, *halo)
 
 
 def local_kernel(
-    odd, cols, inner, basis_stack, coeff, diag, rhs, xa, xb, ya, yb,
+    cols, inner, basis_stack, coeff, diag, rhs, xa, xb, ya, yb,
     part, scaled_stack, value_stack, pair_stack, scaled, scale, upper, scaled_rhs,
 ):
     nx, ny, count, deep = cols.shape
+    odd = parity()
     halo = Halo(odd, (xa, xb, ya, yb))
     lane = lax.broadcasted_iota(jnp.int32, (ny, deep), 1)
     for x in range(nx):
@@ -330,7 +318,7 @@
     part[:, pl.ds(3 * count + 2, 1)] = pairs_rhs
 
 
-def local_sums(odd, cols, inner, basis_stack, coeff, diag, rhs, halo):
+def local_sums(cols, inner, basis_stack, coeff, diag, rhs, halo):
     nx, ny, count, deep = cols.shape
     cells = nx * ny * deep
     tall = 2 * count + EXTRA
@@ -339,7 +327,7 @@
     return call(
         local_kernel,
         outs,
-        [SM] + [VM] * 10,
+        [VM] * 10,
         [
             pltpu.VMEM((tall, cells), BF16),
             pltpu.VMEM((tall, cells), BF16),
@@ -349,10 +337,11 @@
         limit=28,
         work=60 * count * cells,
         moved=24 * count * cells,
-    )(odd, cols, inner, basis_stack, coeff, diag, rhs, *halo)
-
-
-def shared_kernel(odd, part, scaled_stack, coeff, ya, yb, far_x, far_y, total, mine, pair_stack):
+    )(cols, inner, basis_stack, coeff, diag, rhs, *halo)
+
+
+def shared_kernel(part, scaled_stack, coeff, ya, yb, far_x, far_y, total, mine, pair_stack):
+    odd = parity()
     halo = Halo(odd, (None, None, ya, yb))
     count = part.shape[0] - 8
     nx, ny, deep = coeff.shape[1:]
@@ -389,25 +378,56 @@
     total[:, pl.ds(3 * count + 2, 1)] += pairs_rhs
 
 
-def shared_sums(odd, part, scaled_stack, coeff, ya, yb, far_x, far_y):
+def shared_sums(part, scaled_stack, coeff, ya, yb, far_x, far_y):
     nx, ny, deep = coeff.shape[1:]
     wide = pltpu.VMEM((scaled_stack.shape[0], (nx + ny) * deep), BF16)
     return call(
-        shared_kernel, shape(*part.shape), [SM] + [VM] * 7, [wide, wide], limit=12
-    )(odd, part, scaled_stack, coeff, ya, yb, far_x, far_y)
+        shared_kernel, shape(*part.shape), [VM] * 7, [wide, wide], limit=12
+    )(part, scaled_stack, coeff, ya, yb, far_x, far_y)
+
+
+def inverse_two(a, b, c, d):
+    scale = 1.0 / (a * d - b * c)
+    return d * scale, -b * scale, -c * scale, a * scale
+
+
+def apply_two(matrix, first, second):
+    a, b, c, d = matrix
+    return a * first + b * second, c * first + d * second
 
 
 def finish_kernel(total, basis_stack, scaled_stack, guess, stepped):
     count = total.shape[0] - 8
     nx, ny, deep = guess.shape
     sums = total[pl.ds(0, count), :]
-    work = sums
     level = lax.broadcasted_iota(jnp.int32, (count, 1), 0)
-    for k in range(count):
-        line = work[k : k + 1, :] / work[k : k + 1, k : k + 1]
-        column = work[:, k : k + 1]
-        work = jnp.where(level == k, line, work - column * line)
+    lane = lax.broadcasted_iota(jnp.int32, sums.shape, 1)
+    own = jnp.where(lane == level, sums, 0.0)
+    of_row = lax.rsqrt(jnp.sum(own, axis=1, keepdims=True))
+    of_lane = lax.rsqrt(jnp.sum(own, axis=0, keepdims=True))
+    work = sums * of_row * jnp.where(lane[:1] < count, of_lane, 1.0)
+    for k in range(0, count, 4):
+        columns = [jnp.broadcast_to(work[:, k + b : k + b + 1], work.shape) for b in range(4)]
+        rows = [work[k + a : k + a + 1, :] for a in range(4)]
+        pivot = [[column[k + a : k + a + 1, :] for column in columns] for a in range(4)]
+        top = inverse_two(pivot[0][0], pivot[0][1], pivot[1][0], pivot[1][1])
+        line_0, line_1 = apply_two(top, rows[0], rows[1])
+        across = [apply_two(top, pivot[0][b], pivot[1][b]) for b in (2, 3)]
+        low = [rows[a] - pivot[a][0] * line_0 - pivot[a][1] * line_1 for a in (2, 3)]
+        rest = [
+            [pivot[a][b] - pivot[a][0] * across[b - 2][0] - pivot[a][1] * across[b - 2][1] for b in (2, 3)]
+            for a in (2, 3)
+        ]
+        line_2, line_3 = apply_two(inverse_two(*rest[0], *rest[1]), *low)
+        line_0 = line_0 - across[0][0] * line_2 - across[1][0] * line_3
+        line_1 = line_1 - across[0][1] * line_2 - across[1][1] * line_3
+        lines = (line_0, line_1, line_2, line_3)
+        for a in range(4):
+            work = work - columns[a] * lines[a]
+        for a in range(4):
+            work = jnp.where(level == k + a, lines[a], work)
     at = 3 * count
+    work = work * of_row
     turned = work.T
     weights = work[:, at : at + 1]
     weights_row = turned[at : at + 1, :]
@@ -453,13 +473,12 @@
 
 
 def on_device(basis, rhs, extra_diag, coeff):
-    odd = jnp.stack([lax.axis_index("gx") % 2, lax.axis_index("gy") % 2]).astype(jnp.int32)
-    first_x, second_x, first_y, second_y = faces(odd, basis, coeff)
+    first_x, second_x, first_y, second_y, cols = faces(basis, coeff)
     first_y, second_y = swap(first_y, "gy", 0), swap(second_y, "gy", 1)
     first_x, second_x = swap(first_x, "gx", 0), swap(second_x, "gx", 1)
-    cols, inner, basis_stack, diag = inside(basis, coeff, extra_diag)
+    inner, basis_stack, diag = inside(cols, coeff, extra_diag)
     halo = (first_x, second_x, first_y, second_y)
-    face_x, face_y = border(odd, cols, inner, coeff, diag, rhs, halo)
+    face_x, face_y = border(cols, inner, coeff, diag, rhs, halo)
     wide, deep = lax.axis_size("gx"), lax.axis_size("gy")
     route = []
     for i in range(wide):
@@ -467,8 +486,8 @@
         route += [(i * deep + j, i * deep + j + step) for j in range(deep) if 0 <= j + step < deep]
     far_y = lax.ppermute(face_y, ("gx", "gy"), route)
     far_x = send(face_x, "gx", -1)
-    part, scaled_stack = local_sums(odd, cols, inner, basis_stack, coeff, diag, rhs, halo)
-    part = shared_sums(odd, part, scaled_stack, coeff, first_y, second_y, far_x, far_y)
+    part, scaled_stack = local_sums(cols, inner, basis_stack, coeff, diag, rhs, halo)
+    part = shared_sums(part, scaled_stack, coeff, first_y, second_y, far_x, far_y)
     total = sum_all(part)
     return finish(total, basis_stack, scaled_stack, rhs.shape)
 

time: 56.8 us -> 54.7 us (0.963)
  Pallas kernels: 18.7 us -> 10.6 us
  waiting for transfers between devices: 16.4 us -> 19.2 us
  local copies, waits for them, and re-layouts: 0.02 us -> 2.52 us
  starting transfers between devices: 20 us -> 21.4 us
  other arithmetic: 0.63 us -> 0.02 us
    pallas_call x5, Pallas kernels: 13.5 us -> 6.89 us  [the longest x1 3.15 us: local_sums(): call(local_kernel, outs, [VM] * 10, [pltpu.VMEM((tall, cells), BF16), plt...]
    ppermute x4, waiting for transfers between devices: 0.26 us -> 2.96 us  [swap(): return lax.ppermute(block, axis, pairs + [(j, i) for i, j in pairs])]
    unnamed x10 -> x8, local copies, waits for them, and re-layouts: 0.02 us -> 2.52 us
    ppermute x1, waiting for transfers between devices: 6.65 us -> 4.36 us  [on_device(): far_y = lax.ppermute(face_y, ('gx', 'gy'), route)]
    ppermute x1, waiting for transfers between devices: 0.01 us -> 2.28 us  [send(): lax.ppermute(block, axis, [(i, i + step) for i in range(size) if 0 <= i +...]
    pallas_call x1, Pallas kernels: 5.19 us -> 3.73 us  [finish(): call(finish_kernel, (shape(*block),) * 2, [VM] * 3, limit=24)]
    ppermute x7, starting transfers between devices: 12.8 us -> 14.2 us  [sum_all(): lax.ppermute(part, ('gx', 'gy'), [(i * deep + j, (i ^ a) * deep + (j ^ b)...]
    another operation x1 -> x0, other arithmetic: 0.6 us -> none  [on_device(): jnp.stack([lax.axis_index('gx') % 2, lax.axis_index('gy') % 2])]
  transfers between devices with their start and end apart: 13 -> 13, of which waited for: 8 -> 8; matrix products, arithmetic and copies ran while one was open for 0% -> 0% of each run, Pallas kernels for 14% -> 10%
where the time goes in v4:
time: 54.7 us; the launch traced here: 54.5 us
  starting transfers between devices  21.4 us (39%)
  waiting for transfers between devices  19.2 us (35%)
  Pallas kernels  10.6 us (19%)
  local copies, waits for them, and re-layouts  2.52 us (5%)
  between operations  0.75 us (1%)
    ppermute x7, starting transfers between devices, sum_all(): lax.ppermute(part, ('gx', 'gy'), [(i * deep + j, (i ^ a) * deep + (j ^ b)...  14.2 us
    ppermute x7, waiting for transfers between devices, sum_all(): lax.ppermute(part, ('gx', 'gy'), [(i * deep + j, (i ^ a) * deep + (j ^ b)...  9.6 us
    ppermute x4, starting transfers between devices, swap(): return lax.ppermute(block, axis, pairs + [(j, i) for i, j in pairs])  4.53 us
    ppermute x1, waiting for transfers between devices, on_device(): far_y = lax.ppermute(face_y, ('gx', 'gy'), route)  4.36 us
    pallas_call x1, Pallas kernels, finish(): call(finish_kernel, (shape(*block),) * 2, [VM] * 3, limit=24)  3.73 us
    pallas_call x1, Pallas kernels, local_sums(): call(local_kernel, outs, [VM] * 10, [pltpu.VMEM((tall, cells), BF16), plt...  3.15 us
    ppermute x4, waiting for transfers between devices, swap(): return lax.ppermute(block, axis, pairs + [(j, i) for i, j in pairs])  2.96 us
    unnamed x8, local copies, waits for them, and re-layouts  2.52 us
  transfers between devices with their start and end apart: 13, of which 8 were waited for; matrix products, arithmetic and copies ran while one was open for 0% of the time, Pallas kernels for 10%

profile of v4, /device:TPU:0, one launch (start us, length us, event | category | flops | bytes accessed | tf_op | source)
XLA Modules:
  0.0 54.5 jit_solution(12778306932829262558)
XLA Ops:
  0.6 0.9 %copy-done = f32[3,8,8,256]{3,2,1,0:T(8,128)S(1)} copy-done((f32[3,8,8,256]{3,2,1,0:T(8,128)S(1)}, f32[3,8,8,256]{3,2,1,0:T(8,128)}, u32[]{:S(2)}) %copy-start) | copy-done | bytes 196632
  1.6 1.6 %copy-done.1 = f32[32,8,8,256]{3,2,1,0:T(8,128)S(1)} copy-done((f32[32,8,8,256]{3,2,1,0:T(8,128)S(1)}, f32[32,8,8,256]{3,2,1,0:T(8,128)}, u32[]{:S(2)}) %copy-start.1) | copy-done | bytes 2097176
  3.2 0.8 %shard_map.59 = (f32[264,256]{1,0:T(8,128)S(1)}, f32[264,256]{1,0:T(8,128)S(1)}, f32[264,256]{1,0:T(8,128)S(1)}, f32[264,256]{1,0:T(8,128)S(1)}, f32[8,8,32,256]{3,2,1,0:T(8,128)S(1)}) custom-call(f32[32,8,8,256]{3,2,1,0:T(8,128)S(1)} %copy-done.1, f32[3,8,8,256]{3,2,1,0:T(8,128)S(1)} %copy-done), custom_call_target="tpu_custom_call" | custom-call | tf_op jit(solution)/shard_map/pallas_call | solution.py:150
  4.0 3.1 %collective-permute-start.2 = (f32[264,256]{1,0:T(8,128)S(1)}, f32[264,256]{1,0:T(8,128)S(1)}, u32[]{:S(2)}, u32[]{:S(2)}) collective-permute-start(f32[264,256]{1,0:T(8,128)S(1)} %get-tuple-element.20), channel_id=1, source_target_pairs={{0,1},{2,3},{1,0},{3,2},{4,5},{6,7},{5,4},{7,6},{8,9},{10,11},{9,8... | collective-permute-start | bytes 811016 | tf_op jit(solution)/shard_map/ppermute | solution.py:73
  7.1 0.7 %collective-permute-start.3 = (f32[264,256]{1,0:T(8,128)S(1)}, f32[264,256]{1,0:T(8,128)S(1)}, u32[]{:S(2)}, u32[]{:S(2)}) collective-permute-start(f32[264,256]{1,0:T(8,128)S(1)} %get-tuple-element.21), channel_id=1, source_target_pairs={{1,2},{2,1},{5,6},{6,5},{9,10},{10,9},{13,14},{14,13},{17,18},{18,... | collective-permute-start | bytes 811016 | tf_op jit(solution)/shard_map/ppermute | solution.py:73
  7.8 0.7 %collective-permute-start.1 = (f32[264,256]{1,0:T(8,128)S(1)}, f32[264,256]{1,0:T(8,128)S(1)}, u32[]{:S(2)}, u32[]{:S(2)}) collective-permute-start(f32[264,256]{1,0:T(8,128)S(1)} %get-tuple-element.19), channel_id=1, source_target_pairs={{4,8},{12,16},{20,24},{8,4},{16,12},{24,20},{5,9},{13,17},{21,25},... | collective-permute-start | bytes 811016 | tf_op jit(solution)/shard_map/ppermute | solution.py:73
  8.5 2.1 %shard_map.60 = (f32[8,8,32,256]{3,2,1,0:T(8,128)S(1)}, bf16[64,16384]{1,0:T(8,128)(2,1)S(1)}, f32[8,8,256]{2,1,0:T(8,128)S(1)}) custom-call(f32[8,8,32,256]{3,2,1,0:T(8,128)S(1)} %get-tuple-element.14.cols, f32[3,8,8,256]{3,2,1,0:T(8,128)S(1)} %copy-done, f32[8,8,256]{2,1,0:T(8,128)S(1)} %copy-done.3), custom_call_target="tpu_custom_call" | custom-call | flops 10485760 | bytes 8388608 | tf_op jit(solution)/shard_map/pallas_call | solution.py:204
  10.6 2.9 %collective-permute-done.2.ya = f32[264,256]{1,0:T(8,128)S(1)} collective-permute-done((f32[264,256]{1,0:T(8,128)S(1)}, f32[264,256]{1,0:T(8,128)S(1)}, u32[]{:S(2)}, u32[]{:S(2)}) %collective-permute-start.2) | collective-permute-done | bytes 270368 | tf_op jit(solution)/shard_map/ppermute | solution.py:73
  13.8 1.3 %collective-permute-start.4 = (f32[264,256]{1,0:T(8,128)S(1)}, f32[264,256]{1,0:T(8,128)S(1)}, u32[]{:S(2)}, u32[]{:S(2)}) collective-permute-start(f32[264,256]{1,0:T(8,128)S(1)} %get-tuple-element.24), channel_id=1, source_target_pairs={{4,0},{8,4},{12,8},{16,12},{20,16},{24,20},{28,24},{5,1},{9,5},{13... | collective-permute-start | bytes 811016 | tf_op jit(solution)/shard_map/ppermute | solution.py:67
  15.1 1.3 %collective-permute-start.5 = (f32[264,256]{1,0:T(8,128)S(1)}, f32[264,256]{1,0:T(8,128)S(1)}, u32[]{:S(2)}, u32[]{:S(2)}) collective-permute-start(f32[264,256]{1,0:T(8,128)S(1)} %get-tuple-element.25), channel_id=1, source_target_pairs={{1,0},{2,1},{3,2},{4,5},{5,6},{6,7},{9,8},{10,9},{11,10},{12,13},{... | collective-permute-start | bytes 811016 | tf_op jit(solution)/shard_map/ppermute | solution.py:487
  16.4 3.1 %shard_map.61 = (f32[40,128]{1,0:T(8,128)S(1)}, bf16[80,16384]{1,0:T(8,128)(2,1)S(1)}) custom-call(f32[8,8,32,256]{3,2,1,0:T(8,128)S(1)} %get-tuple-element.14.cols, f32[8,8,32,256]{3,2,1,0:T(8,128)S(1)} %get-tuple-element.15.inner, bf16[64,16384]{1,0:T(8,128)(2,1)S(1)} %get-tuple-element.16.basis_stack, f32[3,8,8,256]{3,2,1,0:T(8,128)S(1)} %copy-done, ...), custom_call_target="tpu_custom_call" | custom-call | flops 31457280 | bytes 12582912 | tf_op jit(solution)/shard_map/pallas_call | solution.py:327
  19.5 2.3 %collective-permute-done.4.far_x = f32[264,256]{1,0:T(8,128)S(1)} collective-permute-done((f32[264,256]{1,0:T(8,128)S(1)}, f32[264,256]{1,0:T(8,128)S(1)}, u32[]{:S(2)}, u32[]{:S(2)}) %collective-permute-start.4) | collective-permute-done | bytes 270368 | tf_op jit(solution)/shard_map/ppermute | solution.py:67
  21.8 4.4 %collective-permute-done.5.far_y = f32[264,256]{1,0:T(8,128)S(1)} collective-permute-done((f32[264,256]{1,0:T(8,128)S(1)}, f32[264,256]{1,0:T(8,128)S(1)}, u32[]{:S(2)}, u32[]{:S(2)}) %collective-permute-start.5) | collective-permute-done | bytes 270368 | tf_op jit(solution)/shard_map/ppermute | solution.py:487
  26.9 3.3 %collective-permute-start.6 = (f32[40,128]{1,0:T(8,128)S(1)}, f32[40,128]{1,0:T(8,128)S(1)}, u32[]{:S(2)}, u32[]{:S(2)}) collective-permute-start(f32[40,128]{1,0:T(8,128)S(1)} %shard_map.63), channel_id=1, source_target_pairs={{0,2},{1,3},{2,0},{3,1},{4,6},{5,7},{6,4},{7,5},{8,10},{9,11},{10,... | collective-permute-start | bytes 61448 | tf_op jit(solution)/shard_map/ppermute | solution.py:53
  30.1 1.8 %collective-permute-done.6 = f32[40,128]{1,0:T(8,128)S(1)} collective-permute-done((f32[40,128]{1,0:T(8,128)S(1)}, f32[40,128]{1,0:T(8,128)S(1)}, u32[]{:S(2)}, u32[]{:S(2)}) %collective-permute-start.6) | collective-permute-done | bytes 20512 | tf_op jit(solution)/shard_map/ppermute | solution.py:53
  31.9 2.6 %collective-permute-start.7 = (f32[40,128]{1,0:T(8,128)S(1)}, f32[40,128]{1,0:T(8,128)S(1)}, u32[]{:S(2)}, u32[]{:S(2)}) collective-permute-start(f32[40,128]{1,0:T(8,128)S(1)} %add.21), channel_id=1, source_target_pairs={{0,4},{1,5},{2,6},{3,7},{4,0},{5,1},{6,2},{7,3},{8,12},{9,13},{10,... | collective-permute-start | bytes 61448 | tf_op jit(solution)/shard_map/ppermute | solution.py:53
  34.5 4.4 %collective-permute-start.8 = (f32[40,128]{1,0:T(8,128)S(1)}, f32[40,128]{1,0:T(8,128)S(1)}, u32[]{:S(2)}, u32[]{:S(2)}) collective-permute-start(f32[40,128]{1,0:T(8,128)S(1)} %add.21), channel_id=1, source_target_pairs={{0,8},{1,9},{2,10},{3,11},{4,12},{5,13},{6,14},{7,15},{8,0},{9,1},... | collective-permute-start | bytes 61448 | tf_op jit(solution)/shard_map/ppermute | solution.py:53
  38.9 1.7 %collective-permute-done.8 = f32[40,128]{1,0:T(8,128)S(1)} collective-permute-done((f32[40,128]{1,0:T(8,128)S(1)}, f32[40,128]{1,0:T(8,128)S(1)}, u32[]{:S(2)}, u32[]{:S(2)}) %collective-permute-start.8) | collective-permute-done | bytes 20512 | tf_op jit(solution)/shard_map/ppermute | solution.py:53
  40.6 1.4 %collective-permute-done.9 = f32[40,128]{1,0:T(8,128)S(1)} collective-permute-done((f32[40,128]{1,0:T(8,128)S(1)}, f32[40,128]{1,0:T(8,128)S(1)}, u32[]{:S(2)}, u32[]{:S(2)}) %collective-permute-start.9) | collective-permute-done | bytes 20512 | tf_op jit(solution)/shard_map/ppermute | solution.py:53
  42.1 1.9 %collective-permute-start.10 = (f32[40,128]{1,0:T(8,128)S(1)}, f32[40,128]{1,0:T(8,128)S(1)}, u32[]{:S(2)}, u32[]{:S(2)}) collective-permute-start(f32[40,128]{1,0:T(8,128)S(1)} %add_add_fusion.1), channel_id=1, source_target_pairs={{0,16},{1,17},{2,18},{3,19},{4,20},{5,21},{6,22},{7,23},{8,24},{9,... | collective-permute-start | bytes 61448 | tf_op jit(solution)/shard_map/ppermute | solution.py:53
  44.0 2.0 %collective-permute-start.11 = (f32[40,128]{1,0:T(8,128)S(1)}, f32[40,128]{1,0:T(8,128)S(1)}, u32[]{:S(2)}, u32[]{:S(2)}) collective-permute-start(f32[40,128]{1,0:T(8,128)S(1)} %add_add_fusion.1), channel_id=1, source_target_pairs={{0,1},{1,0},{2,3},{3,2},{4,5},{5,4},{6,7},{7,6},{8,9},{9,8},{10,11... | collective-permute-start | bytes 61448 | tf_op jit(solution)/shard_map/ppermute | solution.py:53
  46.0 1.8 %collective-permute-done.11 = f32[40,128]{1,0:T(8,128)S(1)} collective-permute-done((f32[40,128]{1,0:T(8,128)S(1)}, f32[40,128]{1,0:T(8,128)S(1)}, u32[]{:S(2)}, u32[]{:S(2)}) %collective-permute-start.11) | collective-permute-done | bytes 20512 | tf_op jit(solution)/shard_map/ppermute | solution.py:53
  47.8 2.9 %collective-permute-done.12 = f32[40,128]{1,0:T(8,128)S(1)} collective-permute-done((f32[40,128]{1,0:T(8,128)S(1)}, f32[40,128]{1,0:T(8,128)S(1)}, u32[]{:S(2)}, u32[]{:S(2)}) %collective-permute-start.12) | collective-permute-done | bytes 20512 | tf_op jit(solution)/shard_map/ppermute | solution.py:53
  50.7 3.7 %shard_map.64 = (f32[8,8,256]{2,1,0:T(8,128)}, f32[8,8,256]{2,1,0:T(8,128)}) custom-call(f32[40,128]{1,0:T(8,128)S(1)} %add_add_fusion.total, bf16[64,16384]{1,0:T(8,128)(2,1)S(1)} %get-tuple-element.16.basis_stack, bf16[80,16384]{1,0:T(8,128)(2,1)S(1)} %get-tuple-element.23.scaled_stack), custom_call_target="tpu_custom_call" | custom-call | tf_op jit(solution)/shard_map/pallas_call | solution.py:470
  (19 shorter events, 1.0 us)
Async XLA Ops:
  0.6 0.9 %copy-start = (f32[3,8,8,256]{3,2,1,0:T(8,128)S(1)}, f32[3,8,8,256]{3,2,1,0:T(8,128)}, u32[]{:S(2)}) copy-start(f32[3,8,8,256]{3,2,1,0:T(8,128)} %coeff.9) | copy-start | bytes 589828
  1.6 1.6 %copy-start.1 = (f32[32,8,8,256]{3,2,1,0:T(8,128)S(1)}, f32[32,8,8,256]{3,2,1,0:T(8,128)}, u32[]{:S(2)}) copy-start(f32[32,8,8,256]{3,2,1,0:T(8,128)} %basis.1) | copy-start | bytes 6291460
  3.1 5.4 %copy-start.3 = (f32[8,8,256]{2,1,0:T(8,128)S(1)}, f32[8,8,256]{2,1,0:T(8,128)}, u32[]{:S(2)}) copy-start(f32[8,8,256]{2,1,0:T(8,128)} %extra_raw.1) | copy-start | bytes 196612
  3.2 10.4 %copy-start.2 = (f32[8,8,256]{2,1,0:T(8,128)S(1)}, f32[8,8,256]{2,1,0:T(8,128)}, u32[]{:S(2)}) copy-start(f32[8,8,256]{2,1,0:T(8,128)} %rhs.3) | copy-start | bytes 196612
  4.0 9.6 %collective-permute-start.2 = (f32[264,256]{1,0:T(8,128)S(1)}, f32[264,256]{1,0:T(8,128)S(1)}, u32[]{:S(2)}, u32[]{:S(2)}) collective-permute-start(f32[264,256]{1,0:T(8,128)S(1)} %get-tuple-element.20), channel_id=1, source_target_pairs={{0,1},{2,3},{1,0},{3,2},{4,5},{6,7},{5,4},{7,6},{8,9},{10,11},{9,8... | collective-permute-start | bytes 811016 | tf_op jit(solution)/shard_map/ppermute | solution.py:73
  7.1 6.5 %collective-permute-start.3 = (f32[264,256]{1,0:T(8,128)S(1)}, f32[264,256]{1,0:T(8,128)S(1)}, u32[]{:S(2)}, u32[]{:S(2)}) collective-permute-start(f32[264,256]{1,0:T(8,128)S(1)} %get-tuple-element.21), channel_id=1, source_target_pairs={{1,2},{2,1},{5,6},{6,5},{9,10},{10,9},{13,14},{14,13},{17,18},{18,... | collective-permute-start | bytes 811016 | tf_op jit(solution)/shard_map/ppermute | solution.py:73
  7.7 5.8 %collective-permute-start = (f32[264,256]{1,0:T(8,128)S(1)}, f32[264,256]{1,0:T(8,128)S(1)}, u32[]{:S(2)}, u32[]{:S(2)}) collective-permute-start(f32[264,256]{1,0:T(8,128)S(1)} %get-tuple-element.18), channel_id=1, source_target_pairs={{0,4},{8,12},{16,20},{24,28},{4,0},{12,8},{20,16},{28,24},{1,5},{9... | collective-permute-start | bytes 811016 | tf_op jit(solution)/shard_map/ppermute | solution.py:73
  7.8 5.7 %collective-permute-start.1 = (f32[264,256]{1,0:T(8,128)S(1)}, f32[264,256]{1,0:T(8,128)S(1)}, u32[]{:S(2)}, u32[]{:S(2)}) collective-permute-start(f32[264,256]{1,0:T(8,128)S(1)} %get-tuple-element.19), channel_id=1, source_target_pairs={{4,8},{12,16},{20,24},{8,4},{16,12},{24,20},{5,9},{13,17},{21,25},... | collective-permute-start | bytes 811016 | tf_op jit(solution)/shard_map/ppermute | solution.py:73
  13.8 8.0 %collective-permute-start.4 = (f32[264,256]{1,0:T(8,128)S(1)}, f32[264,256]{1,0:T(8,128)S(1)}, u32[]{:S(2)}, u32[]{:S(2)}) collective-permute-start(f32[264,256]{1,0:T(8,128)S(1)} %get-tuple-element.24), channel_id=1, source_target_pairs={{4,0},{8,4},{12,8},{16,12},{20,16},{24,20},{28,24},{5,1},{9,5},{13... | collective-permute-start | bytes 811016 | tf_op jit(solution)/shard_map/ppermute | solution.py:67
  15.1 11.1 %collective-permute-start.5 = (f32[264,256]{1,0:T(8,128)S(1)}, f32[264,256]{1,0:T(8,128)S(1)}, u32[]{:S(2)}, u32[]{:S(2)}) collective-permute-start(f32[264,256]{1,0:T(8,128)S(1)} %get-tuple-element.25), channel_id=1, source_target_pairs={{1,0},{2,1},{3,2},{4,5},{5,6},{6,7},{9,8},{10,9},{11,10},{12,13},{... | collective-permute-start | bytes 811016 | tf_op jit(solution)/shard_map/ppermute | solution.py:487
  26.9 5.0 %collective-permute-start.6 = (f32[40,128]{1,0:T(8,128)S(1)}, f32[40,128]{1,0:T(8,128)S(1)}, u32[]{:S(2)}, u32[]{:S(2)}) collective-permute-start(f32[40,128]{1,0:T(8,128)S(1)} %shard_map.63), channel_id=1, source_target_pairs={{0,2},{1,3},{2,0},{3,1},{4,6},{5,7},{6,4},{7,5},{8,10},{9,11},{10,... | collective-permute-start | bytes 61448 | tf_op jit(solution)/shard_map/ppermute | solution.py:53
  31.9 7.0 %collective-permute-start.7 = (f32[40,128]{1,0:T(8,128)S(1)}, f32[40,128]{1,0:T(8,128)S(1)}, u32[]{:S(2)}, u32[]{:S(2)}) collective-permute-start(f32[40,128]{1,0:T(8,128)S(1)} %add.21), channel_id=1, source_target_pairs={{0,4},{1,5},{2,6},{3,7},{4,0},{5,1},{6,2},{7,3},{8,12},{9,13},{10,... | collective-permute-start | bytes 61448 | tf_op jit(solution)/shard_map/ppermute | solution.py:53
  34.5 6.1 %collective-permute-start.8 = (f32[40,128]{1,0:T(8,128)S(1)}, f32[40,128]{1,0:T(8,128)S(1)}, u32[]{:S(2)}, u32[]{:S(2)}) collective-permute-start(f32[40,128]{1,0:T(8,128)S(1)} %add.21), channel_id=1, source_target_pairs={{0,8},{1,9},{2,10},{3,11},{4,12},{5,13},{6,14},{7,15},{8,0},{9,1},... | collective-permute-start | bytes 61448 | tf_op jit(solution)/shard_map/ppermute | solution.py:53
  38.9 3.2 %collective-permute-start.9 = (f32[40,128]{1,0:T(8,128)S(1)}, f32[40,128]{1,0:T(8,128)S(1)}, u32[]{:S(2)}, u32[]{:S(2)}) collective-permute-start(f32[40,128]{1,0:T(8,128)S(1)} %add.21), channel_id=1, source_target_pairs={{0,12},{1,13},{2,14},{3,15},{4,8},{5,9},{6,10},{7,11},{8,4},{9,5},... | collective-permute-start | bytes 61448 | tf_op jit(solution)/shard_map/ppermute | solution.py:53
  42.1 4.0 %collective-permute-start.10 = (f32[40,128]{1,0:T(8,128)S(1)}, f32[40,128]{1,0:T(8,128)S(1)}, u32[]{:S(2)}, u32[]{:S(2)}) collective-permute-start(f32[40,128]{1,0:T(8,128)S(1)} %add_add_fusion.1), channel_id=1, source_target_pairs={{0,16},{1,17},{2,18},{3,19},{4,20},{5,21},{6,22},{7,23},{8,24},{9,... | collective-permute-start | bytes 61448 | tf_op jit(solution)/shard_map/ppermute | solution.py:53
  44.0 3.8 %collective-permute-start.11 = (f32[40,128]{1,0:T(8,128)S(1)}, f32[40,128]{1,0:T(8,128)S(1)}, u32[]{:S(2)}, u32[]{:S(2)}) collective-permute-start(f32[40,128]{1,0:T(8,128)S(1)} %add_add_fusion.1), channel_id=1, source_target_pairs={{0,1},{1,0},{2,3},{3,2},{4,5},{5,4},{6,7},{7,6},{8,9},{9,8},{10,11... | collective-permute-start | bytes 61448 | tf_op jit(solution)/shard_map/ppermute | solution.py:53
  46.0 4.7 %collective-permute-start.12 = (f32[40,128]{1,0:T(8,128)S(1)}, f32[40,128]{1,0:T(8,128)S(1)}, u32[]{:S(2)}, u32[]{:S(2)}) collective-permute-start(f32[40,128]{1,0:T(8,128)S(1)} %add_add_fusion.1), channel_id=1, source_target_pairs={{0,17},{1,16},{2,19},{3,18},{4,21},{5,20},{6,23},{7,22},{8,25},{9,... | collective-permute-start | bytes 61448 | tf_op jit(solution)/shard_map/ppermute | solution.py:53

commit v5 on v4

--- a/solution.py
+++ b/solution.py
@@ -115,13 +115,13 @@
 
 
 def faces_kernel(basis, coeff, first_x, second_x, first_y, second_y, cols, slabs, sems):
-    count, nx, ny, deep = basis.shape
+    count, nx, ny, _ = basis.shape
     odd = parity()
     copies = [pltpu.make_async_copy(basis.at[:, x], slabs.at[x], sems.at[x]) for x in range(nx)]
     ends = []
-    for k, target in enumerate((first_x, second_x)):
+    for target in (first_x, second_x):
         ends.append((coeff.at[0, nx - 1], target.at[pl.ds(ny * count, ny)]))
-    for k, target in enumerate((first_y, second_y)):
+    for target in (first_y, second_y):
         ends.append((coeff.at[1, :, ny - 1, :], target.at[pl.ds(nx * count, nx)]))
     ends = [pltpu.make_async_copy(a, b, sems.at[nx + k]) for k, (a, b) in enumerate(ends)]
     for copy in copies + ends:
@@ -147,7 +147,7 @@
     outs = (of_x, of_x, of_y, of_y, shape(nx, ny, count, deep))
     slabs = pltpu.VMEM((nx, count, ny, deep), F32)
     sems = pltpu.SemaphoreType.DMA((nx + 4,))
-    return call(faces_kernel, outs, [RAW, RAW], [slabs, sems], limit=40)(basis, coeff)
+    return call(faces_kernel, outs, [RAW, RAW], [slabs, sems], limit=50)(basis, coeff)
 
 
 def row(ref, *at):
@@ -161,7 +161,7 @@
 
 
 def inner_kernel(cols, coeff, extra_raw, inner, stack, diag, upper, lower, ahead, behind, extra, sem):
-    nx, ny, count, deep = cols.shape
+    nx, ny, _, deep = cols.shape
     extra_copy = pltpu.make_async_copy(extra_raw, extra, sem)
     extra_copy.start()
     level = lax.broadcasted_iota(jnp.int32, (ny, deep), 0)
@@ -228,7 +228,7 @@
 
 
 def full_value(cols, inner, coeff, halo, x, y):
-    nx, ny, count, deep = cols.shape
+    nx, ny, count, _ = cols.shape
     value = inner[x, y]
     if x == 0:
         value += halo.rows(0, False, ny * count + y, 1) * (cols[x, y] - halo.rows(0, False, y * count, count))
@@ -242,7 +242,7 @@
 
 
 def border_kernel(cols, inner, coeff, diag, rhs, xa, xb, ya, yb, face_x, face_y, scale):
-    nx, ny, count, deep = cols.shape
+    nx, ny, count, _ = cols.shape
     odd = parity()
     halo = Halo(odd, (xa, xb, ya, yb))
     for x in range(nx):
@@ -472,10 +472,12 @@
     )
 
 
-def on_device(basis, rhs, extra_diag, coeff):
+def steps(basis, rhs, extra_diag, coeff):
     first_x, second_x, first_y, second_y, cols = faces(basis, coeff)
-    first_y, second_y = swap(first_y, "gy", 0), swap(second_y, "gy", 1)
-    first_x, second_x = swap(first_x, "gx", 0), swap(second_x, "gx", 1)
+    first_x = swap(first_x, "gx", 0)
+    second_x = swap(second_x, "gx", 1)
+    first_y = swap(first_y, "gy", 0)
+    second_y = swap(second_y, "gy", 1)
     inner, basis_stack, diag = inside(cols, coeff, extra_diag)
     halo = (first_x, second_x, first_y, second_y)
     face_x, face_y = border(cols, inner, coeff, diag, rhs, halo)
@@ -500,7 +502,7 @@
         P(None, "gx", "gy", None),
     )
     return jax.shard_map(
-        on_device,
+        steps,
         mesh=mesh,
         in_specs=placed,
         out_specs=(P("gx", "gy", None), P("gx", "gy", None)),

time: 54.7 us -> 54.1 us (0.989)
  local copies, waits for them, and re-layouts: 2.52 us -> 0.93 us
  Pallas kernels: 10.6 us -> 11.6 us
    unnamed x8 -> x6, local copies, waits for them, and re-layouts: 2.52 us -> 0.93 us
    pallas_call x1, Pallas kernels: 0.8 us -> 1.75 us  [faces(): call(faces_kernel, outs, [RAW, RAW], [slabs, sems], limit=50)(basis, coeff)]
where the time goes in v5:
time: 54.1 us; the launch traced here: 53.8 us
  starting transfers between devices  21.4 us (40%)
  waiting for transfers between devices  19.2 us (35%)
  Pallas kernels  11.6 us (21%)
  local copies, waits for them, and re-layouts  0.93 us (2%)
  between operations  0.75 us (1%)
    ppermute x7, starting transfers between devices, sum_all(): lax.ppermute(part, ('gx', 'gy'), [(i * deep + j, (i ^ a) * deep + (j ^ b)...  14.2 us
    ppermute x7, waiting for transfers between devices, sum_all(): lax.ppermute(part, ('gx', 'gy'), [(i * deep + j, (i ^ a) * deep + (j ^ b)...  9.6 us
    ppermute x4, starting transfers between devices, swap(): return lax.ppermute(block, axis, pairs + [(j, i) for i, j in pairs])  4.53 us
    ppermute x1, waiting for transfers between devices, steps(): far_y = lax.ppermute(face_y, ('gx', 'gy'), route)  4.36 us
    pallas_call x1, Pallas kernels, finish(): call(finish_kernel, (shape(*block),) * 2, [VM] * 3, limit=24)  3.72 us
    pallas_call x1, Pallas kernels, local_sums(): call(local_kernel, outs, [VM] * 10, [pltpu.VMEM((tall, cells), BF16), plt...  3.13 us
    ppermute x4, waiting for transfers between devices, swap(): return lax.ppermute(block, axis, pairs + [(j, i) for i, j in pairs])  2.95 us
    ppermute x1, waiting for transfers between devices, send(): lax.ppermute(block, axis, [(i, i + step) for i in range(size) if 0 <= i +...  2.29 us
  transfers between devices with their start and end apart: 13, of which 8 were waited for; matrix products, arithmetic and copies ran while one was open for 0% of the time, Pallas kernels for 10%

profile of v5, /device:TPU:0, one launch (start us, length us, event | category | flops | bytes accessed | tf_op | source)
XLA Modules:
  0.0 53.8 jit_solution(532988442559213847)
XLA Ops:
  0.6 0.9 %copy-done = f32[3,8,8,256]{3,2,1,0:T(8,128)S(1)} copy-done((f32[3,8,8,256]{3,2,1,0:T(8,128)S(1)}, f32[3,8,8,256]{3,2,1,0:T(8,128)}, u32[]{:S(2)}) %copy-start) | copy-done | bytes 196632
  1.6 1.8 %shard_map.59 = (f32[264,256]{1,0:T(8,128)S(1)}, f32[264,256]{1,0:T(8,128)S(1)}, f32[264,256]{1,0:T(8,128)S(1)}, f32[264,256]{1,0:T(8,128)S(1)}, f32[8,8,32,256]{3,2,1,0:T(8,128)S(1)}) custom-call(f32[32,8,8,256]{3,2,1,0:T(8,128)} %basis.1, f32[3,8,8,256]{3,2,1,0:T(8,128)S(1)} %copy-done), custom_call_target="tpu_custom_call" | custom-call | tf_op jit(solution)/shard_map/pallas_call | solution.py:150
  3.3 3.1 %collective-permute-start.2 = (f32[264,256]{1,0:T(8,128)S(1)}, f32[264,256]{1,0:T(8,128)S(1)}, u32[]{:S(2)}, u32[]{:S(2)}) collective-permute-start(f32[264,256]{1,0:T(8,128)S(1)} %get-tuple-element.20), channel_id=1, source_target_pairs={{0,1},{2,3},{1,0},{3,2},{4,5},{6,7},{5,4},{7,6},{8,9},{10,11},{9,8... | collective-permute-start | bytes 811016 | tf_op jit(solution)/shard_map/ppermute | solution.py:73
  6.4 0.7 %collective-permute-start.3 = (f32[264,256]{1,0:T(8,128)S(1)}, f32[264,256]{1,0:T(8,128)S(1)}, u32[]{:S(2)}, u32[]{:S(2)}) collective-permute-start(f32[264,256]{1,0:T(8,128)S(1)} %get-tuple-element.21), channel_id=1, source_target_pairs={{1,2},{2,1},{5,6},{6,5},{9,10},{10,9},{13,14},{14,13},{17,18},{18,... | collective-permute-start | bytes 811016 | tf_op jit(solution)/shard_map/ppermute | solution.py:73
  7.2 0.7 %collective-permute-start.1 = (f32[264,256]{1,0:T(8,128)S(1)}, f32[264,256]{1,0:T(8,128)S(1)}, u32[]{:S(2)}, u32[]{:S(2)}) collective-permute-start(f32[264,256]{1,0:T(8,128)S(1)} %get-tuple-element.19), channel_id=1, source_target_pairs={{4,8},{12,16},{20,24},{8,4},{16,12},{24,20},{5,9},{13,17},{21,25},... | collective-permute-start | bytes 811016 | tf_op jit(solution)/shard_map/ppermute | solution.py:73
  7.9 2.1 %shard_map.60 = (f32[8,8,32,256]{3,2,1,0:T(8,128)S(1)}, bf16[64,16384]{1,0:T(8,128)(2,1)S(1)}, f32[8,8,256]{2,1,0:T(8,128)S(1)}) custom-call(f32[8,8,32,256]{3,2,1,0:T(8,128)S(1)} %get-tuple-element.14.cols, f32[3,8,8,256]{3,2,1,0:T(8,128)S(1)} %copy-done, f32[8,8,256]{2,1,0:T(8,128)S(1)} %copy-done.2), custom_call_target="tpu_custom_call" | custom-call | flops 10485760 | bytes 8388608 | tf_op jit(solution)/shard_map/pallas_call | solution.py:204
  10.0 2.9 %collective-permute-done.2.ya = f32[264,256]{1,0:T(8,128)S(1)} collective-permute-done((f32[264,256]{1,0:T(8,128)S(1)}, f32[264,256]{1,0:T(8,128)S(1)}, u32[]{:S(2)}, u32[]{:S(2)}) %collective-permute-start.2) | collective-permute-done | bytes 270368 | tf_op jit(solution)/shard_map/ppermute | solution.py:73
  13.2 1.3 %collective-permute-start.4 = (f32[264,256]{1,0:T(8,128)S(1)}, f32[264,256]{1,0:T(8,128)S(1)}, u32[]{:S(2)}, u32[]{:S(2)}) collective-permute-start(f32[264,256]{1,0:T(8,128)S(1)} %get-tuple-element.24), channel_id=1, source_target_pairs={{4,0},{8,4},{12,8},{16,12},{20,16},{24,20},{28,24},{5,1},{9,5},{13... | collective-permute-start | bytes 811016 | tf_op jit(solution)/shard_map/ppermute | solution.py:67
  14.5 1.3 %collective-permute-start.5 = (f32[264,256]{1,0:T(8,128)S(1)}, f32[264,256]{1,0:T(8,128)S(1)}, u32[]{:S(2)}, u32[]{:S(2)}) collective-permute-start(f32[264,256]{1,0:T(8,128)S(1)} %get-tuple-element.25), channel_id=1, source_target_pairs={{1,0},{2,1},{3,2},{4,5},{5,6},{6,7},{9,8},{10,9},{11,10},{12,13},{... | collective-permute-start | bytes 811016 | tf_op jit(solution)/shard_map/ppermute | solution.py:489
  15.8 3.1 %shard_map.61 = (f32[40,128]{1,0:T(8,128)S(1)}, bf16[80,16384]{1,0:T(8,128)(2,1)S(1)}) custom-call(f32[8,8,32,256]{3,2,1,0:T(8,128)S(1)} %get-tuple-element.14.cols, f32[8,8,32,256]{3,2,1,0:T(8,128)S(1)} %get-tuple-element.15.inner, bf16[64,16384]{1,0:T(8,128)(2,1)S(1)} %get-tuple-element.16.basis_stack, f32[3,8,8,256]{3,2,1,0:T(8,128)S(1)} %copy-done, ...), custom_call_target="tpu_custom_call" | custom-call | flops 31457280 | bytes 12582912 | tf_op jit(solution)/shard_map/pallas_call | solution.py:327
  18.9 2.3 %collective-permute-done.4.far_x = f32[264,256]{1,0:T(8,128)S(1)} collective-permute-done((f32[264,256]{1,0:T(8,128)S(1)}, f32[264,256]{1,0:T(8,128)S(1)}, u32[]{:S(2)}, u32[]{:S(2)}) %collective-permute-start.4) | collective-permute-done | bytes 270368 | tf_op jit(solution)/shard_map/ppermute | solution.py:67
  21.2 4.4 %collective-permute-done.5.far_y = f32[264,256]{1,0:T(8,128)S(1)} collective-permute-done((f32[264,256]{1,0:T(8,128)S(1)}, f32[264,256]{1,0:T(8,128)S(1)}, u32[]{:S(2)}, u32[]{:S(2)}) %collective-permute-start.5) | collective-permute-done | bytes 270368 | tf_op jit(solution)/shard_map/ppermute | solution.py:489
  25.6 0.7 %shard_map.63 = f32[40,128]{1,0:T(8,128)S(1)} custom-call(f32[40,128]{1,0:T(8,128)S(1)} %get-tuple-element.22.part, bf16[80,16384]{1,0:T(8,128)(2,1)S(1)} %get-tuple-element.23.scaled_stack, f32[3,8,8,256]{3,2,1,0:T(8,128)S(1)} %copy-done, f32[264,256]{1,0:T(8,128)S(1)} %collective-permute-done.2.ya, f32[264,256]{1,0:T(8,128)S(1)} %collective-permute-done.3.yb, ...), custom_call_target="tpu_custom_call" | custom-call | tf_op jit(solution)/shard_map/pallas_call | solution.py:384
  26.2 3.2 %collective-permute-start.6 = (f32[40,128]{1,0:T(8,128)S(1)}, f32[40,128]{1,0:T(8,128)S(1)}, u32[]{:S(2)}, u32[]{:S(2)}) collective-permute-start(f32[40,128]{1,0:T(8,128)S(1)} %shard_map.63), channel_id=1, source_target_pairs={{0,2},{1,3},{2,0},{3,1},{4,6},{5,7},{6,4},{7,5},{8,10},{9,11},{10,... | collective-permute-start | bytes 61448 | tf_op jit(solution)/shard_map/ppermute | solution.py:53
  29.5 1.8 %collective-permute-done.6 = f32[40,128]{1,0:T(8,128)S(1)} collective-permute-done((f32[40,128]{1,0:T(8,128)S(1)}, f32[40,128]{1,0:T(8,128)S(1)}, u32[]{:S(2)}, u32[]{:S(2)}) %collective-permute-start.6) | collective-permute-done | bytes 20512 | tf_op jit(solution)/shard_map/ppermute | solution.py:53
  31.2 2.6 %collective-permute-start.7 = (f32[40,128]{1,0:T(8,128)S(1)}, f32[40,128]{1,0:T(8,128)S(1)}, u32[]{:S(2)}, u32[]{:S(2)}) collective-permute-start(f32[40,128]{1,0:T(8,128)S(1)} %add.21), channel_id=1, source_target_pairs={{0,4},{1,5},{2,6},{3,7},{4,0},{5,1},{6,2},{7,3},{8,12},{9,13},{10,... | collective-permute-start | bytes 61448 | tf_op jit(solution)/shard_map/ppermute | solution.py:53
  33.9 4.4 %collective-permute-start.8 = (f32[40,128]{1,0:T(8,128)S(1)}, f32[40,128]{1,0:T(8,128)S(1)}, u32[]{:S(2)}, u32[]{:S(2)}) collective-permute-start(f32[40,128]{1,0:T(8,128)S(1)} %add.21), channel_id=1, source_target_pairs={{0,8},{1,9},{2,10},{3,11},{4,12},{5,13},{6,14},{7,15},{8,0},{9,1},... | collective-permute-start | bytes 61448 | tf_op jit(solution)/shard_map/ppermute | solution.py:53
  38.3 1.7 %collective-permute-done.8 = f32[40,128]{1,0:T(8,128)S(1)} collective-permute-done((f32[40,128]{1,0:T(8,128)S(1)}, f32[40,128]{1,0:T(8,128)S(1)}, u32[]{:S(2)}, u32[]{:S(2)}) %collective-permute-start.8) | collective-permute-done | bytes 20512 | tf_op jit(solution)/shard_map/ppermute | solution.py:53
  40.0 1.4 %collective-permute-done.9 = f32[40,128]{1,0:T(8,128)S(1)} collective-permute-done((f32[40,128]{1,0:T(8,128)S(1)}, f32[40,128]{1,0:T(8,128)S(1)}, u32[]{:S(2)}, u32[]{:S(2)}) %collective-permute-start.9) | collective-permute-done | bytes 20512 | tf_op jit(solution)/shard_map/ppermute | solution.py:53
  41.4 1.9 %collective-permute-start.10 = (f32[40,128]{1,0:T(8,128)S(1)}, f32[40,128]{1,0:T(8,128)S(1)}, u32[]{:S(2)}, u32[]{:S(2)}) collective-permute-start(f32[40,128]{1,0:T(8,128)S(1)} %add_add_fusion.1), channel_id=1, source_target_pairs={{0,16},{1,17},{2,18},{3,19},{4,20},{5,21},{6,22},{7,23},{8,24},{9,... | collective-permute-start | bytes 61448 | tf_op jit(solution)/shard_map/ppermute | solution.py:53
  43.4 2.0 %collective-permute-start.11 = (f32[40,128]{1,0:T(8,128)S(1)}, f32[40,128]{1,0:T(8,128)S(1)}, u32[]{:S(2)}, u32[]{:S(2)}) collective-permute-start(f32[40,128]{1,0:T(8,128)S(1)} %add_add_fusion.1), channel_id=1, source_target_pairs={{0,1},{1,0},{2,3},{3,2},{4,5},{5,4},{6,7},{7,6},{8,9},{9,8},{10,11... | collective-permute-start | bytes 61448 | tf_op jit(solution)/shard_map/ppermute | solution.py:53
  45.4 1.8 %collective-permute-done.11 = f32[40,128]{1,0:T(8,128)S(1)} collective-permute-done((f32[40,128]{1,0:T(8,128)S(1)}, f32[40,128]{1,0:T(8,128)S(1)}, u32[]{:S(2)}, u32[]{:S(2)}) %collective-permute-start.11) | collective-permute-done | bytes 20512 | tf_op jit(solution)/shard_map/ppermute | solution.py:53
  47.2 2.9 %collective-permute-done.12 = f32[40,128]{1,0:T(8,128)S(1)} collective-permute-done((f32[40,128]{1,0:T(8,128)S(1)}, f32[40,128]{1,0:T(8,128)S(1)}, u32[]{:S(2)}, u32[]{:S(2)}) %collective-permute-start.12) | collective-permute-done | bytes 20512 | tf_op jit(solution)/shard_map/ppermute | solution.py:53
  50.1 3.7 %shard_map.64 = (f32[8,8,256]{2,1,0:T(8,128)}, f32[8,8,256]{2,1,0:T(8,128)}) custom-call(f32[40,128]{1,0:T(8,128)S(1)} %add_add_fusion.total, bf16[64,16384]{1,0:T(8,128)(2,1)S(1)} %get-tuple-element.16.basis_stack, bf16[80,16384]{1,0:T(8,128)(2,1)S(1)} %get-tuple-element.23.scaled_stack), custom_call_target="tpu_custom_call" | custom-call | tf_op jit(solution)/shard_map/pallas_call | solution.py:470
  (17 shorter events, 0.4 us)
Async XLA Ops:
  0.6 0.9 %copy-start = (f32[3,8,8,256]{3,2,1,0:T(8,128)S(1)}, f32[3,8,8,256]{3,2,1,0:T(8,128)}, u32[]{:S(2)}) copy-start(f32[3,8,8,256]{3,2,1,0:T(8,128)} %coeff.9) | copy-start | bytes 589828
  1.6 6.3 %copy-start.2 = (f32[8,8,256]{2,1,0:T(8,128)S(1)}, f32[8,8,256]{2,1,0:T(8,128)}, u32[]{:S(2)}) copy-start(f32[8,8,256]{2,1,0:T(8,128)} %extra_raw.1) | copy-start | bytes 196612
  1.6 11.4 %copy-start.1 = (f32[8,8,256]{2,1,0:T(8,128)S(1)}, f32[8,8,256]{2,1,0:T(8,128)}, u32[]{:S(2)}) copy-start(f32[8,8,256]{2,1,0:T(8,128)} %rhs.3) | copy-start | bytes 196612
  3.3 9.6 %collective-permute-start.2 = (f32[264,256]{1,0:T(8,128)S(1)}, f32[264,256]{1,0:T(8,128)S(1)}, u32[]{:S(2)}, u32[]{:S(2)}) collective-permute-start(f32[264,256]{1,0:T(8,128)S(1)} %get-tuple-element.20), channel_id=1, source_target_pairs={{0,1},{2,3},{1,0},{3,2},{4,5},{6,7},{5,4},{7,6},{8,9},{10,11},{9,8... | collective-permute-start | bytes 811016 | tf_op jit(solution)/shard_map/ppermute | solution.py:73
  6.4 6.5 %collective-permute-start.3 = (f32[264,256]{1,0:T(8,128)S(1)}, f32[264,256]{1,0:T(8,128)S(1)}, u32[]{:S(2)}, u32[]{:S(2)}) collective-permute-start(f32[264,256]{1,0:T(8,128)S(1)} %get-tuple-element.21), channel_id=1, source_target_pairs={{1,2},{2,1},{5,6},{6,5},{9,10},{10,9},{13,14},{14,13},{17,18},{18,... | collective-permute-start | bytes 811016 | tf_op jit(solution)/shard_map/ppermute | solution.py:73
  7.1 5.8 %collective-permute-start = (f32[264,256]{1,0:T(8,128)S(1)}, f32[264,256]{1,0:T(8,128)S(1)}, u32[]{:S(2)}, u32[]{:S(2)}) collective-permute-start(f32[264,256]{1,0:T(8,128)S(1)} %get-tuple-element.18), channel_id=1, source_target_pairs={{0,4},{8,12},{16,20},{24,28},{4,0},{12,8},{20,16},{28,24},{1,5},{9... | collective-permute-start | bytes 811016 | tf_op jit(solution)/shard_map/ppermute | solution.py:73
  7.2 5.7 %collective-permute-start.1 = (f32[264,256]{1,0:T(8,128)S(1)}, f32[264,256]{1,0:T(8,128)S(1)}, u32[]{:S(2)}, u32[]{:S(2)}) collective-permute-start(f32[264,256]{1,0:T(8,128)S(1)} %get-tuple-element.19), channel_id=1, source_target_pairs={{4,8},{12,16},{20,24},{8,4},{16,12},{24,20},{5,9},{13,17},{21,25},... | collective-permute-start | bytes 811016 | tf_op jit(solution)/shard_map/ppermute | solution.py:73
  13.2 8.0 %collective-permute-start.4 = (f32[264,256]{1,0:T(8,128)S(1)}, f32[264,256]{1,0:T(8,128)S(1)}, u32[]{:S(2)}, u32[]{:S(2)}) collective-permute-start(f32[264,256]{1,0:T(8,128)S(1)} %get-tuple-element.24), channel_id=1, source_target_pairs={{4,0},{8,4},{12,8},{16,12},{20,16},{24,20},{28,24},{5,1},{9,5},{13... | collective-permute-start | bytes 811016 | tf_op jit(solution)/shard_map/ppermute | solution.py:67
  14.5 11.1 %collective-permute-start.5 = (f32[264,256]{1,0:T(8,128)S(1)}, f32[264,256]{1,0:T(8,128)S(1)}, u32[]{:S(2)}, u32[]{:S(2)}) collective-permute-start(f32[264,256]{1,0:T(8,128)S(1)} %get-tuple-element.25), channel_id=1, source_target_pairs={{1,0},{2,1},{3,2},{4,5},{5,6},{6,7},{9,8},{10,9},{11,10},{12,13},{... | collective-permute-start | bytes 811016 | tf_op jit(solution)/shard_map/ppermute | solution.py:489
  26.2 5.0 %collective-permute-start.6 = (f32[40,128]{1,0:T(8,128)S(1)}, f32[40,128]{1,0:T(8,128)S(1)}, u32[]{:S(2)}, u32[]{:S(2)}) collective-permute-start(f32[40,128]{1,0:T(8,128)S(1)} %shard_map.63), channel_id=1, source_target_pairs={{0,2},{1,3},{2,0},{3,1},{4,6},{5,7},{6,4},{7,5},{8,10},{9,11},{10,... | collective-permute-start | bytes 61448 | tf_op jit(solution)/shard_map/ppermute | solution.py:53
  31.2 7.0 %collective-permute-start.7 = (f32[40,128]{1,0:T(8,128)S(1)}, f32[40,128]{1,0:T(8,128)S(1)}, u32[]{:S(2)}, u32[]{:S(2)}) collective-permute-start(f32[40,128]{1,0:T(8,128)S(1)} %add.21), channel_id=1, source_target_pairs={{0,4},{1,5},{2,6},{3,7},{4,0},{5,1},{6,2},{7,3},{8,12},{9,13},{10,... | collective-permute-start | bytes 61448 | tf_op jit(solution)/shard_map/ppermute | solution.py:53
  33.9 6.1 %collective-permute-start.8 = (f32[40,128]{1,0:T(8,128)S(1)}, f32[40,128]{1,0:T(8,128)S(1)}, u32[]{:S(2)}, u32[]{:S(2)}) collective-permute-start(f32[40,128]{1,0:T(8,128)S(1)} %add.21), channel_id=1, source_target_pairs={{0,8},{1,9},{2,10},{3,11},{4,12},{5,13},{6,14},{7,15},{8,0},{9,1},... | collective-permute-start | bytes 61448 | tf_op jit(solution)/shard_map/ppermute | solution.py:53
  38.2 3.2 %collective-permute-start.9 = (f32[40,128]{1,0:T(8,128)S(1)}, f32[40,128]{1,0:T(8,128)S(1)}, u32[]{:S(2)}, u32[]{:S(2)}) collective-permute-start(f32[40,128]{1,0:T(8,128)S(1)} %add.21), channel_id=1, source_target_pairs={{0,12},{1,13},{2,14},{3,15},{4,8},{5,9},{6,10},{7,11},{8,4},{9,5},... | collective-permute-start | bytes 61448 | tf_op jit(solution)/shard_map/ppermute | solution.py:53
  41.4 4.0 %collective-permute-start.10 = (f32[40,128]{1,0:T(8,128)S(1)}, f32[40,128]{1,0:T(8,128)S(1)}, u32[]{:S(2)}, u32[]{:S(2)}) collective-permute-start(f32[40,128]{1,0:T(8,128)S(1)} %add_add_fusion.1), channel_id=1, source_target_pairs={{0,16},{1,17},{2,18},{3,19},{4,20},{5,21},{6,22},{7,23},{8,24},{9,... | collective-permute-start | bytes 61448 | tf_op jit(solution)/shard_map/ppermute | solution.py:53
  43.4 3.8 %collective-permute-start.11 = (f32[40,128]{1,0:T(8,128)S(1)}, f32[40,128]{1,0:T(8,128)S(1)}, u32[]{:S(2)}, u32[]{:S(2)}) collective-permute-start(f32[40,128]{1,0:T(8,128)S(1)} %add_add_fusion.1), channel_id=1, source_target_pairs={{0,1},{1,0},{2,3},{3,2},{4,5},{5,4},{6,7},{7,6},{8,9},{9,8},{10,11... | collective-permute-start | bytes 61448 | tf_op jit(solution)/shard_map/ppermute | solution.py:53
  45.4 4.7 %collective-permute-start.12 = (f32[40,128]{1,0:T(8,128)S(1)}, f32[40,128]{1,0:T(8,128)S(1)}, u32[]{:S(2)}, u32[]{:S(2)}) collective-permute-start(f32[40,128]{1,0:T(8,128)S(1)} %add_add_fusion.1), channel_id=1, source_target_pairs={{0,17},{1,16},{2,19},{3,18},{4,21},{5,20},{6,23},{7,22},{8,25},{9,... | collective-permute-start | bytes 61448 | tf_op jit(solution)/shard_map/ppermute | solution.py:53

commit v6 on v5

--- a/solution.py
+++ b/solution.py
@@ -85,29 +85,24 @@
     stack[pl.ds(0, count), lanes] = high
     stack[pl.ds(count, count), lanes] = low
     if extra is not None:
-        high, low = halves(extra)
-        row = lax.broadcasted_iota(jnp.int32, (EXTRA, deep), 0)
-        both = jnp.where(row == 0, high.astype(F32), jnp.where(row == 1, low.astype(F32), 0.0))
-        stack[pl.ds(2 * count, EXTRA), lanes] = both.astype(BF16)
+        stack[pl.ds(2 * count, EXTRA), lanes] = extra
 
 
 def by_rows(left, right):
     return lax.dot_general(left, right, (((1,), (1,)), ((), ())), preferred_element_type=F32)
 
 
-def fold_rows(full, count):
-    top = full[:count] + full[count : 2 * count]
-    if full.shape[0] == 2 * count:
-        return top
-    last = full[2 * count : 2 * count + 1] + full[2 * count + 1 : 2 * count + 2]
-    return jnp.concatenate([top, jnp.broadcast_to(last, (8, full.shape[1]))], axis=0)
-
-
-def fold(full, count):
-    rows = fold_rows(full, count)
-    body = rows[:, :count] + rows[:, count : 2 * count]
-    last = rows[:, 2 * count : 2 * count + 1] + rows[:, 2 * count + 1 : 2 * count + 2]
-    return body, last
+OF_RHS, OF_SCALED, OF_PAIR = 0, 2, 4
+
+
+def fold(full, count, left, right):
+    rows = full[:count] + full[count : 2 * count]
+    if left is not None:
+        at = 2 * count + left
+        last = full[at : at + 1] + full[at + 1 : at + 2]
+        rows = jnp.concatenate([rows, jnp.broadcast_to(last, (8, full.shape[1]))], axis=0)
+    at = 2 * count + right
+    return rows[:, :count] + rows[:, count : 2 * count], rows[:, at : at + 1] + rows[:, at + 1 : at + 2]
 
 
 def parity():
@@ -276,7 +271,7 @@
 
 def local_kernel(
     cols, inner, basis_stack, coeff, diag, rhs, xa, xb, ya, yb,
-    part, scaled_stack, value_stack, pair_stack, scaled, scale, upper, scaled_rhs,
+    part, scaled_stack, value_stack, pair_stack, scaled, scale, upper, scaled_rhs, ends,
 ):
     nx, ny, count, deep = cols.shape
     odd = parity()
@@ -287,28 +282,40 @@
         scale[x] = inverse
         scaled_rhs[x] = inverse * rhs[x]
         upper[x] = jnp.where(lane == deep - 1, 0.0, coeff[2, x])
+    level = lax.broadcasted_iota(jnp.int32, (ny, deep), 0)
+    for x in range(nx):
+        field = scaled_rhs[x]
+        pair = upper[x] * pltpu.roll(field, deep - 1, 1)
+        pair += jnp.where(level == ny - 1, 0.0, coeff[1, x] * pltpu.roll(field, ny - 1, 0))
+        if x + 1 < nx:
+            pair += coeff[0, x] * scaled_rhs[x + 1]
+        parts = []
+        for full in (rhs[x], field, pair):
+            high = full.astype(BF16).astype(F32)
+            parts += [high, full - high]
+        parts += [jnp.zeros_like(pair)] * 2
+        ends[x] = jnp.swapaxes(jnp.stack(parts), 0, 1)
+    blank = jnp.zeros((EXTRA - 8, deep), F32)
     for x in range(nx):
         for y in range(ny):
+            extra = jnp.concatenate([ends[x, y], blank], axis=0).astype(BF16)
             value = full_value(cols, inner, coeff, halo, x, y)
             result = value * row(scale, x, y)
             scaled[x, y] = result
-            put(value_stack, x * ny + y, value, row(rhs, x, y))
-            put(scaled_stack, x * ny + y, result, row(scaled_rhs, x, y))
+            put(value_stack, x * ny + y, value, extra)
+            put(scaled_stack, x * ny + y, result, extra)
     for x in range(nx):
         for y in range(ny):
-            over, ahead = row(upper, x, y), pltpu.roll(scaled[x, y], deep - 1, 1)
-            pair = over * ahead
-            pair_rhs = over * pltpu.roll(jnp.broadcast_to(row(scaled_rhs, x, y), (8, deep)), deep - 1, 1)[:1]
+            pair = row(upper, x, y) * pltpu.roll(scaled[x, y], deep - 1, 1)
             if x + 1 < nx:
                 pair += row(coeff, 0, x, y) * scaled[x + 1, y]
-                pair_rhs += row(coeff, 0, x, y) * row(scaled_rhs, x + 1, y)
             if y + 1 < ny:
                 pair += row(coeff, 1, x, y) * scaled[x, y + 1]
-                pair_rhs += row(coeff, 1, x, y) * row(scaled_rhs, x, y + 1)
-            put(pair_stack, x * ny + y, pair, pair_rhs)
-    gram, projected = fold(by_rows(basis_stack[...], value_stack[...]), count)
-    square, square_rhs = fold(by_rows(value_stack[...], scaled_stack[...]), count)
-    pairs, pairs_rhs = fold(by_rows(scaled_stack[...], pair_stack[...]), count)
+            extra = jnp.concatenate([ends[x, y], blank], axis=0).astype(BF16)
+            put(pair_stack, x * ny + y, pair, extra)
+    gram, projected = fold(by_rows(basis_stack[...], value_stack[...]), count, None, OF_RHS)
+    square, square_rhs = fold(by_rows(value_stack[...], scaled_stack[...]), count, OF_RHS, OF_SCALED)
+    pairs, pairs_rhs = fold(by_rows(scaled_stack[...], pair_stack[...]), count, OF_SCALED, OF_PAIR)
     part[...] = jnp.zeros_like(part)
     part[pl.ds(0, count), pl.ds(0, count)] = gram
     part[:, pl.ds(count, count)] = square
@@ -333,11 +340,19 @@
             pltpu.VMEM((tall, cells), BF16),
             pltpu.VMEM((nx, ny, count, deep), F32),
             small, small, small,
+            pltpu.VMEM((nx, ny, 8, deep), F32),
         ],
         limit=28,
         work=60 * count * cells,
         moved=24 * count * cells,
     )(cols, inner, basis_stack, coeff, diag, rhs, *halo)
+
+
+def pair_rows(field):
+    high = field.astype(BF16).astype(F32)
+    at = lax.broadcasted_iota(jnp.int32, (EXTRA, field.shape[1]), 0)
+    both = jnp.where(at == OF_PAIR, high, jnp.where(at == OF_PAIR + 1, field - high, 0.0))
+    return both.astype(BF16)
 
 
 def shared_kernel(part, scaled_stack, coeff, ya, yb, far_x, far_y, total, mine, pair_stack):
@@ -349,7 +364,7 @@
         face = row(coeff, 0, nx - 1, y)
         put(
             pair_stack, y, face * far_x[pl.ds(y * count, count), :],
-            face * far_x[pl.ds(ny * count + y, 1), :],
+            pair_rows(face * far_x[pl.ds(ny * count + y, 1), :]),
         )
         mine[:, pl.ds(y * deep, deep)] = scaled_stack[:, pl.ds(((nx - 1) * ny + y) * deep, deep)]
     for x in range(nx):
@@ -357,7 +372,7 @@
         face = jnp.where(odd[0] == 0, row(coeff, 1, x, ny - 1), own)
         put(
             pair_stack, ny + x, face * far_y[pl.ds(x * count, count), :],
-            face * far_y[pl.ds(nx * count + x, 1), :],
+            pair_rows(face * far_y[pl.ds(nx * count + x, 1), :]),
         )
 
     def side(y):
@@ -372,7 +387,7 @@
     def _():
         side(0)
 
-    pairs, pairs_rhs = fold(by_rows(mine[...], pair_stack[...]), count)
+    pairs, pairs_rhs = fold(by_rows(mine[...], pair_stack[...]), count, OF_SCALED, OF_PAIR)
     total[...] = part[...]
     total[:, pl.ds(2 * count, count)] += pairs
     total[:, pl.ds(3 * count + 2, 1)] += pairs_rhs
@@ -394,6 +409,13 @@
 def apply_two(matrix, first, second):
     a, b, c, d = matrix
     return a * first + b * second, c * first + d * second
+
+
+def output_rows(first, second, width):
+    at = lax.broadcasted_iota(jnp.int32, (EXTRA, width), 0)
+    both = jnp.where(at % 2 == 0, first, second)
+    high = both.astype(BF16).astype(F32)
+    return jnp.where(at < 2, high, jnp.where(at < 4, both - high, 0.0))
 
 
 def finish_kernel(total, basis_stack, scaled_stack, guess, stepped):
@@ -445,22 +467,18 @@
     ) + tail[:, at + 2 : at + 3]
     lost = jnp.sum(correction * shift_row, axis=1, keepdims=True)
     step = size / (size - 2.0 * crossing - lost)
-    first = lax.broadcasted_iota(jnp.int32, (EXTRA, count), 0)
-    of_basis = jnp.where(first == 0, weights_row, jnp.where(first == 1, weights_row - step * shift_row, 0.0))
-    of_scaled = jnp.where(first == 1, -step * weights_row, 0.0)
-    last = lax.broadcasted_iota(jnp.int32, (EXTRA, EXTRA), 0)
-    place = lax.broadcasted_iota(jnp.int32, (EXTRA, EXTRA), 1)
-    of_rhs = jnp.where((last == 1) & (place < 2), step, 0.0)
-    basis_high, basis_low = halves(jnp.concatenate([of_basis, of_basis], axis=1))
-    scaled_high, scaled_low = halves(jnp.concatenate([of_scaled, of_scaled, of_rhs], axis=1))
+    of_basis = output_rows(weights_row, weights_row - step * shift_row, count)
+    of_scaled = output_rows(jnp.zeros_like(weights_row), -step * weights_row, count)
+    place = lax.broadcasted_iota(jnp.int32, (1, EXTRA), 1)
+    of_rhs = jnp.where((place == OF_SCALED) | (place == OF_SCALED + 1), step, 0.0)
+    of_rhs = output_rows(jnp.zeros_like(of_rhs), of_rhs, EXTRA)
+    of_basis = jnp.concatenate([of_basis, of_basis], axis=1).astype(BF16)
+    of_scaled = jnp.concatenate([of_scaled, of_scaled, of_rhs], axis=1).astype(BF16)
     for x in range(nx):
         lanes = pl.ds(x * ny * deep, ny * deep)
-        fields = basis_stack[:, lanes]
-        result = jnp.dot(basis_high, fields, preferred_element_type=F32)
-        result += jnp.dot(basis_low, fields, preferred_element_type=F32)
-        fields = scaled_stack[:, lanes]
-        result += jnp.dot(scaled_high, fields, preferred_element_type=F32)
-        result += jnp.dot(scaled_low, fields, preferred_element_type=F32)
+        result = jnp.dot(of_basis, basis_stack[:, lanes], preferred_element_type=F32)
+        result += jnp.dot(of_scaled, scaled_stack[:, lanes], preferred_element_type=F32)
+        result = result[0:2] + result[2:4]
         for y in range(ny):
             guess[x, pl.ds(y, 1), :] = result[0:1, y * deep : (y + 1) * deep]
             stepped[x, pl.ds(y, 1), :] = result[1:2, y * deep : (y + 1) * deep]

time: 54.1 us -> 53.4 us (0.987)
  Pallas kernels: 11.6 us -> 10.7 us
    pallas_call x1, Pallas kernels: 3.72 us -> 3.09 us  [finish(): call(finish_kernel, (shape(*block),) * 2, [VM] * 3, limit=24)]
  transfers between devices with their start and end apart: 13 -> 13, of which waited for: 8 -> 8; matrix products, arithmetic and copies ran while one was open for 0% -> 0% of each run, Pallas kernels for 10% -> 9%
where the time goes in v6:
time: 53.4 us; the launch traced here: 53.2 us
  starting transfers between devices  21.4 us (40%)
  waiting for transfers between devices  19.4 us (36%)
  Pallas kernels  10.7 us (20%)
  local copies, waits for them, and re-layouts  0.93 us (2%)
  between operations  0.75 us (1%)
    ppermute x7, starting transfers between devices, sum_all(): lax.ppermute(part, ('gx', 'gy'), [(i * deep + j, (i ^ a) * deep + (j ^ b)...  14.2 us
    ppermute x7, waiting for transfers between devices, sum_all(): lax.ppermute(part, ('gx', 'gy'), [(i * deep + j, (i ^ a) * deep + (j ^ b)...  9.6 us
    ppermute x4, starting transfers between devices, swap(): return lax.ppermute(block, axis, pairs + [(j, i) for i, j in pairs])  4.53 us
    ppermute x1, waiting for transfers between devices, steps(): far_y = lax.ppermute(face_y, ('gx', 'gy'), route)  4.36 us
    pallas_call x1, Pallas kernels, finish(): call(finish_kernel, (shape(*block),) * 2, [VM] * 3, limit=24)  3.09 us
    ppermute x4, waiting for transfers between devices, swap(): return lax.ppermute(block, axis, pairs + [(j, i) for i, j in pairs])  2.95 us
    pallas_call x1, Pallas kernels, local_sums(): call(local_kernel, outs, [VM] * 10, [pltpu.VMEM((tall, cells), BF16), plt...  2.92 us
    ppermute x1, waiting for transfers between devices, send(): lax.ppermute(block, axis, [(i, i + step) for i in range(size) if 0 <= i +...  2.5 us
  transfers between devices with their start and end apart: 13, of which 8 were waited for; matrix products, arithmetic and copies ran while one was open for 0% of the time, Pallas kernels for 9%

profile of v6, /device:TPU:0, one launch (start us, length us, event | category | flops | bytes accessed | tf_op | source)
XLA Modules:
  0.0 53.2 jit_solution(13319401395783109461)
XLA Ops:
  0.6 0.9 %copy-done = f32[3,8,8,256]{3,2,1,0:T(8,128)S(1)} copy-done((f32[3,8,8,256]{3,2,1,0:T(8,128)S(1)}, f32[3,8,8,256]{3,2,1,0:T(8,128)}, u32[]{:S(2)}) %copy-start) | copy-done | bytes 196632
  1.6 1.8 %shard_map.59 = (f32[264,256]{1,0:T(8,128)S(1)}, f32[264,256]{1,0:T(8,128)S(1)}, f32[264,256]{1,0:T(8,128)S(1)}, f32[264,256]{1,0:T(8,128)S(1)}, f32[8,8,32,256]{3,2,1,0:T(8,128)S(1)}) custom-call(f32[32,8,8,256]{3,2,1,0:T(8,128)} %basis.1, f32[3,8,8,256]{3,2,1,0:T(8,128)S(1)} %copy-done), custom_call_target="tpu_custom_call" | custom-call | tf_op jit(solution)/shard_map/pallas_call | solution.py:145
  3.3 3.1 %collective-permute-start.2 = (f32[264,256]{1,0:T(8,128)S(1)}, f32[264,256]{1,0:T(8,128)S(1)}, u32[]{:S(2)}, u32[]{:S(2)}) collective-permute-start(f32[264,256]{1,0:T(8,128)S(1)} %get-tuple-element.20), channel_id=1, source_target_pairs={{0,1},{2,3},{1,0},{3,2},{4,5},{6,7},{5,4},{7,6},{8,9},{10,11},{9,8... | collective-permute-start | bytes 811016 | tf_op jit(solution)/shard_map/ppermute | solution.py:73
  6.4 0.7 %collective-permute-start.3 = (f32[264,256]{1,0:T(8,128)S(1)}, f32[264,256]{1,0:T(8,128)S(1)}, u32[]{:S(2)}, u32[]{:S(2)}) collective-permute-start(f32[264,256]{1,0:T(8,128)S(1)} %get-tuple-element.21), channel_id=1, source_target_pairs={{1,2},{2,1},{5,6},{6,5},{9,10},{10,9},{13,14},{14,13},{17,18},{18,... | collective-permute-start | bytes 811016 | tf_op jit(solution)/shard_map/ppermute | solution.py:73
  7.2 0.7 %collective-permute-start.1 = (f32[264,256]{1,0:T(8,128)S(1)}, f32[264,256]{1,0:T(8,128)S(1)}, u32[]{:S(2)}, u32[]{:S(2)}) collective-permute-start(f32[264,256]{1,0:T(8,128)S(1)} %get-tuple-element.19), channel_id=1, source_target_pairs={{4,8},{12,16},{20,24},{8,4},{16,12},{24,20},{5,9},{13,17},{21,25},... | collective-permute-start | bytes 811016 | tf_op jit(solution)/shard_map/ppermute | solution.py:73
  7.9 2.1 %shard_map.60 = (f32[8,8,32,256]{3,2,1,0:T(8,128)S(1)}, bf16[64,16384]{1,0:T(8,128)(2,1)S(1)}, f32[8,8,256]{2,1,0:T(8,128)S(1)}) custom-call(f32[8,8,32,256]{3,2,1,0:T(8,128)S(1)} %get-tuple-element.14.cols, f32[3,8,8,256]{3,2,1,0:T(8,128)S(1)} %copy-done, f32[8,8,256]{2,1,0:T(8,128)S(1)} %copy-done.2), custom_call_target="tpu_custom_call" | custom-call | flops 10485760 | bytes 8388608 | tf_op jit(solution)/shard_map/pallas_call | solution.py:199
  10.0 2.9 %collective-permute-done.2.ya = f32[264,256]{1,0:T(8,128)S(1)} collective-permute-done((f32[264,256]{1,0:T(8,128)S(1)}, f32[264,256]{1,0:T(8,128)S(1)}, u32[]{:S(2)}, u32[]{:S(2)}) %collective-permute-start.2) | collective-permute-done | bytes 270368 | tf_op jit(solution)/shard_map/ppermute | solution.py:73
  13.2 1.3 %collective-permute-start.4 = (f32[264,256]{1,0:T(8,128)S(1)}, f32[264,256]{1,0:T(8,128)S(1)}, u32[]{:S(2)}, u32[]{:S(2)}) collective-permute-start(f32[264,256]{1,0:T(8,128)S(1)} %get-tuple-element.24), channel_id=1, source_target_pairs={{4,0},{8,4},{12,8},{16,12},{20,16},{24,20},{28,24},{5,1},{9,5},{13... | collective-permute-start | bytes 811016 | tf_op jit(solution)/shard_map/ppermute | solution.py:67
  14.5 1.3 %collective-permute-start.5 = (f32[264,256]{1,0:T(8,128)S(1)}, f32[264,256]{1,0:T(8,128)S(1)}, u32[]{:S(2)}, u32[]{:S(2)}) collective-permute-start(f32[264,256]{1,0:T(8,128)S(1)} %get-tuple-element.25), channel_id=1, source_target_pairs={{1,0},{2,1},{3,2},{4,5},{5,6},{6,7},{9,8},{10,9},{11,10},{12,13},{... | collective-permute-start | bytes 811016 | tf_op jit(solution)/shard_map/ppermute | solution.py:507
  15.8 2.9 %shard_map.61 = (f32[40,128]{1,0:T(8,128)S(1)}, bf16[80,16384]{1,0:T(8,128)(2,1)S(1)}) custom-call(f32[8,8,32,256]{3,2,1,0:T(8,128)S(1)} %get-tuple-element.14.cols, f32[8,8,32,256]{3,2,1,0:T(8,128)S(1)} %get-tuple-element.15.inner, bf16[64,16384]{1,0:T(8,128)(2,1)S(1)} %get-tuple-element.16.basis_stack, f32[3,8,8,256]{3,2,1,0:T(8,128)S(1)} %copy-done, ...), custom_call_target="tpu_custom_call" | custom-call | flops 31457280 | bytes 12582912 | tf_op jit(solution)/shard_map/pallas_call | solution.py:334
  18.7 2.5 %collective-permute-done.4.far_x = f32[264,256]{1,0:T(8,128)S(1)} collective-permute-done((f32[264,256]{1,0:T(8,128)S(1)}, f32[264,256]{1,0:T(8,128)S(1)}, u32[]{:S(2)}, u32[]{:S(2)}) %collective-permute-start.4) | collective-permute-done | bytes 270368 | tf_op jit(solution)/shard_map/ppermute | solution.py:67
  21.2 4.4 %collective-permute-done.5.far_y = f32[264,256]{1,0:T(8,128)S(1)} collective-permute-done((f32[264,256]{1,0:T(8,128)S(1)}, f32[264,256]{1,0:T(8,128)S(1)}, u32[]{:S(2)}, u32[]{:S(2)}) %collective-permute-start.5) | collective-permute-done | bytes 270368 | tf_op jit(solution)/shard_map/ppermute | solution.py:507
  25.6 0.7 %shard_map.63 = f32[40,128]{1,0:T(8,128)S(1)} custom-call(f32[40,128]{1,0:T(8,128)S(1)} %get-tuple-element.22.part, bf16[80,16384]{1,0:T(8,128)(2,1)S(1)} %get-tuple-element.23.scaled_stack, f32[3,8,8,256]{3,2,1,0:T(8,128)S(1)} %copy-done, f32[264,256]{1,0:T(8,128)S(1)} %collective-permute-done.2.ya, f32[264,256]{1,0:T(8,128)S(1)} %collective-permute-done.3.yb, ...), custom_call_target="tpu_custom_call" | custom-call | tf_op jit(solution)/shard_map/pallas_call | solution.py:399
  26.2 3.2 %collective-permute-start.6 = (f32[40,128]{1,0:T(8,128)S(1)}, f32[40,128]{1,0:T(8,128)S(1)}, u32[]{:S(2)}, u32[]{:S(2)}) collective-permute-start(f32[40,128]{1,0:T(8,128)S(1)} %shard_map.63), channel_id=1, source_target_pairs={{0,2},{1,3},{2,0},{3,1},{4,6},{5,7},{6,4},{7,5},{8,10},{9,11},{10,... | collective-permute-start | bytes 61448 | tf_op jit(solution)/shard_map/ppermute | solution.py:53
  29.5 1.8 %collective-permute-done.6 = f32[40,128]{1,0:T(8,128)S(1)} collective-permute-done((f32[40,128]{1,0:T(8,128)S(1)}, f32[40,128]{1,0:T(8,128)S(1)}, u32[]{:S(2)}, u32[]{:S(2)}) %collective-permute-start.6) | collective-permute-done | bytes 20512 | tf_op jit(solution)/shard_map/ppermute | solution.py:53
  31.2 2.6 %collective-permute-start.7 = (f32[40,128]{1,0:T(8,128)S(1)}, f32[40,128]{1,0:T(8,128)S(1)}, u32[]{:S(2)}, u32[]{:S(2)}) collective-permute-start(f32[40,128]{1,0:T(8,128)S(1)} %add.21), channel_id=1, source_target_pairs={{0,4},{1,5},{2,6},{3,7},{4,0},{5,1},{6,2},{7,3},{8,12},{9,13},{10,... | collective-permute-start | bytes 61448 | tf_op jit(solution)/shard_map/ppermute | solution.py:53
  33.8 4.4 %collective-permute-start.8 = (f32[40,128]{1,0:T(8,128)S(1)}, f32[40,128]{1,0:T(8,128)S(1)}, u32[]{:S(2)}, u32[]{:S(2)}) collective-permute-start(f32[40,128]{1,0:T(8,128)S(1)} %add.21), channel_id=1, source_target_pairs={{0,8},{1,9},{2,10},{3,11},{4,12},{5,13},{6,14},{7,15},{8,0},{9,1},... | collective-permute-start | bytes 61448 | tf_op jit(solution)/shard_map/ppermute | solution.py:53
  38.3 1.7 %collective-permute-done.8 = f32[40,128]{1,0:T(8,128)S(1)} collective-permute-done((f32[40,128]{1,0:T(8,128)S(1)}, f32[40,128]{1,0:T(8,128)S(1)}, u32[]{:S(2)}, u32[]{:S(2)}) %collective-permute-start.8) | collective-permute-done | bytes 20512 | tf_op jit(solution)/shard_map/ppermute | solution.py:53
  40.0 1.4 %collective-permute-done.9 = f32[40,128]{1,0:T(8,128)S(1)} collective-permute-done((f32[40,128]{1,0:T(8,128)S(1)}, f32[40,128]{1,0:T(8,128)S(1)}, u32[]{:S(2)}, u32[]{:S(2)}) %collective-permute-start.9) | collective-permute-done | bytes 20512 | tf_op jit(solution)/shard_map/ppermute | solution.py:53
  41.4 1.9 %collective-permute-start.10 = (f32[40,128]{1,0:T(8,128)S(1)}, f32[40,128]{1,0:T(8,128)S(1)}, u32[]{:S(2)}, u32[]{:S(2)}) collective-permute-start(f32[40,128]{1,0:T(8,128)S(1)} %add_add_fusion.1), channel_id=1, source_target_pairs={{0,16},{1,17},{2,18},{3,19},{4,20},{5,21},{6,22},{7,23},{8,24},{9,... | collective-permute-start | bytes 61448 | tf_op jit(solution)/shard_map/ppermute | solution.py:53
  43.4 2.0 %collective-permute-start.11 = (f32[40,128]{1,0:T(8,128)S(1)}, f32[40,128]{1,0:T(8,128)S(1)}, u32[]{:S(2)}, u32[]{:S(2)}) collective-permute-start(f32[40,128]{1,0:T(8,128)S(1)} %add_add_fusion.1), channel_id=1, source_target_pairs={{0,1},{1,0},{2,3},{3,2},{4,5},{5,4},{6,7},{7,6},{8,9},{9,8},{10,11... | collective-permute-start | bytes 61448 | tf_op jit(solution)/shard_map/ppermute | solution.py:53
  45.4 1.8 %collective-permute-done.11 = f32[40,128]{1,0:T(8,128)S(1)} collective-permute-done((f32[40,128]{1,0:T(8,128)S(1)}, f32[40,128]{1,0:T(8,128)S(1)}, u32[]{:S(2)}, u32[]{:S(2)}) %collective-permute-start.11) | collective-permute-done | bytes 20512 | tf_op jit(solution)/shard_map/ppermute | solution.py:53
  47.2 2.9 %collective-permute-done.12 = f32[40,128]{1,0:T(8,128)S(1)} collective-permute-done((f32[40,128]{1,0:T(8,128)S(1)}, f32[40,128]{1,0:T(8,128)S(1)}, u32[]{:S(2)}, u32[]{:S(2)}) %collective-permute-start.12) | collective-permute-done | bytes 20512 | tf_op jit(solution)/shard_map/ppermute | solution.py:53
  50.1 3.1 %shard_map.64 = (f32[8,8,256]{2,1,0:T(8,128)}, f32[8,8,256]{2,1,0:T(8,128)}) custom-call(f32[40,128]{1,0:T(8,128)S(1)} %add_add_fusion.total, bf16[64,16384]{1,0:T(8,128)(2,1)S(1)} %get-tuple-element.16.basis_stack, bf16[80,16384]{1,0:T(8,128)(2,1)S(1)} %get-tuple-element.23.scaled_stack), custom_call_target="tpu_custom_call" | custom-call | tf_op jit(solution)/shard_map/pallas_call | solution.py:488
  (17 shorter events, 0.4 us)
Async XLA Ops:
  0.6 0.9 %copy-start = (f32[3,8,8,256]{3,2,1,0:T(8,128)S(1)}, f32[3,8,8,256]{3,2,1,0:T(8,128)}, u32[]{:S(2)}) copy-start(f32[3,8,8,256]{3,2,1,0:T(8,128)} %coeff.9) | copy-start | bytes 589828
  1.6 6.3 %copy-start.2 = (f32[8,8,256]{2,1,0:T(8,128)S(1)}, f32[8,8,256]{2,1,0:T(8,128)}, u32[]{:S(2)}) copy-start(f32[8,8,256]{2,1,0:T(8,128)} %extra_raw.1) | copy-start | bytes 196612
  1.6 11.4 %copy-start.1 = (f32[8,8,256]{2,1,0:T(8,128)S(1)}, f32[8,8,256]{2,1,0:T(8,128)}, u32[]{:S(2)}) copy-start(f32[8,8,256]{2,1,0:T(8,128)} %rhs.3) | copy-start | bytes 196612
  3.3 9.6 %collective-permute-start.2 = (f32[264,256]{1,0:T(8,128)S(1)}, f32[264,256]{1,0:T(8,128)S(1)}, u32[]{:S(2)}, u32[]{:S(2)}) collective-permute-start(f32[264,256]{1,0:T(8,128)S(1)} %get-tuple-element.20), channel_id=1, source_target_pairs={{0,1},{2,3},{1,0},{3,2},{4,5},{6,7},{5,4},{7,6},{8,9},{10,11},{9,8... | collective-permute-start | bytes 811016 | tf_op jit(solution)/shard_map/ppermute | solution.py:73
  6.4 6.5 %collective-permute-start.3 = (f32[264,256]{1,0:T(8,128)S(1)}, f32[264,256]{1,0:T(8,128)S(1)}, u32[]{:S(2)}, u32[]{:S(2)}) collective-permute-start(f32[264,256]{1,0:T(8,128)S(1)} %get-tuple-element.21), channel_id=1, source_target_pairs={{1,2},{2,1},{5,6},{6,5},{9,10},{10,9},{13,14},{14,13},{17,18},{18,... | collective-permute-start | bytes 811016 | tf_op jit(solution)/shard_map/ppermute | solution.py:73
  7.1 5.8 %collective-permute-start = (f32[264,256]{1,0:T(8,128)S(1)}, f32[264,256]{1,0:T(8,128)S(1)}, u32[]{:S(2)}, u32[]{:S(2)}) collective-permute-start(f32[264,256]{1,0:T(8,128)S(1)} %get-tuple-element.18), channel_id=1, source_target_pairs={{0,4},{8,12},{16,20},{24,28},{4,0},{12,8},{20,16},{28,24},{1,5},{9... | collective-permute-start | bytes 811016 | tf_op jit(solution)/shard_map/ppermute | solution.py:73
  7.2 5.7 %collective-permute-start.1 = (f32[264,256]{1,0:T(8,128)S(1)}, f32[264,256]{1,0:T(8,128)S(1)}, u32[]{:S(2)}, u32[]{:S(2)}) collective-permute-start(f32[264,256]{1,0:T(8,128)S(1)} %get-tuple-element.19), channel_id=1, source_target_pairs={{4,8},{12,16},{20,24},{8,4},{16,12},{24,20},{5,9},{13,17},{21,25},... | collective-permute-start | bytes 811016 | tf_op jit(solution)/shard_map/ppermute | solution.py:73
  13.2 8.0 %collective-permute-start.4 = (f32[264,256]{1,0:T(8,128)S(1)}, f32[264,256]{1,0:T(8,128)S(1)}, u32[]{:S(2)}, u32[]{:S(2)}) collective-permute-start(f32[264,256]{1,0:T(8,128)S(1)} %get-tuple-element.24), channel_id=1, source_target_pairs={{4,0},{8,4},{12,8},{16,12},{20,16},{24,20},{28,24},{5,1},{9,5},{13... | collective-permute-start | bytes 811016 | tf_op jit(solution)/shard_map/ppermute | solution.py:67
  14.5 11.1 %collective-permute-start.5 = (f32[264,256]{1,0:T(8,128)S(1)}, f32[264,256]{1,0:T(8,128)S(1)}, u32[]{:S(2)}, u32[]{:S(2)}) collective-permute-start(f32[264,256]{1,0:T(8,128)S(1)} %get-tuple-element.25), channel_id=1, source_target_pairs={{1,0},{2,1},{3,2},{4,5},{5,6},{6,7},{9,8},{10,9},{11,10},{12,13},{... | collective-permute-start | bytes 811016 | tf_op jit(solution)/shard_map/ppermute | solution.py:507
  26.2 5.0 %collective-permute-start.6 = (f32[40,128]{1,0:T(8,128)S(1)}, f32[40,128]{1,0:T(8,128)S(1)}, u32[]{:S(2)}, u32[]{:S(2)}) collective-permute-start(f32[40,128]{1,0:T(8,128)S(1)} %shard_map.63), channel_id=1, source_target_pairs={{0,2},{1,3},{2,0},{3,1},{4,6},{5,7},{6,4},{7,5},{8,10},{9,11},{10,... | collective-permute-start | bytes 61448 | tf_op jit(solution)/shard_map/ppermute | solution.py:53
  31.2 7.0 %collective-permute-start.7 = (f32[40,128]{1,0:T(8,128)S(1)}, f32[40,128]{1,0:T(8,128)S(1)}, u32[]{:S(2)}, u32[]{:S(2)}) collective-permute-start(f32[40,128]{1,0:T(8,128)S(1)} %add.21), channel_id=1, source_target_pairs={{0,4},{1,5},{2,6},{3,7},{4,0},{5,1},{6,2},{7,3},{8,12},{9,13},{10,... | collective-permute-start | bytes 61448 | tf_op jit(solution)/shard_map/ppermute | solution.py:53
  33.8 6.1 %collective-permute-start.8 = (f32[40,128]{1,0:T(8,128)S(1)}, f32[40,128]{1,0:T(8,128)S(1)}, u32[]{:S(2)}, u32[]{:S(2)}) collective-permute-start(f32[40,128]{1,0:T(8,128)S(1)} %add.21), channel_id=1, source_target_pairs={{0,8},{1,9},{2,10},{3,11},{4,12},{5,13},{6,14},{7,15},{8,0},{9,1},... | collective-permute-start | bytes 61448 | tf_op jit(solution)/shard_map/ppermute | solution.py:53
  38.2 3.2 %collective-permute-start.9 = (f32[40,128]{1,0:T(8,128)S(1)}, f32[40,128]{1,0:T(8,128)S(1)}, u32[]{:S(2)}, u32[]{:S(2)}) collective-permute-start(f32[40,128]{1,0:T(8,128)S(1)} %add.21), channel_id=1, source_target_pairs={{0,12},{1,13},{2,14},{3,15},{4,8},{5,9},{6,10},{7,11},{8,4},{9,5},... | collective-permute-start | bytes 61448 | tf_op jit(solution)/shard_map/ppermute | solution.py:53
  41.4 4.0 %collective-permute-start.10 = (f32[40,128]{1,0:T(8,128)S(1)}, f32[40,128]{1,0:T(8,128)S(1)}, u32[]{:S(2)}, u32[]{:S(2)}) collective-permute-start(f32[40,128]{1,0:T(8,128)S(1)} %add_add_fusion.1), channel_id=1, source_target_pairs={{0,16},{1,17},{2,18},{3,19},{4,20},{5,21},{6,22},{7,23},{8,24},{9,... | collective-permute-start | bytes 61448 | tf_op jit(solution)/shard_map/ppermute | solution.py:53
  43.4 3.8 %collective-permute-start.11 = (f32[40,128]{1,0:T(8,128)S(1)}, f32[40,128]{1,0:T(8,128)S(1)}, u32[]{:S(2)}, u32[]{:S(2)}) collective-permute-start(f32[40,128]{1,0:T(8,128)S(1)} %add_add_fusion.1), channel_id=1, source_target_pairs={{0,1},{1,0},{2,3},{3,2},{4,5},{5,4},{6,7},{7,6},{8,9},{9,8},{10,11... | collective-permute-start | bytes 61448 | tf_op jit(solution)/shard_map/ppermute | solution.py:53
  45.4 4.7 %collective-permute-start.12 = (f32[40,128]{1,0:T(8,128)S(1)}, f32[40,128]{1,0:T(8,128)S(1)}, u32[]{:S(2)}, u32[]{:S(2)}) collective-permute-start(f32[40,128]{1,0:T(8,128)S(1)} %add_add_fusion.1), channel_id=1, source_target_pairs={{0,17},{1,16},{2,19},{3,18},{4,21},{5,20},{6,23},{7,22},{8,25},{9,... | collective-permute-start | bytes 61448 | tf_op jit(solution)/shard_map/ppermute | solution.py:53

commit v7 on v6

--- a/solution.py
+++ b/solution.py
@@ -155,7 +155,30 @@
     return upper * above + lower * below
 
 
-def inner_kernel(cols, coeff, extra_raw, inner, stack, diag, upper, lower, ahead, behind, extra, sem):
+def outer_columns(nx, ny):
+    ends = [(x, y) for x in range(1, nx - 1) for y in (0, ny - 1)]
+    return [(x, y) for x in (0, nx - 1) for y in range(ny)] + ends
+
+
+def end_rows(fields):
+    parts = []
+    for full in fields:
+        high = full.astype(BF16).astype(F32)
+        parts += [high, full - high]
+    parts += [jnp.zeros_like(parts[0])] * (8 - len(parts))
+    return jnp.swapaxes(jnp.stack(parts), 0, 1)
+
+
+def end_block(rows):
+    blank = jnp.zeros((EXTRA - rows.shape[0], rows.shape[1]), F32)
+    return jnp.concatenate([rows, blank], axis=0).astype(BF16)
+
+
+def inner_kernel(
+    cols, coeff, rhs, extra_raw,
+    inner, inside_basis, outside_basis, inside_scaled, scaled, diag, gram, square,
+    upper, lower, ahead, behind, extra, ends, inside_value, sem,
+):
     nx, ny, _, deep = cols.shape
     extra_copy = pltpu.make_async_copy(extra_raw, extra, sem)
     extra_copy.start()
@@ -185,21 +208,56 @@
             if y:
                 sums += row(coeff, 1, x, y - 1) * cols[x, y - 1]
             inner[x, y] = row(diag, x, y) * here - sums
-            put(stack, x * ny + y, here)
         return carry
 
+    def middle(x, carry):
+        scale = 1.0 / diag[x]
+        ends[...] = end_rows((rhs[x], scale * rhs[x]))
+        behind[x] = scale
+        for y in range(1, ny - 1):
+            at = (x - 1) * (ny - 2) + y - 1
+            block = end_block(ends[y])
+            value = inner[x, y]
+            result = value * row(behind, x, y)
+            scaled[x, y] = result
+            put(inside_basis, at, cols[x, y])
+            put(inside_value, at, value, block)
+            put(inside_scaled, at, result, block)
+        return carry
+
     lax.fori_loop(0, nx, slab, 0)
-
-
-def inside(cols, coeff, extra):
+    lax.fori_loop(1, nx - 1, middle, 0)
+    for at, (x, y) in enumerate(outer_columns(nx, ny)):
+        put(outside_basis, at, cols[x, y])
+    gram[...] = by_rows(inside_basis[...], inside_value[...])
+    square[...] = by_rows(inside_value[...], inside_scaled[...])
+
+
+def inside(cols, coeff, rhs, extra):
     nx, ny, count, deep = cols.shape
     cells = nx * ny * deep
-    outs = (shape(nx, ny, count, deep), shape(2 * count, cells, dtype=BF16), shape(nx, ny, deep))
+    tall = 2 * count + EXTRA
+    outer = len(outer_columns(nx, ny)) * deep
+    full = shape(nx, ny, count, deep)
+    outs = (
+        full,
+        shape(2 * count, cells - outer, dtype=BF16),
+        shape(2 * count, outer, dtype=BF16),
+        shape(tall, cells - outer, dtype=BF16),
+        full,
+        shape(nx, ny, deep),
+        shape(2 * count, tall),
+        shape(tall, tall),
+    )
     small = pltpu.VMEM((nx, ny, deep), F32)
+    scratch = [small] * 5 + [
+        pltpu.VMEM((ny, 8, deep), F32),
+        pltpu.VMEM((tall, cells - outer), BF16),
+        pltpu.SemaphoreType.DMA,
+    ]
     return call(
-        inner_kernel, outs, [VM, VM, RAW], [small] * 5 + [pltpu.SemaphoreType.DMA],
-        work=20 * count * cells, moved=16 * count * cells,
-    )(cols, coeff, extra)
+        inner_kernel, outs, [VM, VM, VM, RAW], scratch, work=60 * count * cells, moved=24 * count * cells
+    )(cols, coeff, rhs, extra)
 
 
 class Halo:
@@ -270,52 +328,56 @@
 
 
 def local_kernel(
-    cols, inner, basis_stack, coeff, diag, rhs, xa, xb, ya, yb,
-    part, scaled_stack, value_stack, pair_stack, scaled, scale, upper, scaled_rhs, ends,
+    cols, inner, outside_basis, inside_scaled, scaled, gram_in, square_in, coeff, diag, rhs, xa, xb, ya, yb,
+    part, outside_scaled, outside_value, inside_pair, outside_pair, border, scale, upper, scaled_rhs, ends,
 ):
     nx, ny, count, deep = cols.shape
     odd = parity()
     halo = Halo(odd, (xa, xb, ya, yb))
     lane = lax.broadcasted_iota(jnp.int32, (ny, deep), 1)
+    level = lax.broadcasted_iota(jnp.int32, (ny, deep), 0)
     for x in range(nx):
         inverse = inverse_diagonal(diag, halo, count, x)
         scale[x] = inverse
         scaled_rhs[x] = inverse * rhs[x]
         upper[x] = jnp.where(lane == deep - 1, 0.0, coeff[2, x])
-    level = lax.broadcasted_iota(jnp.int32, (ny, deep), 0)
     for x in range(nx):
         field = scaled_rhs[x]
         pair = upper[x] * pltpu.roll(field, deep - 1, 1)
         pair += jnp.where(level == ny - 1, 0.0, coeff[1, x] * pltpu.roll(field, ny - 1, 0))
         if x + 1 < nx:
             pair += coeff[0, x] * scaled_rhs[x + 1]
-        parts = []
-        for full in (rhs[x], field, pair):
-            high = full.astype(BF16).astype(F32)
-            parts += [high, full - high]
-        parts += [jnp.zeros_like(pair)] * 2
-        ends[x] = jnp.swapaxes(jnp.stack(parts), 0, 1)
-    blank = jnp.zeros((EXTRA - 8, deep), F32)
+        ends[x] = end_rows((rhs[x], field, pair))
+    outer = {place: at for at, place in enumerate(outer_columns(nx, ny))}
+    for (x, y), at in outer.items():
+        block = end_block(ends[x, y])
+        value = full_value(cols, inner, coeff, halo, x, y)
+        result = value * row(scale, x, y)
+        border[at] = result
+        put(outside_value, at, value, block)
+        put(outside_scaled, at, result, block)
+
+    def field_at(x, y):
+        return border[outer[x, y]] if (x, y) in outer else scaled[x, y]
+
     for x in range(nx):
         for y in range(ny):
-            extra = jnp.concatenate([ends[x, y], blank], axis=0).astype(BF16)
-            value = full_value(cols, inner, coeff, halo, x, y)
-            result = value * row(scale, x, y)
-            scaled[x, y] = result
-            put(value_stack, x * ny + y, value, extra)
-            put(scaled_stack, x * ny + y, result, extra)
-    for x in range(nx):
-        for y in range(ny):
-            pair = row(upper, x, y) * pltpu.roll(scaled[x, y], deep - 1, 1)
+            pair = row(upper, x, y) * pltpu.roll(field_at(x, y), deep - 1, 1)
             if x + 1 < nx:
-                pair += row(coeff, 0, x, y) * scaled[x + 1, y]
+                pair += row(coeff, 0, x, y) * field_at(x + 1, y)
             if y + 1 < ny:
-                pair += row(coeff, 1, x, y) * scaled[x, y + 1]
-            extra = jnp.concatenate([ends[x, y], blank], axis=0).astype(BF16)
-            put(pair_stack, x * ny + y, pair, extra)
-    gram, projected = fold(by_rows(basis_stack[...], value_stack[...]), count, None, OF_RHS)
-    square, square_rhs = fold(by_rows(value_stack[...], scaled_stack[...]), count, OF_RHS, OF_SCALED)
-    pairs, pairs_rhs = fold(by_rows(scaled_stack[...], pair_stack[...]), count, OF_SCALED, OF_PAIR)
+                pair += row(coeff, 1, x, y) * field_at(x, y + 1)
+            block = end_block(ends[x, y])
+            if (x, y) in outer:
+                put(outside_pair, outer[x, y], pair, block)
+            else:
+                put(inside_pair, (x - 1) * (ny - 2) + y - 1, pair, block)
+    gram = gram_in[...] + by_rows(outside_basis[...], outside_value[...])
+    gram, projected = fold(gram, count, None, OF_RHS)
+    square = square_in[...] + by_rows(outside_value[...], outside_scaled[...])
+    square, square_rhs = fold(square, count, OF_RHS, OF_SCALED)
+    pairs = by_rows(inside_scaled[...], inside_pair[...]) + by_rows(outside_scaled[...], outside_pair[...])
+    pairs, pairs_rhs = fold(pairs, count, OF_SCALED, OF_PAIR)
     part[...] = jnp.zeros_like(part)
     part[pl.ds(0, count), pl.ds(0, count)] = gram
     part[:, pl.ds(count, count)] = square
@@ -325,27 +387,30 @@
     part[:, pl.ds(3 * count + 2, 1)] = pairs_rhs
 
 
-def local_sums(cols, inner, basis_stack, coeff, diag, rhs, halo):
+def local_sums(cols, inner, outside_basis, inside_scaled, scaled, gram, square, coeff, diag, rhs, halo):
     nx, ny, count, deep = cols.shape
     cells = nx * ny * deep
     tall = 2 * count + EXTRA
+    columns = len(outer_columns(nx, ny))
+    outer = columns * deep
     small = pltpu.VMEM((nx, ny, deep), F32)
-    outs = (shape(count + 8, -(-(3 * count + 3) // LANES) * LANES), shape(tall, cells, dtype=BF16))
+    width = -(-(3 * count + 3) // LANES) * LANES
     return call(
         local_kernel,
-        outs,
-        [VM] * 10,
+        (shape(count + 8, width), shape(tall, outer, dtype=BF16)),
+        [VM] * 14,
         [
-            pltpu.VMEM((tall, cells), BF16),
-            pltpu.VMEM((tall, cells), BF16),
-            pltpu.VMEM((nx, ny, count, deep), F32),
+            pltpu.VMEM((tall, outer), BF16),
+            pltpu.VMEM((tall, cells - outer), BF16),
+            pltpu.VMEM((tall, outer), BF16),
+            pltpu.VMEM((columns, count, deep), F32),
             small, small, small,
             pltpu.VMEM((nx, ny, 8, deep), F32),
         ],
         limit=28,
         work=60 * count * cells,
         moved=24 * count * cells,
-    )(cols, inner, basis_stack, coeff, diag, rhs, *halo)
+    )(cols, inner, outside_basis, inside_scaled, scaled, gram, square, coeff, diag, rhs, *halo)
 
 
 def pair_rows(field):
@@ -360,13 +425,14 @@
     halo = Halo(odd, (None, None, ya, yb))
     count = part.shape[0] - 8
     nx, ny, deep = coeff.shape[1:]
+    outer = {place: at for at, place in enumerate(outer_columns(nx, ny))}
     for y in range(ny):
         face = row(coeff, 0, nx - 1, y)
         put(
             pair_stack, y, face * far_x[pl.ds(y * count, count), :],
             pair_rows(face * far_x[pl.ds(ny * count + y, 1), :]),
         )
-        mine[:, pl.ds(y * deep, deep)] = scaled_stack[:, pl.ds(((nx - 1) * ny + y) * deep, deep)]
+        mine[:, pl.ds(y * deep, deep)] = scaled_stack[:, pl.ds(outer[nx - 1, y] * deep, deep)]
     for x in range(nx):
         own = halo.rows(1, False, nx * count + x, 1)
         face = jnp.where(odd[0] == 0, row(coeff, 1, x, ny - 1), own)
@@ -377,7 +443,7 @@
 
     def side(y):
         for x in range(nx):
-            mine[:, pl.ds((ny + x) * deep, deep)] = scaled_stack[:, pl.ds((x * ny + y) * deep, deep)]
+            mine[:, pl.ds((ny + x) * deep, deep)] = scaled_stack[:, pl.ds(outer[x, y] * deep, deep)]
 
     @pl.when(odd[0] == 0)
     def _():
@@ -418,7 +484,7 @@
     return jnp.where(at < 2, high, jnp.where(at < 4, both - high, 0.0))
 
 
-def finish_kernel(total, basis_stack, scaled_stack, guess, stepped):
+def finish_kernel(total, inside_basis, outside_basis, inside_scaled, outside_scaled, guess, stepped):
     count = total.shape[0] - 8
     nx, ny, deep = guess.shape
     sums = total[pl.ds(0, count), :]
@@ -474,20 +540,25 @@
     of_rhs = output_rows(jnp.zeros_like(of_rhs), of_rhs, EXTRA)
     of_basis = jnp.concatenate([of_basis, of_basis], axis=1).astype(BF16)
     of_scaled = jnp.concatenate([of_scaled, of_scaled, of_rhs], axis=1).astype(BF16)
-    for x in range(nx):
-        lanes = pl.ds(x * ny * deep, ny * deep)
-        result = jnp.dot(of_basis, basis_stack[:, lanes], preferred_element_type=F32)
-        result += jnp.dot(of_scaled, scaled_stack[:, lanes], preferred_element_type=F32)
+    groups = [(False, x, range(ny)) for x in (0, nx - 1)]
+    for x in range(1, nx - 1):
+        groups += [(True, x, range(1, ny - 1)), (False, x, (0, ny - 1))]
+    starts = {True: 0, False: 0}
+    order = sorted(groups, key=lambda group: not group[0])
+    for within, x, places in order:
+        lanes = pl.ds(starts[within] * deep, len(places) * deep)
+        starts[within] += len(places)
+        basis, scaled = (inside_basis, inside_scaled) if within else (outside_basis, outside_scaled)
+        result = jnp.dot(of_basis, basis[:, lanes], preferred_element_type=F32)
+        result += jnp.dot(of_scaled, scaled[:, lanes], preferred_element_type=F32)
         result = result[0:2] + result[2:4]
-        for y in range(ny):
-            guess[x, pl.ds(y, 1), :] = result[0:1, y * deep : (y + 1) * deep]
-            stepped[x, pl.ds(y, 1), :] = result[1:2, y * deep : (y + 1) * deep]
-
-
-def finish(total, basis_stack, scaled_stack, block):
-    return call(finish_kernel, (shape(*block),) * 2, [VM] * 3, limit=24)(
-        total, basis_stack, scaled_stack
-    )
+        for at, y in enumerate(places):
+            guess[x, pl.ds(y, 1), :] = result[0:1, at * deep : (at + 1) * deep]
+            stepped[x, pl.ds(y, 1), :] = result[1:2, at * deep : (at + 1) * deep]
+
+
+def finish(total, stacks, block):
+    return call(finish_kernel, (shape(*block),) * 2, [VM] * 5, limit=24)(total, *stacks)
 
 
 def steps(basis, rhs, extra_diag, coeff):
@@ -496,7 +567,8 @@
     second_x = swap(second_x, "gx", 1)
     first_y = swap(first_y, "gy", 0)
     second_y = swap(second_y, "gy", 1)
-    inner, basis_stack, diag = inside(cols, coeff, extra_diag)
+    results = inside(cols, coeff, rhs, extra_diag)
+    inner, inside_basis, outside_basis, inside_scaled, scaled, diag, gram, square = results
     halo = (first_x, second_x, first_y, second_y)
     face_x, face_y = border(cols, inner, coeff, diag, rhs, halo)
     wide, deep = lax.axis_size("gx"), lax.axis_size("gy")
@@ -506,10 +578,13 @@
         route += [(i * deep + j, i * deep + j + step) for j in range(deep) if 0 <= j + step < deep]
     far_y = lax.ppermute(face_y, ("gx", "gy"), route)
     far_x = send(face_x, "gx", -1)
-    part, scaled_stack = local_sums(cols, inner, basis_stack, coeff, diag, rhs, halo)
-    part = shared_sums(part, scaled_stack, coeff, first_y, second_y, far_x, far_y)
+    part, outside_scaled = local_sums(
+        cols, inner, outside_basis, inside_scaled, scaled, gram, square, coeff, diag, rhs, halo
+    )
+    part = shared_sums(part, outside_scaled, coeff, first_y, second_y, far_x, far_y)
     total = sum_all(part)
-    return finish(total, basis_stack, scaled_stack, rhs.shape)
+    stacks = (inside_basis, outside_basis, inside_scaled, outside_scaled)
+    return finish(total, stacks, rhs.shape)
 
 
 def solution(mesh):

time: 53.4 us -> 50.5 us (0.946)
  waiting for transfers between devices: 19.4 us -> 16 us
  Pallas kernels: 10.7 us -> 11.4 us
    ppermute x1, waiting for transfers between devices: 4.36 us -> 7.9 us  [steps(): far_y = lax.ppermute(face_y, ('gx', 'gy'), route)]
    ppermute x7, waiting for transfers between devices: 9.6 us -> 6.93 us  [sum_all(): lax.ppermute(part, ('gx', 'gy'), [(i * deep + j, (i ^ a) * deep + (j ^ b)...]
    ppermute x4, waiting for transfers between devices: 2.95 us -> 0.55 us  [swap(): return lax.ppermute(block, axis, pairs + [(j, i) for i, j in pairs])]
    ppermute x1, waiting for transfers between devices: 2.5 us -> 0.6 us  [send(): lax.ppermute(block, axis, [(i, i + step) for i in range(size) if 0 <= i +...]
    pallas_call x3, Pallas kernels: 8.09 us -> 8.85 us  [the longest x1 3.76 us: inside(): call(inner_kernel, outs, [VM, VM, VM, RAW], scratch, work=60 * count * ce...]
  transfers between devices with their start and end apart: 13 -> 13, of which waited for: 8 -> 7; matrix products, arithmetic and copies ran while one was open for 0% -> 0% of each run, Pallas kernels for 9% -> 11%
where the time goes in v7:
time: 50.5 us; the launch traced here: 50.2 us
  starting transfers between devices  21.1 us (42%)
  waiting for transfers between devices  16 us (32%)
  Pallas kernels  11.4 us (23%)
  local copies, waits for them, and re-layouts  0.93 us (2%)
  between operations  0.76 us (2%)
    ppermute x7, starting transfers between devices, sum_all(): lax.ppermute(part, ('gx', 'gy'), [(i * deep + j, (i ^ a) * deep + (j ^ b)...  14 us
    ppermute x1, waiting for transfers between devices, steps(): far_y = lax.ppermute(face_y, ('gx', 'gy'), route)  7.9 us
    ppermute x7, waiting for transfers between devices, sum_all(): lax.ppermute(part, ('gx', 'gy'), [(i * deep + j, (i ^ a) * deep + (j ^ b)...  6.93 us
    ppermute x4, starting transfers between devices, swap(): return lax.ppermute(block, axis, pairs + [(j, i) for i, j in pairs])  4.54 us
    pallas_call x1, Pallas kernels, inside(): call(inner_kernel, outs, [VM, VM, VM, RAW], scratch, work=60 * count * ce...  3.76 us
    pallas_call x1, Pallas kernels, finish(): call(finish_kernel, (shape(*block),) * 2, [VM] * 5, limit=24)  3.09 us
    pallas_call x1, Pallas kernels, local_sums(): call(local_kernel, (shape(count + 8, width), shape(tall, outer, dtype=BF1...  2.01 us
    pallas_call x1, Pallas kernels, faces(): call(faces_kernel, outs, [RAW, RAW], [slabs, sems], limit=50)(basis, coeff)  1.75 us
  transfers between devices with their start and end apart: 13, of which 7 were waited for; matrix products, arithmetic and copies ran while one was open for 0% of the time, Pallas kernels for 11%

profile of v7, /device:TPU:0, one launch (start us, length us, event | category | flops | bytes accessed | tf_op | source)
XLA Modules:
  0.0 50.2 jit_solution(8012728277609929817)
XLA Ops:
  0.6 0.9 %copy-done = f32[3,8,8,256]{3,2,1,0:T(8,128)S(1)} copy-done((f32[3,8,8,256]{3,2,1,0:T(8,128)S(1)}, f32[3,8,8,256]{3,2,1,0:T(8,128)}, u32[]{:S(2)}) %copy-start) | copy-done | bytes 196632
  1.6 1.8 %shard_map.59 = (f32[264,256]{1,0:T(8,128)S(1)}, f32[264,256]{1,0:T(8,128)S(1)}, f32[264,256]{1,0:T(8,128)S(1)}, f32[264,256]{1,0:T(8,128)S(1)}, f32[8,8,32,256]{3,2,1,0:T(8,128)S(1)}) custom-call(f32[32,8,8,256]{3,2,1,0:T(8,128)} %basis.1, f32[3,8,8,256]{3,2,1,0:T(8,128)S(1)} %copy-done), custom_call_target="tpu_custom_call" | custom-call | tf_op jit(solution)/shard_map/pallas_call | solution.py:145
  3.3 0.6 %collective-permute-start = (f32[264,256]{1,0:T(8,128)S(1)}, f32[264,256]{1,0:T(8,128)S(1)}, u32[]{:S(2)}, u32[]{:S(2)}) collective-permute-start(f32[264,256]{1,0:T(8,128)S(1)} %get-tuple-element.27), channel_id=1, source_target_pairs={{0,4},{8,12},{16,20},{24,28},{4,0},{12,8},{20,16},{28,24},{1,5},{9... | collective-permute-start | bytes 811016 | tf_op jit(solution)/shard_map/ppermute | solution.py:73
  3.9 0.7 %collective-permute-start.1 = (f32[264,256]{1,0:T(8,128)S(1)}, f32[264,256]{1,0:T(8,128)S(1)}, u32[]{:S(2)}, u32[]{:S(2)}) collective-permute-start(f32[264,256]{1,0:T(8,128)S(1)} %get-tuple-element.28), channel_id=1, source_target_pairs={{4,8},{12,16},{20,24},{8,4},{16,12},{24,20},{5,9},{13,17},{21,25},... | collective-permute-start | bytes 811016 | tf_op jit(solution)/shard_map/ppermute | solution.py:73
  4.6 2.6 %collective-permute-start.2 = (f32[264,256]{1,0:T(8,128)S(1)}, f32[264,256]{1,0:T(8,128)S(1)}, u32[]{:S(2)}, u32[]{:S(2)}) collective-permute-start(f32[264,256]{1,0:T(8,128)S(1)} %get-tuple-element.29), channel_id=1, source_target_pairs={{0,1},{2,3},{1,0},{3,2},{4,5},{6,7},{5,4},{7,6},{8,9},{10,11},{9,8... | collective-permute-start | bytes 811016 | tf_op jit(solution)/shard_map/ppermute | solution.py:73
  7.2 0.7 %collective-permute-start.3 = (f32[264,256]{1,0:T(8,128)S(1)}, f32[264,256]{1,0:T(8,128)S(1)}, u32[]{:S(2)}, u32[]{:S(2)}) collective-permute-start(f32[264,256]{1,0:T(8,128)S(1)} %get-tuple-element.30), channel_id=1, source_target_pairs={{1,2},{2,1},{5,6},{6,5},{9,10},{10,9},{13,14},{14,13},{17,18},{18,... | collective-permute-start | bytes 811016 | tf_op jit(solution)/shard_map/ppermute | solution.py:73
  7.9 3.8 %shard_map.60 = (f32[8,8,32,256]{3,2,1,0:T(8,128)S(1)}, bf16[64,9216]{1,0:T(8,128)(2,1)S(1)}, bf16[64,7168]{1,0:T(8,128)(2,1)S(1)}, bf16[80,9216]{1,0:T(8,128)(2...) custom-call(f32[8,8,32,256]{3,2,1,0:T(8,128)S(1)} %get-tuple-element, ...), custom_call_target="tpu_custom_call" | custom-call | flops 31457280 | bytes 12582912 | tf_op jit(solution)/shard_map/pallas_call | solution.py:258
  11.7 0.5 %collective-permute-done.2.ya = f32[264,256]{1,0:T(8,128)S(1)} collective-permute-done((f32[264,256]{1,0:T(8,128)S(1)}, f32[264,256]{1,0:T(8,128)S(1)}, u32[]{:S(2)}, u32[]{:S(2)}) %collective-permute-start.2) | collective-permute-done | bytes 270368 | tf_op jit(solution)/shard_map/ppermute | solution.py:73
  12.4 1.3 %collective-permute-start.4 = (f32[264,256]{1,0:T(8,128)S(1)}, f32[264,256]{1,0:T(8,128)S(1)}, u32[]{:S(2)}, u32[]{:S(2)}) collective-permute-start(f32[264,256]{1,0:T(8,128)S(1)} %get-tuple-element.33), channel_id=1, source_target_pairs={{4,0},{8,4},{12,8},{16,12},{20,16},{24,20},{28,24},{5,1},{9,5},{13... | collective-permute-start | bytes 811016 | tf_op jit(solution)/shard_map/ppermute | solution.py:67
  13.7 1.3 %collective-permute-start.5 = (f32[264,256]{1,0:T(8,128)S(1)}, f32[264,256]{1,0:T(8,128)S(1)}, u32[]{:S(2)}, u32[]{:S(2)}) collective-permute-start(f32[264,256]{1,0:T(8,128)S(1)} %get-tuple-element.34), channel_id=1, source_target_pairs={{1,0},{2,1},{3,2},{4,5},{5,6},{6,7},{9,8},{10,9},{11,10},{12,13},{... | collective-permute-start | bytes 811016 | tf_op jit(solution)/shard_map/ppermute | solution.py:579
  15.0 2.0 %shard_map.61 = (f32[40,128]{1,0:T(8,128)S(1)}, bf16[80,7168]{1,0:T(8,128)(2,1)S(1)}) custom-call(f32[8,8,32,256]{3,2,1,0:T(8,128)S(1)} %get-tuple-element.19.cols, f32[8,8,32,256]{3,2,1,0:T(8,128)S(1)} %get-tuple-element.20.inner, bf16[64,7168]{1,0:T(8,128)(2,1)S(1)} %get-tuple-element.21.outside_basis, ...), custom_call_target="tpu_custom_call" | custom-call | flops 31457280 | bytes 12582912 | tf_op jit(solution)/shard_map/pallas_call | solution.py:398
  17.1 0.6 %collective-permute-done.4.far_x = f32[264,256]{1,0:T(8,128)S(1)} collective-permute-done((f32[264,256]{1,0:T(8,128)S(1)}, f32[264,256]{1,0:T(8,128)S(1)}, u32[]{:S(2)}, u32[]{:S(2)}) %collective-permute-start.4) | collective-permute-done | bytes 270368 | tf_op jit(solution)/shard_map/ppermute | solution.py:67
  17.7 7.9 %collective-permute-done.5.far_y = f32[264,256]{1,0:T(8,128)S(1)} collective-permute-done((f32[264,256]{1,0:T(8,128)S(1)}, f32[264,256]{1,0:T(8,128)S(1)}, u32[]{:S(2)}, u32[]{:S(2)}) %collective-permute-start.5) | collective-permute-done | bytes 270368 | tf_op jit(solution)/shard_map/ppermute | solution.py:579
  25.6 0.6 %shard_map.63 = f32[40,128]{1,0:T(8,128)S(1)} custom-call(f32[40,128]{1,0:T(8,128)S(1)} %get-tuple-element.31.part, bf16[80,7168]{1,0:T(8,128)(2,1)S(1)} %get-tuple-element.32.scaled_stack.outside_scaled, f32[3,8,8,256]{3,2,1,0:T(8,128)S(1)} %copy-done, f32[264,256]{1,0:T(8,128)S(1)} %collective-permute-done.2.ya, f32[264,256]{1,0:T(8,128)S(1)} %collective-permute-done.3.yb, ...), custom_call_target="tpu_custom_call" | custom-call | tf_op jit(solution)/shard_map/pallas_call | solution.py:465
  26.2 3.8 %collective-permute-start.6 = (f32[40,128]{1,0:T(8,128)S(1)}, f32[40,128]{1,0:T(8,128)S(1)}, u32[]{:S(2)}, u32[]{:S(2)}) collective-permute-start(f32[40,128]{1,0:T(8,128)S(1)} %shard_map.63), channel_id=1, source_target_pairs={{0,2},{1,3},{2,0},{3,1},{4,6},{5,7},{6,4},{7,5},{8,10},{9,11},{10,... | collective-permute-start | bytes 61448 | tf_op jit(solution)/shard_map/ppermute | solution.py:53
  30.0 1.8 %collective-permute-done.6 = f32[40,128]{1,0:T(8,128)S(1)} collective-permute-done((f32[40,128]{1,0:T(8,128)S(1)}, f32[40,128]{1,0:T(8,128)S(1)}, u32[]{:S(2)}, u32[]{:S(2)}) %collective-permute-start.6) | collective-permute-done | bytes 20512 | tf_op jit(solution)/shard_map/ppermute | solution.py:53
  31.8 3.7 %collective-permute-start.9 = (f32[40,128]{1,0:T(8,128)S(1)}, f32[40,128]{1,0:T(8,128)S(1)}, u32[]{:S(2)}, u32[]{:S(2)}) collective-permute-start(f32[40,128]{1,0:T(8,128)S(1)} %add.21), channel_id=1, source_target_pairs={{0,12},{1,13},{2,14},{3,15},{4,8},{5,9},{6,10},{7,11},{8,4},{9,5},... | collective-permute-start | bytes 61448 | tf_op jit(solution)/shard_map/ppermute | solution.py:53
  35.5 1.7 %collective-permute-start.8 = (f32[40,128]{1,0:T(8,128)S(1)}, f32[40,128]{1,0:T(8,128)S(1)}, u32[]{:S(2)}, u32[]{:S(2)}) collective-permute-start(f32[40,128]{1,0:T(8,128)S(1)} %add.21), channel_id=1, source_target_pairs={{0,8},{1,9},{2,10},{3,11},{4,12},{5,13},{6,14},{7,15},{8,0},{9,1},... | collective-permute-start | bytes 61448 | tf_op jit(solution)/shard_map/ppermute | solution.py:53
  37.3 2.0 %collective-permute-done.8 = f32[40,128]{1,0:T(8,128)S(1)} collective-permute-done((f32[40,128]{1,0:T(8,128)S(1)}, f32[40,128]{1,0:T(8,128)S(1)}, u32[]{:S(2)}, u32[]{:S(2)}) %collective-permute-start.8) | collective-permute-done | bytes 20512 | tf_op jit(solution)/shard_map/ppermute | solution.py:53
  39.3 4.1 %collective-permute-start.12 = (f32[40,128]{1,0:T(8,128)S(1)}, f32[40,128]{1,0:T(8,128)S(1)}, u32[]{:S(2)}, u32[]{:S(2)}) collective-permute-start(f32[40,128]{1,0:T(8,128)S(1)} %add_add_fusion.1), channel_id=1, source_target_pairs={{0,17},{1,16},{2,19},{3,18},{4,21},{5,20},{6,23},{7,22},{8,25},{9,... | collective-permute-start | bytes 61448 | tf_op jit(solution)/shard_map/ppermute | solution.py:53
  43.3 0.6 %collective-permute-start.10 = (f32[40,128]{1,0:T(8,128)S(1)}, f32[40,128]{1,0:T(8,128)S(1)}, u32[]{:S(2)}, u32[]{:S(2)}) collective-permute-start(f32[40,128]{1,0:T(8,128)S(1)} %add_add_fusion.1), channel_id=1, source_target_pairs={{0,16},{1,17},{2,18},{3,19},{4,20},{5,21},{6,22},{7,23},{8,24},{9,... | collective-permute-start | bytes 61448 | tf_op jit(solution)/shard_map/ppermute | solution.py:53
  44.0 1.4 %collective-permute-done.12 = f32[40,128]{1,0:T(8,128)S(1)} collective-permute-done((f32[40,128]{1,0:T(8,128)S(1)}, f32[40,128]{1,0:T(8,128)S(1)}, u32[]{:S(2)}, u32[]{:S(2)}) %collective-permute-start.12) | collective-permute-done | bytes 20512 | tf_op jit(solution)/shard_map/ppermute | solution.py:53
  45.4 1.7 %collective-permute-done.11 = f32[40,128]{1,0:T(8,128)S(1)} collective-permute-done((f32[40,128]{1,0:T(8,128)S(1)}, f32[40,128]{1,0:T(8,128)S(1)}, u32[]{:S(2)}, u32[]{:S(2)}) %collective-permute-start.11) | collective-permute-done | bytes 20512 | tf_op jit(solution)/shard_map/ppermute | solution.py:53
  47.1 3.1 %shard_map.64 = (f32[8,8,256]{2,1,0:T(8,128)}, f32[8,8,256]{2,1,0:T(8,128)}) custom-call(f32[40,128]{1,0:T(8,128)S(1)} %add_add_fusion.total, bf16[64,9216]{1,0:T(8,128)(2,1)S(1)} %get-tuple-element.35.inside_basis, bf16[64,7168]{1,0:T(8,128)(2,1)S(1)} %get-tuple-element.21.outside_basis, bf16[80,9216]{1,0:T(8,128)(2,1)S(1)} %get-tuple-element.22.inside_scaled, ...), custom_call_target="tpu_custom_call" | custom-call | tf_op jit(solution)/shard_map/pallas_call | solution.py:561
  (17 shorter events, 0.4 us)
Async XLA Ops:
  0.6 0.9 %copy-start = (f32[3,8,8,256]{3,2,1,0:T(8,128)S(1)}, f32[3,8,8,256]{3,2,1,0:T(8,128)}, u32[]{:S(2)}) copy-start(f32[3,8,8,256]{3,2,1,0:T(8,128)} %coeff.9) | copy-start | bytes 589828
  1.6 6.3 %copy-start.1 = (f32[8,8,256]{2,1,0:T(8,128)S(1)}, f32[8,8,256]{2,1,0:T(8,128)}, u32[]{:S(2)}) copy-start(f32[8,8,256]{2,1,0:T(8,128)} %rhs.5) | copy-start | bytes 196612
  1.6 6.3 %copy-start.2 = (f32[8,8,256]{2,1,0:T(8,128)S(1)}, f32[8,8,256]{2,1,0:T(8,128)}, u32[]{:S(2)}) copy-start(f32[8,8,256]{2,1,0:T(8,128)} %extra_raw.1) | copy-start | bytes 196612
  3.3 8.3 %collective-permute-start = (f32[264,256]{1,0:T(8,128)S(1)}, f32[264,256]{1,0:T(8,128)S(1)}, u32[]{:S(2)}, u32[]{:S(2)}) collective-permute-start(f32[264,256]{1,0:T(8,128)S(1)} %get-tuple-element.27), channel_id=1, source_target_pairs={{0,4},{8,12},{16,20},{24,28},{4,0},{12,8},{20,16},{28,24},{1,5},{9... | collective-permute-start | bytes 811016 | tf_op jit(solution)/shard_map/ppermute | solution.py:73
  3.9 7.8 %collective-permute-start.1 = (f32[264,256]{1,0:T(8,128)S(1)}, f32[264,256]{1,0:T(8,128)S(1)}, u32[]{:S(2)}, u32[]{:S(2)}) collective-permute-start(f32[264,256]{1,0:T(8,128)S(1)} %get-tuple-element.28), channel_id=1, source_target_pairs={{4,8},{12,16},{20,24},{8,4},{16,12},{24,20},{5,9},{13,17},{21,25},... | collective-permute-start | bytes 811016 | tf_op jit(solution)/shard_map/ppermute | solution.py:73
  4.6 7.7 %collective-permute-start.2 = (f32[264,256]{1,0:T(8,128)S(1)}, f32[264,256]{1,0:T(8,128)S(1)}, u32[]{:S(2)}, u32[]{:S(2)}) collective-permute-start(f32[264,256]{1,0:T(8,128)S(1)} %get-tuple-element.29), channel_id=1, source_target_pairs={{0,1},{2,3},{1,0},{3,2},{4,5},{6,7},{5,4},{7,6},{8,9},{10,11},{9,8... | collective-permute-start | bytes 811016 | tf_op jit(solution)/shard_map/ppermute | solution.py:73
  7.2 5.0 %collective-permute-start.3 = (f32[264,256]{1,0:T(8,128)S(1)}, f32[264,256]{1,0:T(8,128)S(1)}, u32[]{:S(2)}, u32[]{:S(2)}) collective-permute-start(f32[264,256]{1,0:T(8,128)S(1)} %get-tuple-element.30), channel_id=1, source_target_pairs={{1,2},{2,1},{5,6},{6,5},{9,10},{10,9},{13,14},{14,13},{17,18},{18,... | collective-permute-start | bytes 811016 | tf_op jit(solution)/shard_map/ppermute | solution.py:73
  12.4 5.2 %collective-permute-start.4 = (f32[264,256]{1,0:T(8,128)S(1)}, f32[264,256]{1,0:T(8,128)S(1)}, u32[]{:S(2)}, u32[]{:S(2)}) collective-permute-start(f32[264,256]{1,0:T(8,128)S(1)} %get-tuple-element.33), channel_id=1, source_target_pairs={{4,0},{8,4},{12,8},{16,12},{20,16},{24,20},{28,24},{5,1},{9,5},{13... | collective-permute-start | bytes 811016 | tf_op jit(solution)/shard_map/ppermute | solution.py:67
  13.7 11.8 %collective-permute-start.5 = (f32[264,256]{1,0:T(8,128)S(1)}, f32[264,256]{1,0:T(8,128)S(1)}, u32[]{:S(2)}, u32[]{:S(2)}) collective-permute-start(f32[264,256]{1,0:T(8,128)S(1)} %get-tuple-element.34), channel_id=1, source_target_pairs={{1,0},{2,1},{3,2},{4,5},{5,6},{6,7},{9,8},{10,9},{11,10},{12,13},{... | collective-permute-start | bytes 811016 | tf_op jit(solution)/shard_map/ppermute | solution.py:579
  26.2 5.6 %collective-permute-start.6 = (f32[40,128]{1,0:T(8,128)S(1)}, f32[40,128]{1,0:T(8,128)S(1)}, u32[]{:S(2)}, u32[]{:S(2)}) collective-permute-start(f32[40,128]{1,0:T(8,128)S(1)} %shard_map.63), channel_id=1, source_target_pairs={{0,2},{1,3},{2,0},{3,1},{4,6},{5,7},{6,4},{7,5},{8,10},{9,11},{10,... | collective-permute-start | bytes 61448 | tf_op jit(solution)/shard_map/ppermute | solution.py:53
  31.8 5.5 %collective-permute-start.9 = (f32[40,128]{1,0:T(8,128)S(1)}, f32[40,128]{1,0:T(8,128)S(1)}, u32[]{:S(2)}, u32[]{:S(2)}) collective-permute-start(f32[40,128]{1,0:T(8,128)S(1)} %add.21), channel_id=1, source_target_pairs={{0,12},{1,13},{2,14},{3,15},{4,8},{5,9},{6,10},{7,11},{8,4},{9,5},... | collective-permute-start | bytes 61448 | tf_op jit(solution)/shard_map/ppermute | solution.py:53
  35.5 3.8 %collective-permute-start.8 = (f32[40,128]{1,0:T(8,128)S(1)}, f32[40,128]{1,0:T(8,128)S(1)}, u32[]{:S(2)}, u32[]{:S(2)}) collective-permute-start(f32[40,128]{1,0:T(8,128)S(1)} %add.21), channel_id=1, source_target_pairs={{0,8},{1,9},{2,10},{3,11},{4,12},{5,13},{6,14},{7,15},{8,0},{9,1},... | collective-permute-start | bytes 61448 | tf_op jit(solution)/shard_map/ppermute | solution.py:53
  37.2 2.0 %collective-permute-start.7 = (f32[40,128]{1,0:T(8,128)S(1)}, f32[40,128]{1,0:T(8,128)S(1)}, u32[]{:S(2)}, u32[]{:S(2)}) collective-permute-start(f32[40,128]{1,0:T(8,128)S(1)} %add.21), channel_id=1, source_target_pairs={{0,4},{1,5},{2,6},{3,7},{4,0},{5,1},{6,2},{7,3},{8,12},{9,13},{10,... | collective-permute-start | bytes 61448 | tf_op jit(solution)/shard_map/ppermute | solution.py:53
  39.3 6.1 %collective-permute-start.12 = (f32[40,128]{1,0:T(8,128)S(1)}, f32[40,128]{1,0:T(8,128)S(1)}, u32[]{:S(2)}, u32[]{:S(2)}) collective-permute-start(f32[40,128]{1,0:T(8,128)S(1)} %add_add_fusion.1), channel_id=1, source_target_pairs={{0,17},{1,16},{2,19},{3,18},{4,21},{5,20},{6,23},{7,22},{8,25},{9,... | collective-permute-start | bytes 61448 | tf_op jit(solution)/shard_map/ppermute | solution.py:53
  43.3 3.8 %collective-permute-start.11 = (f32[40,128]{1,0:T(8,128)S(1)}, f32[40,128]{1,0:T(8,128)S(1)}, u32[]{:S(2)}, u32[]{:S(2)}) collective-permute-start(f32[40,128]{1,0:T(8,128)S(1)} %add_add_fusion.1), channel_id=1, source_target_pairs={{0,1},{1,0},{2,3},{3,2},{4,5},{5,4},{6,7},{7,6},{8,9},{9,8},{10,11... | collective-permute-start | bytes 61448 | tf_op jit(solution)/shard_map/ppermute | solution.py:53
  43.3 3.8 %collective-permute-start.10 = (f32[40,128]{1,0:T(8,128)S(1)}, f32[40,128]{1,0:T(8,128)S(1)}, u32[]{:S(2)}, u32[]{:S(2)}) collective-permute-start(f32[40,128]{1,0:T(8,128)S(1)} %add_add_fusion.1), channel_id=1, source_target_pairs={{0,16},{1,17},{2,18},{3,19},{4,20},{5,21},{6,22},{7,23},{8,24},{9,... | collective-permute-start | bytes 61448 | tf_op jit(solution)/shard_map/ppermute | solution.py:53

commit v8 on v7

--- a/solution.py
+++ b/solution.py
@@ -34,13 +34,18 @@
     wide, deep = lax.axis_size("gx"), lax.axis_size("gy")
     along_x = [(1 << k, 0) for k in range(wide.bit_length() - 1)]
     along_y = [(0, 1 << k) for k in range(deep.bit_length() - 1)]
-    steps = along_y[:0:-1] + along_x + along_y[:1]
-    single = len(steps) % 2
-    stages = [[step] for step in steps[:single]]
-    for at in range(single, len(steps), 2):
-        (a, b), (c, d) = steps[at], steps[at + 1]
-        stages.append([(a, b), (c, d), (a ^ c, b ^ d)])
-    return stages
+    first = along_x[-2:-1] + along_y[:1]
+    rest = along_y[:0:-1] + along_x[:-2] + along_x[-1:]
+    groups = [first, rest[: len(rest) % 2]]
+    groups += [rest[at : at + 2] for at in range(len(rest) % 2, len(rest), 2)]
+    stages = []
+    for group in groups:
+        stage = list(group)
+        if len(group) == 2:
+            (a, b), (c, d) = group
+            stage.append((a ^ c, b ^ d))
+        stages.append(stage)
+    return [stage for stage in stages if stage]
 
 
 def sum_all(part):
@@ -510,8 +515,8 @@
         line_0 = line_0 - across[0][0] * line_2 - across[1][0] * line_3
         line_1 = line_1 - across[0][1] * line_2 - across[1][1] * line_3
         lines = (line_0, line_1, line_2, line_3)
-        for a in range(4):
-            work = work - columns[a] * lines[a]
+        terms = [columns[a] * lines[a] for a in range(4)]
+        work = work - ((terms[0] + terms[1]) + (terms[2] + terms[3]))
         for a in range(4):
             work = jnp.where(level == k + a, lines[a], work)
     at = 3 * count

time: 50.5 us -> 49.6 us (0.982)
  starting transfers between devices: 21.1 us -> 20.2 us
    ppermute x7, starting transfers between devices: 14 us -> 13.1 us  [sum_all(): lax.ppermute(part, ('gx', 'gy'), [(i * deep + j, (i ^ a) * deep + (j ^ b)...]
  transfers between devices with their start and end apart: 13 -> 13, of which waited for: 7 -> 8; matrix products, arithmetic and copies ran while one was open for 0% -> 0% of each run, Pallas kernels for 11% -> 12%
where the time goes in v8:
time: 49.6 us; the launch traced here: 49.4 us
  starting transfers between devices  20.2 us (41%)
  waiting for transfers between devices  16 us (32%)
  Pallas kernels  11.5 us (23%)
  local copies, waits for them, and re-layouts  0.93 us (2%)
  between operations  0.76 us (2%)
    ppermute x7, starting transfers between devices, sum_all(): lax.ppermute(part, ('gx', 'gy'), [(i * deep + j, (i ^ a) * deep + (j ^ b)...  13.1 us
    ppermute x1, waiting for transfers between devices, steps(): far_y = lax.ppermute(face_y, ('gx', 'gy'), route)  7.9 us
    ppermute x7, waiting for transfers between devices, sum_all(): lax.ppermute(part, ('gx', 'gy'), [(i * deep + j, (i ^ a) * deep + (j ^ b)...  6.91 us
    ppermute x4, starting transfers between devices, swap(): return lax.ppermute(block, axis, pairs + [(j, i) for i, j in pairs])  4.54 us
    pallas_call x1, Pallas kernels, inside(): call(inner_kernel, outs, [VM, VM, VM, RAW], scratch, work=60 * count * ce...  3.76 us
    pallas_call x1, Pallas kernels, finish(): call(finish_kernel, (shape(*block),) * 2, [VM] * 5, limit=24)  3.1 us
    pallas_call x1, Pallas kernels, local_sums(): call(local_kernel, (shape(count + 8, width), shape(tall, outer, dtype=BF1...  2.01 us
    pallas_call x1, Pallas kernels, faces(): call(faces_kernel, outs, [RAW, RAW], [slabs, sems], limit=50)(basis, coeff)  1.75 us
  transfers between devices with their start and end apart: 13, of which 8 were waited for; matrix products, arithmetic and copies ran while one was open for 0% of the time, Pallas kernels for 12%

profile of v8, /device:TPU:0, one launch (start us, length us, event | category | flops | bytes accessed | tf_op | source)
XLA Modules:
  0.0 49.4 jit_solution(12082016133703665284)
XLA Ops:
  0.6 0.9 %copy-done = f32[3,8,8,256]{3,2,1,0:T(8,128)S(1)} copy-done((f32[3,8,8,256]{3,2,1,0:T(8,128)S(1)}, f32[3,8,8,256]{3,2,1,0:T(8,128)}, u32[]{:S(2)}) %copy-start) | copy-done | bytes 196632
  1.6 1.8 %shard_map.59 = (f32[264,256]{1,0:T(8,128)S(1)}, f32[264,256]{1,0:T(8,128)S(1)}, f32[264,256]{1,0:T(8,128)S(1)}, f32[264,256]{1,0:T(8,128)S(1)}, f32[8,8,32,256]{3,2,1,0:T(8,128)S(1)}) custom-call(f32[32,8,8,256]{3,2,1,0:T(8,128)} %basis.1, f32[3,8,8,256]{3,2,1,0:T(8,128)S(1)} %copy-done), custom_call_target="tpu_custom_call" | custom-call | tf_op jit(solution)/shard_map/pallas_call | solution.py:150
  3.3 0.6 %collective-permute-start = (f32[264,256]{1,0:T(8,128)S(1)}, f32[264,256]{1,0:T(8,128)S(1)}, u32[]{:S(2)}, u32[]{:S(2)}) collective-permute-start(f32[264,256]{1,0:T(8,128)S(1)} %get-tuple-element.27), channel_id=1, source_target_pairs={{0,4},{8,12},{16,20},{24,28},{4,0},{12,8},{20,16},{28,24},{1,5},{9... | collective-permute-start | bytes 811016 | tf_op jit(solution)/shard_map/ppermute | solution.py:78
  3.9 0.7 %collective-permute-start.1 = (f32[264,256]{1,0:T(8,128)S(1)}, f32[264,256]{1,0:T(8,128)S(1)}, u32[]{:S(2)}, u32[]{:S(2)}) collective-permute-start(f32[264,256]{1,0:T(8,128)S(1)} %get-tuple-element.28), channel_id=1, source_target_pairs={{4,8},{12,16},{20,24},{8,4},{16,12},{24,20},{5,9},{13,17},{21,25},... | collective-permute-start | bytes 811016 | tf_op jit(solution)/shard_map/ppermute | solution.py:78
  4.6 2.6 %collective-permute-start.2 = (f32[264,256]{1,0:T(8,128)S(1)}, f32[264,256]{1,0:T(8,128)S(1)}, u32[]{:S(2)}, u32[]{:S(2)}) collective-permute-start(f32[264,256]{1,0:T(8,128)S(1)} %get-tuple-element.29), channel_id=1, source_target_pairs={{0,1},{2,3},{1,0},{3,2},{4,5},{6,7},{5,4},{7,6},{8,9},{10,11},{9,8... | collective-permute-start | bytes 811016 | tf_op jit(solution)/shard_map/ppermute | solution.py:78
  7.2 0.7 %collective-permute-start.3 = (f32[264,256]{1,0:T(8,128)S(1)}, f32[264,256]{1,0:T(8,128)S(1)}, u32[]{:S(2)}, u32[]{:S(2)}) collective-permute-start(f32[264,256]{1,0:T(8,128)S(1)} %get-tuple-element.30), channel_id=1, source_target_pairs={{1,2},{2,1},{5,6},{6,5},{9,10},{10,9},{13,14},{14,13},{17,18},{18,... | collective-permute-start | bytes 811016 | tf_op jit(solution)/shard_map/ppermute | solution.py:78
  7.9 3.8 %shard_map.60 = (f32[8,8,32,256]{3,2,1,0:T(8,128)S(1)}, bf16[64,9216]{1,0:T(8,128)(2,1)S(1)}, bf16[64,7168]{1,0:T(8,128)(2,1)S(1)}, bf16[80,9216]{1,0:T(8,128)(2...) custom-call(f32[8,8,32,256]{3,2,1,0:T(8,128)S(1)} %get-tuple-element, ...), custom_call_target="tpu_custom_call" | custom-call | flops 31457280 | bytes 12582912 | tf_op jit(solution)/shard_map/pallas_call | solution.py:263
  11.7 0.5 %collective-permute-done.2.ya = f32[264,256]{1,0:T(8,128)S(1)} collective-permute-done((f32[264,256]{1,0:T(8,128)S(1)}, f32[264,256]{1,0:T(8,128)S(1)}, u32[]{:S(2)}, u32[]{:S(2)}) %collective-permute-start.2) | collective-permute-done | bytes 270368 | tf_op jit(solution)/shard_map/ppermute | solution.py:78
  12.4 1.3 %collective-permute-start.4 = (f32[264,256]{1,0:T(8,128)S(1)}, f32[264,256]{1,0:T(8,128)S(1)}, u32[]{:S(2)}, u32[]{:S(2)}) collective-permute-start(f32[264,256]{1,0:T(8,128)S(1)} %get-tuple-element.33), channel_id=1, source_target_pairs={{4,0},{8,4},{12,8},{16,12},{20,16},{24,20},{28,24},{5,1},{9,5},{13... | collective-permute-start | bytes 811016 | tf_op jit(solution)/shard_map/ppermute | solution.py:72
  13.7 1.3 %collective-permute-start.5 = (f32[264,256]{1,0:T(8,128)S(1)}, f32[264,256]{1,0:T(8,128)S(1)}, u32[]{:S(2)}, u32[]{:S(2)}) collective-permute-start(f32[264,256]{1,0:T(8,128)S(1)} %get-tuple-element.34), channel_id=1, source_target_pairs={{1,0},{2,1},{3,2},{4,5},{5,6},{6,7},{9,8},{10,9},{11,10},{12,13},{... | collective-permute-start | bytes 811016 | tf_op jit(solution)/shard_map/ppermute | solution.py:584
  15.0 2.0 %shard_map.61 = (f32[40,128]{1,0:T(8,128)S(1)}, bf16[80,7168]{1,0:T(8,128)(2,1)S(1)}) custom-call(f32[8,8,32,256]{3,2,1,0:T(8,128)S(1)} %get-tuple-element.19.cols, f32[8,8,32,256]{3,2,1,0:T(8,128)S(1)} %get-tuple-element.20.inner, bf16[64,7168]{1,0:T(8,128)(2,1)S(1)} %get-tuple-element.21.outside_basis, ...), custom_call_target="tpu_custom_call" | custom-call | flops 31457280 | bytes 12582912 | tf_op jit(solution)/shard_map/pallas_call | solution.py:403
  17.1 0.6 %collective-permute-done.4.far_x = f32[264,256]{1,0:T(8,128)S(1)} collective-permute-done((f32[264,256]{1,0:T(8,128)S(1)}, f32[264,256]{1,0:T(8,128)S(1)}, u32[]{:S(2)}, u32[]{:S(2)}) %collective-permute-start.4) | collective-permute-done | bytes 270368 | tf_op jit(solution)/shard_map/ppermute | solution.py:72
  17.7 7.9 %collective-permute-done.5.far_y = f32[264,256]{1,0:T(8,128)S(1)} collective-permute-done((f32[264,256]{1,0:T(8,128)S(1)}, f32[264,256]{1,0:T(8,128)S(1)}, u32[]{:S(2)}, u32[]{:S(2)}) %collective-permute-start.5) | collective-permute-done | bytes 270368 | tf_op jit(solution)/shard_map/ppermute | solution.py:584
  25.6 0.6 %shard_map.63 = f32[40,128]{1,0:T(8,128)S(1)} custom-call(f32[40,128]{1,0:T(8,128)S(1)} %get-tuple-element.31.part, bf16[80,7168]{1,0:T(8,128)(2,1)S(1)} %get-tuple-element.32.scaled_stack.outside_scaled, f32[3,8,8,256]{3,2,1,0:T(8,128)S(1)} %copy-done, f32[264,256]{1,0:T(8,128)S(1)} %collective-permute-done.2.ya, f32[264,256]{1,0:T(8,128)S(1)} %collective-permute-done.3.yb, ...), custom_call_target="tpu_custom_call" | custom-call | tf_op jit(solution)/shard_map/pallas_call | solution.py:470
  26.2 7.3 %collective-permute-start.8 = (f32[40,128]{1,0:T(8,128)S(1)}, f32[40,128]{1,0:T(8,128)S(1)}, u32[]{:S(2)}, u32[]{:S(2)}) collective-permute-start(f32[40,128]{1,0:T(8,128)S(1)} %shard_map.63), channel_id=1, source_target_pairs={{0,9},{1,8},{2,11},{3,10},{4,13},{5,12},{6,15},{7,14},{8,1},{9,0},... | collective-permute-start | bytes 61448 | tf_op jit(solution)/shard_map/ppermute | solution.py:58
  33.6 0.6 %collective-permute-start.6 = (f32[40,128]{1,0:T(8,128)S(1)}, f32[40,128]{1,0:T(8,128)S(1)}, u32[]{:S(2)}, u32[]{:S(2)}) collective-permute-start(f32[40,128]{1,0:T(8,128)S(1)} %shard_map.63), channel_id=1, source_target_pairs={{0,8},{1,9},{2,10},{3,11},{4,12},{5,13},{6,14},{7,15},{8,0},{9,1},... | collective-permute-start | bytes 61448 | tf_op jit(solution)/shard_map/ppermute | solution.py:58
  34.2 1.1 %collective-permute-done.8 = f32[40,128]{1,0:T(8,128)S(1)} collective-permute-done((f32[40,128]{1,0:T(8,128)S(1)}, f32[40,128]{1,0:T(8,128)S(1)}, u32[]{:S(2)}, u32[]{:S(2)}) %collective-permute-start.8) | collective-permute-done | bytes 20512 | tf_op jit(solution)/shard_map/ppermute | solution.py:58
  35.3 2.0 %collective-permute-done.7 = f32[40,128]{1,0:T(8,128)S(1)} collective-permute-done((f32[40,128]{1,0:T(8,128)S(1)}, f32[40,128]{1,0:T(8,128)S(1)}, u32[]{:S(2)}, u32[]{:S(2)}) %collective-permute-start.7) | collective-permute-done | bytes 20512 | tf_op jit(solution)/shard_map/ppermute | solution.py:58
  37.3 3.3 %collective-permute-start.9 = (f32[40,128]{1,0:T(8,128)S(1)}, f32[40,128]{1,0:T(8,128)S(1)}, u32[]{:S(2)}, u32[]{:S(2)}) collective-permute-start(f32[40,128]{1,0:T(8,128)S(1)} %add_add_fusion.1), channel_id=1, source_target_pairs={{0,2},{1,3},{2,0},{3,1},{4,6},{5,7},{6,4},{7,5},{8,10},{9,11},{10,... | collective-permute-start | bytes 61448 | tf_op jit(solution)/shard_map/ppermute | solution.py:58
  40.6 1.8 %collective-permute-done.9 = f32[40,128]{1,0:T(8,128)S(1)} collective-permute-done((f32[40,128]{1,0:T(8,128)S(1)}, f32[40,128]{1,0:T(8,128)S(1)}, u32[]{:S(2)}, u32[]{:S(2)}) %collective-permute-start.9) | collective-permute-done | bytes 20512 | tf_op jit(solution)/shard_map/ppermute | solution.py:58
  42.4 1.6 %collective-permute-start.11 = (f32[40,128]{1,0:T(8,128)S(1)}, f32[40,128]{1,0:T(8,128)S(1)}, u32[]{:S(2)}, u32[]{:S(2)}) collective-permute-start(f32[40,128]{1,0:T(8,128)S(1)} %add.24), channel_id=1, source_target_pairs={{0,16},{1,17},{2,18},{3,19},{4,20},{5,21},{6,22},{7,23},{8,24},{9,... | collective-permute-start | bytes 61448 | tf_op jit(solution)/shard_map/ppermute | solution.py:58
  44.3 1.5 %collective-permute-done.12 = f32[40,128]{1,0:T(8,128)S(1)} collective-permute-done((f32[40,128]{1,0:T(8,128)S(1)}, f32[40,128]{1,0:T(8,128)S(1)}, u32[]{:S(2)}, u32[]{:S(2)}) %collective-permute-start.12) | collective-permute-done | bytes 20512 | tf_op jit(solution)/shard_map/ppermute | solution.py:58
  45.8 0.5 collective-permute-done.11
  46.3 3.1 %shard_map.64 = (f32[8,8,256]{2,1,0:T(8,128)}, f32[8,8,256]{2,1,0:T(8,128)}) custom-call(f32[40,128]{1,0:T(8,128)S(1)} %add_add_fusion.total, bf16[64,9216]{1,0:T(8,128)(2,1)S(1)} %get-tuple-element.35.inside_basis, bf16[64,7168]{1,0:T(8,128)(2,1)S(1)} %get-tuple-element.21.outside_basis, bf16[80,9216]{1,0:T(8,128)(2,1)S(1)} %get-tuple-element.22.inside_scaled, ...), custom_call_target="tpu_custom_call" | custom-call | tf_op jit(solution)/shard_map/pallas_call | solution.py:566
  (17 shorter events, 0.6 us)
Async XLA Ops:
  0.6 0.9 %copy-start = (f32[3,8,8,256]{3,2,1,0:T(8,128)S(1)}, f32[3,8,8,256]{3,2,1,0:T(8,128)}, u32[]{:S(2)}) copy-start(f32[3,8,8,256]{3,2,1,0:T(8,128)} %coeff.9) | copy-start | bytes 589828
  1.6 6.3 %copy-start.1 = (f32[8,8,256]{2,1,0:T(8,128)S(1)}, f32[8,8,256]{2,1,0:T(8,128)}, u32[]{:S(2)}) copy-start(f32[8,8,256]{2,1,0:T(8,128)} %rhs.5) | copy-start | bytes 196612
  1.6 6.3 %copy-start.2 = (f32[8,8,256]{2,1,0:T(8,128)S(1)}, f32[8,8,256]{2,1,0:T(8,128)}, u32[]{:S(2)}) copy-start(f32[8,8,256]{2,1,0:T(8,128)} %extra_raw.1) | copy-start | bytes 196612
  3.3 8.3 %collective-permute-start = (f32[264,256]{1,0:T(8,128)S(1)}, f32[264,256]{1,0:T(8,128)S(1)}, u32[]{:S(2)}, u32[]{:S(2)}) collective-permute-start(f32[264,256]{1,0:T(8,128)S(1)} %get-tuple-element.27), channel_id=1, source_target_pairs={{0,4},{8,12},{16,20},{24,28},{4,0},{12,8},{20,16},{28,24},{1,5},{9... | collective-permute-start | bytes 811016 | tf_op jit(solution)/shard_map/ppermute | solution.py:78
  3.9 7.8 %collective-permute-start.1 = (f32[264,256]{1,0:T(8,128)S(1)}, f32[264,256]{1,0:T(8,128)S(1)}, u32[]{:S(2)}, u32[]{:S(2)}) collective-permute-start(f32[264,256]{1,0:T(8,128)S(1)} %get-tuple-element.28), channel_id=1, source_target_pairs={{4,8},{12,16},{20,24},{8,4},{16,12},{24,20},{5,9},{13,17},{21,25},... | collective-permute-start | bytes 811016 | tf_op jit(solution)/shard_map/ppermute | solution.py:78
  4.6 7.7 %collective-permute-start.2 = (f32[264,256]{1,0:T(8,128)S(1)}, f32[264,256]{1,0:T(8,128)S(1)}, u32[]{:S(2)}, u32[]{:S(2)}) collective-permute-start(f32[264,256]{1,0:T(8,128)S(1)} %get-tuple-element.29), channel_id=1, source_target_pairs={{0,1},{2,3},{1,0},{3,2},{4,5},{6,7},{5,4},{7,6},{8,9},{10,11},{9,8... | collective-permute-start | bytes 811016 | tf_op jit(solution)/shard_map/ppermute | solution.py:78
  7.2 5.0 %collective-permute-start.3 = (f32[264,256]{1,0:T(8,128)S(1)}, f32[264,256]{1,0:T(8,128)S(1)}, u32[]{:S(2)}, u32[]{:S(2)}) collective-permute-start(f32[264,256]{1,0:T(8,128)S(1)} %get-tuple-element.30), channel_id=1, source_target_pairs={{1,2},{2,1},{5,6},{6,5},{9,10},{10,9},{13,14},{14,13},{17,18},{18,... | collective-permute-start | bytes 811016 | tf_op jit(solution)/shard_map/ppermute | solution.py:78
  12.4 5.2 %collective-permute-start.4 = (f32[264,256]{1,0:T(8,128)S(1)}, f32[264,256]{1,0:T(8,128)S(1)}, u32[]{:S(2)}, u32[]{:S(2)}) collective-permute-start(f32[264,256]{1,0:T(8,128)S(1)} %get-tuple-element.33), channel_id=1, source_target_pairs={{4,0},{8,4},{12,8},{16,12},{20,16},{24,20},{28,24},{5,1},{9,5},{13... | collective-permute-start | bytes 811016 | tf_op jit(solution)/shard_map/ppermute | solution.py:72
  13.7 11.8 %collective-permute-start.5 = (f32[264,256]{1,0:T(8,128)S(1)}, f32[264,256]{1,0:T(8,128)S(1)}, u32[]{:S(2)}, u32[]{:S(2)}) collective-permute-start(f32[264,256]{1,0:T(8,128)S(1)} %get-tuple-element.34), channel_id=1, source_target_pairs={{1,0},{2,1},{3,2},{4,5},{5,6},{6,7},{9,8},{10,9},{11,10},{12,13},{... | collective-permute-start | bytes 811016 | tf_op jit(solution)/shard_map/ppermute | solution.py:584
  26.2 9.1 %collective-permute-start.8 = (f32[40,128]{1,0:T(8,128)S(1)}, f32[40,128]{1,0:T(8,128)S(1)}, u32[]{:S(2)}, u32[]{:S(2)}) collective-permute-start(f32[40,128]{1,0:T(8,128)S(1)} %shard_map.63), channel_id=1, source_target_pairs={{0,9},{1,8},{2,11},{3,10},{4,13},{5,12},{6,15},{7,14},{8,1},{9,0},... | collective-permute-start | bytes 61448 | tf_op jit(solution)/shard_map/ppermute | solution.py:58
  33.5 3.8 %collective-permute-start.7 = (f32[40,128]{1,0:T(8,128)S(1)}, f32[40,128]{1,0:T(8,128)S(1)}, u32[]{:S(2)}, u32[]{:S(2)}) collective-permute-start(f32[40,128]{1,0:T(8,128)S(1)} %shard_map.63), channel_id=1, source_target_pairs={{0,1},{1,0},{2,3},{3,2},{4,5},{5,4},{6,7},{7,6},{8,9},{9,8},{10,11... | collective-permute-start | bytes 61448 | tf_op jit(solution)/shard_map/ppermute | solution.py:58
  33.6 3.8 %collective-permute-start.6 = (f32[40,128]{1,0:T(8,128)S(1)}, f32[40,128]{1,0:T(8,128)S(1)}, u32[]{:S(2)}, u32[]{:S(2)}) collective-permute-start(f32[40,128]{1,0:T(8,128)S(1)} %shard_map.63), channel_id=1, source_target_pairs={{0,8},{1,9},{2,10},{3,11},{4,12},{5,13},{6,14},{7,15},{8,0},{9,1},... | collective-permute-start | bytes 61448 | tf_op jit(solution)/shard_map/ppermute | solution.py:58
  37.3 5.0 %collective-permute-start.9 = (f32[40,128]{1,0:T(8,128)S(1)}, f32[40,128]{1,0:T(8,128)S(1)}, u32[]{:S(2)}, u32[]{:S(2)}) collective-permute-start(f32[40,128]{1,0:T(8,128)S(1)} %add_add_fusion.1), channel_id=1, source_target_pairs={{0,2},{1,3},{2,0},{3,1},{4,6},{5,7},{6,4},{7,5},{8,10},{9,11},{10,... | collective-permute-start | bytes 61448 | tf_op jit(solution)/shard_map/ppermute | solution.py:58
  42.4 3.4 %collective-permute-start.12 = (f32[40,128]{1,0:T(8,128)S(1)}, f32[40,128]{1,0:T(8,128)S(1)}, u32[]{:S(2)}, u32[]{:S(2)}) collective-permute-start(f32[40,128]{1,0:T(8,128)S(1)} %add.24), channel_id=1, source_target_pairs={{0,20},{1,21},{2,22},{3,23},{4,16},{5,17},{6,18},{7,19},{8,28},{9,... | collective-permute-start | bytes 61448 | tf_op jit(solution)/shard_map/ppermute | solution.py:58
  42.4 3.8 %collective-permute-start.11 = (f32[40,128]{1,0:T(8,128)S(1)}, f32[40,128]{1,0:T(8,128)S(1)}, u32[]{:S(2)}, u32[]{:S(2)}) collective-permute-start(f32[40,128]{1,0:T(8,128)S(1)} %add.24), channel_id=1, source_target_pairs={{0,16},{1,17},{2,18},{3,19},{4,20},{5,21},{6,22},{7,23},{8,24},{9,... | collective-permute-start | bytes 61448 | tf_op jit(solution)/shard_map/ppermute | solution.py:58
  44.0 2.3 %collective-permute-start.10 = (f32[40,128]{1,0:T(8,128)S(1)}, f32[40,128]{1,0:T(8,128)S(1)}, u32[]{:S(2)}, u32[]{:S(2)}) collective-permute-start(f32[40,128]{1,0:T(8,128)S(1)} %add.24), channel_id=1, source_target_pairs={{0,4},{1,5},{2,6},{3,7},{4,0},{5,1},{6,2},{7,3},{8,12},{9,13},{10,... | collective-permute-start | bytes 61448 | tf_op jit(solution)/shard_map/ppermute | solution.py:58
